TPU v7x, 512 devices: a whole 4x8x8 slice. The times are simulated.
512 devices in a mesh: items: 8 (over y), codes: 64 (over x, z, core).
Axes of the slice: x: 4, y: 8, z: 8, core: 2. Of those that a mesh axis runs over, the one named last changes fastest.
Arguments:
- residuals: bfloat16 [8192, 256], P(('items', 'codes')), may hold values from -6 to 6
- codebook: bfloat16 [16384, 256], P('codes'), may hold values from -6 to 6
Outputs:
- new_codebook: float32 [16384, 256], P('codes')
- next_residuals: float32 [8192, 256], P(('items', 'codes'))
All inputs are finite; a program needn't handle non-finite values.
Results may differ from a plain program's by a relative error of at most 0.0024.
Values may be sent and summed in bfloat16 or wider, within the bound.
No kernel may reach another device: no remote copies, remote signals or barrier semaphores. Data moves between devices by JAX's collectives and lax.ppermute only.
A program may use at most 64 MiB of HBM per device.

v0:
```python
import jax
import jax.numpy as jnp
from jax import lax
from jax.sharding import PartitionSpec as P

ITERS = 3


EPSILON = 1e-06
SHARPNESS = 40.0


def shards(residuals, codebook):
    gathered = lax.all_gather(residuals, "codes", axis=0, tiled=True)
    feature_count = gathered.shape[1]
    rows_float = gathered.astype(jnp.float32)
    codes_float = codebook.astype(jnp.float32)
    row_scale = lax.rsqrt(jnp.mean(rows_float * rows_float, axis=1) + EPSILON)
    code_scale = lax.rsqrt(jnp.mean(codes_float * codes_float, axis=1) + EPSILON)
    similarity = lax.dot_general(
        gathered, codebook, (((1,), (1,)), ((), ())), preferred_element_type=jnp.float32
    )
    kernel = jnp.exp(
        SHARPNESS * similarity * row_scale[:, None] * code_scale[None, :] / feature_count
    )
    balance = gathered.shape[0] * lax.axis_size("items") / codebook.shape[0]
    weights_rows = jnp.ones((gathered.shape[0],), jnp.float32)
    weights_cols = jnp.ones((codebook.shape[0],), jnp.float32)
    for sweep in range(ITERS):
        column_total = lax.psum(
            jnp.dot(weights_rows, kernel, precision=lax.Precision.HIGHEST), "items"
        )
        weights_cols = balance / column_total
        row_total = lax.psum(
            jnp.dot(kernel, weights_cols, precision=lax.Precision.HIGHEST), "codes"
        )
        weights_rows = 1.0 / row_total
    transport = (kernel * weights_rows[:, None] * weights_cols[None, :]).astype(jnp.bfloat16)
    numerator = lax.dot_general(
        transport, gathered, (((0,), (0,)), ((), ())), preferred_element_type=jnp.float32
    )
    mass = jnp.sum(transport.astype(jnp.float32), axis=0)
    numerator, mass = lax.psum((numerator, mass), "items")
    new_codebook = numerator / mass[:, None]
    moved = lax.all_to_all(transport, "codes", split_axis=0, concat_axis=1, tiled=True)
    rebuilt = jnp.dot(
        moved,
        lax.all_gather(codebook, "codes", axis=0, tiled=True),
        preferred_element_type=jnp.float32,
    )
    following = residuals.astype(jnp.float32) - rebuilt
    return (new_codebook, following)


def solution(mesh):
    return jax.shard_map(
        shards,
        mesh=mesh,
        in_specs=(P(("items", "codes"), None), P("codes", None)),
        out_specs=(P("codes", None), P(("items", "codes"), None)),
        check_vma=False,
    )
```

profile of v0, /device:TPU:1, one launch (start us, length us, event | category | flops | bytes accessed | tf_op | source)
XLA Modules:
  0.0 592.9 jit_solution(12532103684570617176)
XLA Ops:
  8.1 57.9 %all_gather.6 = bf16[1024,256]{1,0:T(8,128)(2,1)S(1)} all-gather(bf16[16,256]{1,0:T(8,128)(2,1)} %param.2), channel_id=1, replica_groups=mesh['items'=8,'codes'=64] {'codes'}, dimensions={0}, use_global_device_ids=true | all-gather | bytes 532480 | tf_op jit(solution)/shard_map/all_gather | solution.py:14
  65.9 1.0 multiply_reduce_fusion.1
  67.2 1.3 fusion.2
  68.5 0.5 fusion.3
  69.0 13.9 %psum.56 = f32[256]{0:T(256)S(1)} all-reduce(f32[256]{0:T(256)S(1)} %bitcast.44), channel_id=1, replica_groups=mesh['items'=8,'codes'=64] {'items'}, use_global_device_ids=true, to_apply=%region_2.0 | all-reduce | flops 256 | bytes 2048 | tf_op jit(solution)/shard_map/psum | solution.py:30
  82.9 1.0 fusion.6
  83.9 127.3 %psum.57 = f32[1024]{0:T(1024)S(1)} all-reduce(f32[1024]{0:T(1024)S(1)} %bitcast.34), channel_id=1, replica_groups=mesh['items'=8,'codes'=64] {'codes'}, use_global_device_ids=true, to_apply=%region_3.0 | all-reduce | flops 1024 | bytes 8192 | tf_op jit(solution)/shard_map/psum | solution.py:34
  211.2 0.5 fusion.7
  211.7 11.2 %psum.58 = f32[256]{0:T(256)S(1)} all-reduce(f32[256]{0:T(256)S(1)} %bitcast.41), channel_id=1, replica_groups=mesh['items'=8,'codes'=64] {'items'}, use_global_device_ids=true, to_apply=%region_4.0 | all-reduce | flops 256 | bytes 2048 | tf_op jit(solution)/shard_map/psum | solution.py:30
  222.9 1.0 fusion.8
  223.9 127.8 %psum.59 = f32[1024]{0:T(1024)S(1)} all-reduce(f32[1024]{0:T(1024)S(1)} %bitcast.36), channel_id=1, replica_groups=mesh['items'=8,'codes'=64] {'codes'}, use_global_device_ids=true, to_apply=%region_5.0 | all-reduce | flops 1024 | bytes 8192 | tf_op jit(solution)/shard_map/psum | solution.py:34
  351.7 0.5 fusion.9
  352.2 11.6 %psum.60 = f32[256]{0:T(256)S(1)} all-reduce(f32[256]{0:T(256)S(1)} %bitcast.43), channel_id=1, replica_groups=mesh['items'=8,'codes'=64] {'items'}, use_global_device_ids=true, to_apply=%region_6.0 | all-reduce | flops 256 | bytes 2048 | tf_op jit(solution)/shard_map/psum | solution.py:30
  363.8 1.0 fusion.10
  364.8 127.8 %psum.61 = f32[1024]{0:T(1024)S(1)} all-reduce(f32[1024]{0:T(1024)S(1)} %bitcast.38), channel_id=1, replica_groups=mesh['items'=8,'codes'=64] {'codes'}, use_global_device_ids=true, to_apply=%region_7.0 | all-reduce | flops 1024 | bytes 8192 | tf_op jit(solution)/shard_map/psum | solution.py:34
  492.6 1.1 convert_reduce_fusion
  493.7 2.1 fusion.11
  495.8 0.5 all-gather.2.cloned.1.call-update
  496.4 4.7 all-to-all-start
  501.1 12.6 %psum.63 = f32[256]{0:T(256)S(1)} all-reduce(f32[256]{0:T(256)S(1)} %get-tuple-element.2), channel_id=1, replica_groups=mesh['items'=8,'codes'=64] {'items'}, use_global_device_ids=true, to_apply=%region_10.0 | all-reduce | flops 256 | bytes 2048 | tf_op jit(solution)/shard_map/psum | solution.py:43
  513.7 46.6 %all-reduce.2.cloned.1.call-done = f32[256,256]{1,0:T(8,128)} async-done(((f32[256,256]{1,0:T(8,128)}), f32[256,256]{1,0:T(8,128)}) %all-reduce.2.cloned.1.call-update) | async-done | bytes 262160 | tf_op jit(solution)/shard_map/psum | solution.py:43
  560.3 1.8 broadcast_divide_fusion
  562.1 18.1 %all-gather.2.cloned.1.call-done = bf16[16384,256]{1,0:T(8,128)(2,1)} async-done(((bf16[256,256]{1,0:T(8,128)(2,1)}), bf16[16384,256]{1,0:T(8,128)(2,1)}) %all-gather.2.cloned.1.call-update) | async-done | bytes 8388624 | tf_op jit(solution)/shard_map/all_gather | solution.py:48
  580.2 5.2 convolution_subtract_fusion
  (16 shorter events, 0.4 us)
Async XLA Ops:
  8.0 572.3 %copy-start = (bf16[16,256]{1,0:T(8,128)(2,1)S(1)}, bf16[16,256]{1,0:T(8,128)(2,1)}, u32[]{:S(2)}) copy-start(bf16[16,256]{1,0:T(8,128)(2,1)} %param.2) | copy-start | bytes 24580
  8.0 552.3 %all-reduce.2.cloned.1.call-start = ((), (), s32[]{:S(2)}) async-start(), calls=%async_computation.1 | async-start | bytes 524288 | tf_op jit(solution)/shard_map/psum | solution.py:43
  495.8 84.5 %all-gather.2.cloned.1.call-start = ((), (), s32[]{:S(2)}) async-start(), calls=%async_computation.2 | async-start | bytes 8519680 | tf_op jit(solution)/shard_map/all_gather | solution.py:48
  496.4 65.7 %all-to-all-start = ((bf16[64,16,256]{2,1,0:T(8,128)(2,1)}), bf16[64,16,256]{2,1,0:T(8,128)(2,1)S(1)}, u32[]{:S(2)}, u32[]{:S(2)}) async-start(bf16[64,16,256]{2,1,0:T(8,128)(2,1)} %bitcast.11), calls=%async_computation | async-start | bytes 1048576 | tf_op jit(solution)/shard_map/all_to_all | solution.py:45
Sparse Core Ops, SparseCore 0:
  495.9 64.3 all-reduce.1
Sparse Core Ops, SparseCore 1:
  499.6 80.5 all-gather.1
where the time goes:
time: 593 us
  blocking collectives  490 us (83%)
  waiting for transfers between devices  65.2 us (11%)
  between operations  15.5 us (3%)
  matrix products  13 us (2%)
    psum x3, blocking collectives, shards(): lax.psum(jnp.dot(kernel, weights_cols, precision=lax.Precision.HIGHEST),...  383 us
    all_gather x1, blocking collectives, shards(): gathered = lax.all_gather(residuals, 'codes', axis=0, tiled=True)  57.9 us
    psum x1, waiting for transfers between devices, shards(): numerator, mass = lax.psum((numerator, mass), 'items')  46.6 us
    psum x3, blocking collectives, shards(): lax.psum(jnp.dot(weights_rows, kernel, precision=lax.Precision.HIGHEST),...  36.7 us
    all_gather x1, waiting for transfers between devices, shards(): lax.all_gather(codebook, 'codes', axis=0, tiled=True)  18.1 us
    psum x1, blocking collectives, shards(): numerator, mass = lax.psum((numerator, mass), 'items')  12.6 us
  transfers between devices with their start and end apart: 3, of which 2 were waited for; matrix products, arithmetic and copies ran while one was open for 0% of the time, Pallas kernels for 0%

commit v1 on v0

v1 whole, which is shorter than its diff:
```python
import jax
import jax.numpy as jnp
from jax import lax
from jax.sharding import Mesh, PartitionSpec as P

ITERS = 3
EPSILON = 1e-06
SHARPNESS = 40.0

ITEM_AXES = ("y",)
CODE_AXES = ("x", "z", "c")


def spread(block, axes):
    members = lax.axis_size(axes)
    copies = jnp.broadcast_to(block[None], (members,) + block.shape)
    return lax.all_to_all(copies, axes, 0, 0, tiled=True)


def shards(residuals, codebook):
    rows, width = residuals.shape
    codes = codebook.shape[0]
    groups = lax.axis_size(ITEM_AXES)
    parts = lax.axis_size(CODE_AXES)
    gathered = spread(residuals, CODE_AXES).reshape(parts * rows, width)
    rows_float = gathered.astype(jnp.float32)
    codes_float = codebook.astype(jnp.float32)
    row_scale = lax.rsqrt(jnp.mean(rows_float * rows_float, axis=1) + EPSILON)
    code_scale = lax.rsqrt(jnp.mean(codes_float * codes_float, axis=1) + EPSILON)
    similarity = lax.dot_general(
        gathered, codebook, (((1,), (1,)), ((), ())), preferred_element_type=jnp.float32
    )
    kernel = jnp.exp(
        SHARPNESS * similarity * row_scale[:, None] * code_scale[None, :] / width
    )
    balance = (gathered.shape[0] * groups) / (codes * parts)
    weights_rows = None
    for sweep in range(ITERS):
        scaled = kernel if weights_rows is None else kernel * weights_rows[:, None]
        column_total = jnp.sum(spread(jnp.sum(scaled, axis=0), ITEM_AXES), axis=0)
        weights_cols = balance / column_total
        row_part = jnp.sum(kernel * weights_cols[None, :], axis=1)
        row_total = jnp.sum(spread(row_part, CODE_AXES), axis=0)
        weights_rows = 1.0 / row_total
    shares = (kernel * weights_cols[None, :]).astype(jnp.bfloat16)
    rebuilt = jnp.dot(shares, codebook, preferred_element_type=jnp.float32)
    rebuilt = rebuilt.astype(jnp.bfloat16).reshape(parts, rows, width)
    rebuilt = lax.all_to_all(rebuilt, CODE_AXES, 0, 0, tiled=True)
    rebuilt = jnp.sum(rebuilt.astype(jnp.float32), axis=0)

    transport = (kernel * weights_rows[:, None] * weights_cols[None, :]).astype(jnp.bfloat16)
    numerator = lax.dot_general(
        transport, gathered, (((0,), (0,)), ((), ())), preferred_element_type=jnp.float32
    )
    mass = jnp.sum(transport.astype(jnp.float32), axis=0)
    share = codes // groups
    high = mass.astype(jnp.bfloat16)
    low = (mass - high.astype(jnp.float32)).astype(jnp.bfloat16)
    masses = jnp.stack([high.reshape(groups, share), low.reshape(groups, share)], axis=1)
    masses = jnp.pad(masses, ((0, 0), (0, 14), (0, width - share)))
    packed = jnp.concatenate(
        [numerator.astype(jnp.bfloat16).reshape(groups, share, width), masses], axis=1
    )
    packed = lax.all_to_all(packed, ITEM_AXES, 0, 0, tiled=True)
    total = jnp.sum(packed.astype(jnp.float32), axis=0)
    mass_total = total[share, :share] + total[share + 1, :share]
    means = (total[:share] / mass_total[:, None]).astype(jnp.bfloat16)
    new_codebook = spread(means, ITEM_AXES).reshape(codes, width).astype(jnp.float32)

    mine = lax.axis_index(CODE_AXES) * rows
    own = lax.dynamic_slice_in_dim(weights_rows, mine, rows)
    following = residuals.astype(jnp.float32) - rebuilt * own[:, None]
    return (new_codebook, following)


def solution(mesh):
    fine = Mesh(mesh.devices.reshape(8, 4, 8, 2), ("y", "x", "z", "c"))
    return jax.shard_map(
        shards,
        mesh=fine,
        in_specs=(P(("y", "x", "z", "c"), None), P(("x", "z", "c"), None)),
        out_specs=(P(("x", "z", "c"), None), P(("y", "x", "z", "c"), None)),
        check_vma=False,
    )
```

time: 593 us -> 179 us (0.30)
  blocking collectives: 490 us -> 88.5 us
  starting transfers between devices: 4.8 us -> 28.9 us
  waiting for transfers between devices: 65.2 us -> 49.8 us
  between operations: 15.5 us -> 0.81 us
  matrix products: 13 us -> 2.07 us
    psum x7 -> x0, blocking collectives: 432 us -> none  [the longest x3 383 us: shards(): lax.psum(jnp.dot(kernel, weights_cols, precision=lax.Precision.HIGHEST),...]
    all_to_all x0 -> x6, blocking collectives: none -> 88.5 us  [spread(): return lax.all_to_all(copies, axes, 0, 0, tiled=True)]
    all_gather x1 -> x0, blocking collectives: 57.9 us -> none  [shards(): gathered = lax.all_gather(residuals, 'codes', axis=0, tiled=True)]
    all_to_all x1 -> x4, waiting for transfers between devices: 0.01 us -> 49.8 us  [the longest x2 24.2 us: spread(): return lax.all_to_all(copies, axes, 0, 0, tiled=True)]
    psum x1 -> x0, waiting for transfers between devices: 46.6 us -> none  [shards(): numerator, mass = lax.psum((numerator, mass), 'items')]
    all_to_all x1 -> x4, starting transfers between devices: 4.72 us -> 28.9 us  [the longest x2 18.3 us: spread(): return lax.all_to_all(copies, axes, 0, 0, tiled=True)]
    all_gather x1 -> x0, waiting for transfers between devices: 18.1 us -> none  [shards(): lax.all_gather(codebook, 'codes', axis=0, tiled=True)]
    dot_general x7 -> x1, matrix products: 9.69 us -> 1.1 us  [shards(): rebuilt = jnp.dot(shares, codebook, preferred_element_type=jnp.float32)]
  transfers between devices with their start and end apart: 3 -> 4, of which waited for: 2 -> 4; matrix products, arithmetic and copies ran while one was open for 0% -> 1% of each run, Pallas kernels for 0% -> 0%
where the time goes in v1:
time: 179 us; the launch traced here: 178 us
  blocking collectives  88.5 us (49%)
  waiting for transfers between devices  49.8 us (28%)
  starting transfers between devices  28.9 us (16%)
  other arithmetic  4.69 us (3%)
  local copies, waits for them, and re-layouts  3.45 us (2%)
  matrix products  2.07 us (1%)
    all_to_all x6, blocking collectives, spread(): return lax.all_to_all(copies, axes, 0, 0, tiled=True)  88.5 us
    all_to_all x2, waiting for transfers between devices, spread(): return lax.all_to_all(copies, axes, 0, 0, tiled=True)  24.2 us
    all_to_all x2, starting transfers between devices, spread(): return lax.all_to_all(copies, axes, 0, 0, tiled=True)  18.3 us
    all_to_all x1, waiting for transfers between devices, shards(): rebuilt = lax.all_to_all(rebuilt, CODE_AXES, 0, 0, tiled=True)  17.1 us
    all_to_all x1, waiting for transfers between devices, shards(): packed = lax.all_to_all(packed, ITEM_AXES, 0, 0, tiled=True)  8.51 us
    all_to_all x1, starting transfers between devices, shards(): rebuilt = lax.all_to_all(rebuilt, CODE_AXES, 0, 0, tiled=True)  7.21 us
  transfers between devices with their start and end apart: 4, of which 4 were waited for; matrix products, arithmetic and copies ran while one was open for 1% of the time, Pallas kernels for 0%

profile of v1, /device:TPU:1, one launch (start us, length us, event | category | flops | bytes accessed | tf_op | source)
XLA Modules:
  0.0 178.2 jit_solution(15994710085911482853)
XLA Ops:
  0.6 1.5 broadcast_in_dim.16
  2.2 15.0 %all-to-all-start = ((bf16[64,16,256]{2,1,0:T(8,128)(2,1)}), bf16[64,16,256]{2,1,0:T(8,128)(2,1)S(1)}, u32[]{:S(2)}, u32[]{:S(2)}) async-start(bf16[64,16,256]{2,1,0:T(8,128)(2,1)} %broadcast_in_dim.16), calls=%async_computation | async-start | bytes 1048576 | tf_op jit(solution)/shard_map/all_to_all | solution.py:17
  17.3 17.1 %all-to-all-done = bf16[64,16,256]{2,1,0:T(8,128)(2,1)S(1)} async-done(((bf16[64,16,256]{2,1,0:T(8,128)(2,1)}), bf16[64,16,256]{2,1,0:T(8,128)(2,1)S(1)}, u32[]{:S(2)}, u32[]{:S(2)}) %all-to-all-start) | async-done | bytes 524320 | tf_op jit(solution)/shard_map/all_to_all | solution.py:17
  34.7 0.4 fusion.13
  35.2 13.2 %all_to_all.56 = f32[8,1,256]{2,1,0:T(1,128)S(1)} all-to-all(f32[8,1,256]{2,1,0:T(1,128)S(1)} %broadcast_in_dim.17), channel_id=1, replica_groups=mesh['y'=8,'x'=4,'z'=8,'c'=2] {'y'}, dimensions={0} | all-to-all | bytes 16384 | tf_op jit(solution)/shard_map/all_to_all | solution.py:17
  48.8 19.5 %all_to_all.57 = f32[64,1,1024]{2,1,0:T(1,128)S(1)} all-to-all(f32[64,1,1024]{2,1,0:T(1,128)S(1)} %broadcast_in_dim.18), channel_id=1, replica_groups=mesh['y'=8,'x'=4,'z'=8,'c'=2] {'x','z','c'}, dimensions={0} | all-to-all | bytes 524288 | tf_op jit(solution)/shard_map/all_to_all | solution.py:17
  68.7 8.9 %all_to_all.58 = f32[8,1,256]{2,1,0:T(1,128)S(1)} all-to-all(f32[8,1,256]{2,1,0:T(1,128)S(1)} %broadcast_in_dim.19), channel_id=1, replica_groups=mesh['y'=8,'x'=4,'z'=8,'c'=2] {'y'}, dimensions={0} | all-to-all | bytes 16384 | tf_op jit(solution)/shard_map/all_to_all | solution.py:17
  78.0 19.0 %all_to_all.59 = f32[64,1,1024]{2,1,0:T(1,128)S(1)} all-to-all(f32[64,1,1024]{2,1,0:T(1,128)S(1)} %broadcast_in_dim.20), channel_id=1, replica_groups=mesh['y'=8,'x'=4,'z'=8,'c'=2] {'x','z','c'}, dimensions={0} | all-to-all | bytes 524288 | tf_op jit(solution)/shard_map/all_to_all | solution.py:17
  97.4 8.9 %all_to_all.60 = f32[8,1,256]{2,1,0:T(1,128)S(1)} all-to-all(f32[8,1,256]{2,1,0:T(1,128)S(1)} %broadcast_in_dim.21), channel_id=1, replica_groups=mesh['y'=8,'x'=4,'z'=8,'c'=2] {'y'}, dimensions={0} | all-to-all | bytes 16384 | tf_op jit(solution)/shard_map/all_to_all | solution.py:17
  106.7 19.0 %all_to_all.61 = f32[64,1,1024]{2,1,0:T(1,128)S(1)} all-to-all(f32[64,1,1024]{2,1,0:T(1,128)S(1)} %broadcast_in_dim.22), channel_id=1, replica_groups=mesh['y'=8,'x'=4,'z'=8,'c'=2] {'x','z','c'}, dimensions={0} | all-to-all | bytes 524288 | tf_op jit(solution)/shard_map/all_to_all | solution.py:17
  125.9 0.2 convert_reduce_fusion.1
  126.1 0.5 convolution_convert_fusion.1
  126.8 0.7 pad_maximum_fusion
  127.5 3.4 %all-to-all-start.7 = ((bf16[8,48,256]{2,1,0:T(8,128)(2,1)}), bf16[8,48,256]{2,1,0:T(8,128)(2,1)S(1)}, u32[]{:S(2)}, u32[]{:S(2)}) async-start(bf16[8,48,256]{2,1,0:T(8,128)(2,1)} %pad_maximum_fusion), calls=%async_computation.7 | async-start | bytes 393216 | tf_op jit(solution)/shard_map/all_to_all | solution.py:64
  130.9 1.1 convolution_convert_fusion
  132.0 8.5 %all-to-all-done.7 = bf16[8,48,256]{2,1,0:T(8,128)(2,1)S(1)} async-done(((bf16[8,48,256]{2,1,0:T(8,128)(2,1)}), bf16[8,48,256]{2,1,0:T(8,128)(2,1)S(1)}, u32[]{:S(2)}, u32[]{:S(2)}) %all-to-all-start.7) | async-done | bytes 196640 | tf_op jit(solution)/shard_map/all_to_all | solution.py:64
  140.5 7.2 %all-to-all-start.9 = ((bf16[64,16,256]{2,1,0:T(8,128)(2,1)}), bf16[64,16,256]{2,1,0:T(8,128)(2,1)S(1)}, u32[]{:S(2)}, u32[]{:S(2)}) async-start(bf16[64,16,256]{2,1,0:T(8,128)(2,1)} %bitcast.4), calls=%async_computation.9 | async-start | bytes 1048576 | tf_op jit(solution)/shard_map/all_to_all | solution.py:48
  147.9 17.1 %all-to-all-done.9 = bf16[64,16,256]{2,1,0:T(8,128)(2,1)S(1)} async-done(((bf16[64,16,256]{2,1,0:T(8,128)(2,1)}), bf16[64,16,256]{2,1,0:T(8,128)(2,1)S(1)}, u32[]{:S(2)}, u32[]{:S(2)}) %all-to-all-start.9) | async-done | bytes 524320 | tf_op jit(solution)/shard_map/all_to_all | solution.py:48
  165.0 0.7 broadcast_in_dim.23
  165.7 3.4 %all-to-all-start.8 = ((bf16[8,32,256]{2,1,0:T(8,128)(2,1)}), bf16[8,32,256]{2,1,0:T(8,128)(2,1)S(1)}, u32[]{:S(2)}, u32[]{:S(2)}) async-start(bf16[8,32,256]{2,1,0:T(8,128)(2,1)} %broadcast_in_dim.23), calls=%async_computation.8 | async-start | bytes 262144 | tf_op jit(solution)/shard_map/all_to_all | solution.py:17
  169.2 0.6 copy-done.1
  169.7 0.7 multiply_subtract_fusion
  170.4 7.1 %all-to-all-done.8 = bf16[8,32,256]{2,1,0:T(8,128)(2,1)S(1)} async-done(((bf16[8,32,256]{2,1,0:T(8,128)(2,1)}), bf16[8,32,256]{2,1,0:T(8,128)(2,1)S(1)}, u32[]{:S(2)}, u32[]{:S(2)}) %all-to-all-start.8) | async-done | bytes 131104 | tf_op jit(solution)/shard_map/all_to_all | solution.py:17
  177.5 0.7 bitcast_convert_fusion
  (39 shorter events, 3.0 us)
Async XLA Ops:
  2.1 15.0 %copy-start = (bf16[256,256]{1,0:T(8,128)(2,1)S(1)}, bf16[256,256]{1,0:T(8,128)(2,1)}, u32[]{:S(2)}) copy-start(bf16[256,256]{1,0:T(8,128)(2,1)} %param.3) | copy-start | bytes 393220
  2.2 32.2 %all-to-all-start = ((bf16[64,16,256]{2,1,0:T(8,128)(2,1)}), bf16[64,16,256]{2,1,0:T(8,128)(2,1)S(1)}, u32[]{:S(2)}, u32[]{:S(2)}) async-start(bf16[64,16,256]{2,1,0:T(8,128)(2,1)} %broadcast_in_dim.16), calls=%async_computation | async-start | bytes 1048576 | tf_op jit(solution)/shard_map/all_to_all | solution.py:17
  127.5 13.0 %all-to-all-start.7 = ((bf16[8,48,256]{2,1,0:T(8,128)(2,1)}), bf16[8,48,256]{2,1,0:T(8,128)(2,1)S(1)}, u32[]{:S(2)}, u32[]{:S(2)}) async-start(bf16[8,48,256]{2,1,0:T(8,128)(2,1)} %pad_maximum_fusion), calls=%async_computation.7 | async-start | bytes 393216 | tf_op jit(solution)/shard_map/all_to_all | solution.py:64
  140.5 24.5 %all-to-all-start.9 = ((bf16[64,16,256]{2,1,0:T(8,128)(2,1)}), bf16[64,16,256]{2,1,0:T(8,128)(2,1)S(1)}, u32[]{:S(2)}, u32[]{:S(2)}) async-start(bf16[64,16,256]{2,1,0:T(8,128)(2,1)} %bitcast.4), calls=%async_computation.9 | async-start | bytes 1048576 | tf_op jit(solution)/shard_map/all_to_all | solution.py:48
  165.7 11.8 %all-to-all-start.8 = ((bf16[8,32,256]{2,1,0:T(8,128)(2,1)}), bf16[8,32,256]{2,1,0:T(8,128)(2,1)S(1)}, u32[]{:S(2)}, u32[]{:S(2)}) async-start(bf16[8,32,256]{2,1,0:T(8,128)(2,1)} %broadcast_in_dim.23), calls=%async_computation.8 | async-start | bytes 262144 | tf_op jit(solution)/shard_map/all_to_all | solution.py:17
  169.0 0.7 copy-start.1

commit v2 on v1

v2 whole, which is shorter than its diff:
```python
import jax
import jax.numpy as jnp
from jax import lax
from jax.sharding import Mesh, PartitionSpec as P

ITERS = 3
EPSILON = 1e-06
SHARPNESS = 40.0

ITEM_AXES = ("c", "y")
CODE_AXES = ("x", "z")


def spread(block, axes):
    members = lax.axis_size(axes)
    copies = jnp.broadcast_to(block[None], (members,) + block.shape)
    return lax.all_to_all(copies, axes, 0, 0, tiled=True)


def shards(residuals, codebook):
    rows, width = residuals.shape
    items = rows * lax.axis_size(CODE_AXES)
    codes = codebook.shape[0] * lax.axis_size("c")
    groups = lax.axis_size(ITEM_AXES)
    parts = lax.axis_size(CODE_AXES)
    codebook = spread(codebook, "c").reshape(codes, width)
    gathered = spread(residuals, CODE_AXES).reshape(items, width)
    rows_float = gathered.astype(jnp.float32)
    codes_float = codebook.astype(jnp.float32)
    row_scale = lax.rsqrt(jnp.mean(rows_float * rows_float, axis=1) + EPSILON)
    code_scale = lax.rsqrt(jnp.mean(codes_float * codes_float, axis=1) + EPSILON)
    similarity = lax.dot_general(
        gathered, codebook, (((1,), (1,)), ((), ())), preferred_element_type=jnp.float32
    )
    kernel = jnp.exp(
        SHARPNESS * similarity * row_scale[:, None] * code_scale[None, :] / width
    )
    balance = (items * groups) / (codes * parts)
    weights_rows = None
    for _ in range(ITERS):
        scaled = kernel if weights_rows is None else kernel * weights_rows[:, None]
        column_total = jnp.sum(spread(jnp.sum(scaled, axis=0), ITEM_AXES), axis=0)
        weights_cols = balance / column_total
        row_part = jnp.sum(kernel * weights_cols[None, :], axis=1)
        row_total = jnp.sum(spread(row_part, CODE_AXES), axis=0)
        weights_rows = 1.0 / row_total

    transport = (
        kernel * weights_rows[:, None] * weights_cols[None, :]
    ).astype(jnp.bfloat16)
    numerator = lax.dot_general(
        transport, gathered, (((0,), (0,)), ((), ())), preferred_element_type=jnp.float32
    )
    mass = jnp.sum(transport.astype(jnp.float32), axis=0)
    share = codes // groups
    high = mass.astype(jnp.bfloat16)
    low = (mass - high.astype(jnp.float32)).astype(jnp.bfloat16)
    masses = jnp.stack([high.reshape(groups, share), low.reshape(groups, share)], axis=1)
    masses = jnp.pad(masses, ((0, 0), (0, 6), (0, width - share)))
    packed = jnp.concatenate(
        [numerator.astype(jnp.bfloat16).reshape(groups, share, width), masses], axis=1
    )
    packed = lax.all_to_all(packed, ITEM_AXES, 0, 0, tiled=True)

    shares = (kernel * weights_cols[None, :]).astype(jnp.bfloat16)
    rebuilt = jnp.dot(shares, codebook, preferred_element_type=jnp.float32)
    rebuilt = rebuilt.astype(jnp.bfloat16).reshape(parts, rows, width)
    rebuilt = lax.all_to_all(rebuilt, CODE_AXES, 0, 0, tiled=True)

    total = jnp.sum(packed.astype(jnp.float32), axis=0)
    mass_total = total[share, :share] + total[share + 1, :share]
    means = total[:share] / mass_total[:, None]
    new_codebook = spread(means, "y").reshape(-1, width)

    rebuilt = jnp.sum(rebuilt.astype(jnp.float32), axis=0)
    mine = lax.axis_index(CODE_AXES) * rows
    own = lax.dynamic_slice_in_dim(weights_rows, mine, rows)
    following = residuals.astype(jnp.float32) - rebuilt * own[:, None]
    return (new_codebook, following)


def solution(mesh):
    fine = Mesh(mesh.devices.reshape(8, 4, 8, 2), ("y", "x", "z", "c"))
    return jax.shard_map(
        shards,
        mesh=fine,
        in_specs=(P(("y", "x", "z", "c"), None), P(("x", "z", "c"), None)),
        out_specs=(P(("x", "z", "c"), None), P(("y", "x", "z", "c"), None)),
        check_vma=False,
    )
```

time: 179 us -> 160 us (0.89); the launches traced: 178 us -> 157 us
  waiting for transfers between devices: 49.8 us -> 37.4 us
  starting transfers between devices: 28.9 us -> 22.7 us
    all_to_all x1, waiting for transfers between devices: 17.1 us -> 9.51 us  [shards(): rebuilt = lax.all_to_all(rebuilt, CODE_AXES, 0, 0, tiled=True)]
    all_to_all x2, waiting for transfers between devices: 24.2 us -> 18.2 us  [spread(): return lax.all_to_all(copies, axes, 0, 0, tiled=True)]
    all_to_all x2, starting transfers between devices: 18.3 us -> 13.4 us  [spread(): return lax.all_to_all(copies, axes, 0, 0, tiled=True)]
    all_to_all x1, starting transfers between devices: 7.21 us -> 3.87 us  [shards(): rebuilt = lax.all_to_all(rebuilt, CODE_AXES, 0, 0, tiled=True)]
    all_to_all x1, starting transfers between devices: 3.39 us -> 5.44 us  [shards(): packed = lax.all_to_all(packed, ITEM_AXES, 0, 0, tiled=True)]
    all_to_all x6 -> x7, blocking collectives: 88.5 us -> 87.7 us  [spread(): return lax.all_to_all(copies, axes, 0, 0, tiled=True)]
where the time goes in v2:
time: 160 us; the launch traced here: 157 us
  blocking collectives  87.7 us (55%)
  waiting for transfers between devices  37.4 us (23%)
  starting transfers between devices  22.7 us (14%)
  local copies, waits for them, and re-layouts  3.5 us (2%)
  other arithmetic  3.29 us (2%)
  matrix products  1.9 us (1%)
    all_to_all x7, blocking collectives, spread(): return lax.all_to_all(copies, axes, 0, 0, tiled=True)  87.7 us
    all_to_all x2, waiting for transfers between devices, spread(): return lax.all_to_all(copies, axes, 0, 0, tiled=True)  18.2 us
    all_to_all x2, starting transfers between devices, spread(): return lax.all_to_all(copies, axes, 0, 0, tiled=True)  13.4 us
    all_to_all x1, waiting for transfers between devices, shards(): packed = lax.all_to_all(packed, ITEM_AXES, 0, 0, tiled=True)  9.74 us
    all_to_all x1, waiting for transfers between devices, shards(): rebuilt = lax.all_to_all(rebuilt, CODE_AXES, 0, 0, tiled=True)  9.51 us
    all_to_all x1, starting transfers between devices, shards(): packed = lax.all_to_all(packed, ITEM_AXES, 0, 0, tiled=True)  5.44 us
    all_to_all x1, starting transfers between devices, shards(): rebuilt = lax.all_to_all(rebuilt, CODE_AXES, 0, 0, tiled=True)  3.87 us
  transfers between devices with their start and end apart: 4, of which 4 were waited for; matrix products, arithmetic and copies ran while one was open for 1% of the time, Pallas kernels for 0%

profile of v2, /device:TPU:1, one launch (start us, length us, event | category | flops | bytes accessed | tf_op | source)
XLA Modules:
  0.0 157.2 jit_solution(3612022912690591405)
XLA Ops:
  0.6 0.9 broadcast_in_dim.19
  1.6 10.4 %all_to_all.61 = bf16[2,256,256]{2,1,0:T(8,128)(2,1)S(1)} all-to-all(bf16[2,256,256]{2,1,0:T(8,128)(2,1)S(1)} %broadcast_in_dim.19), channel_id=1, replica_groups=mesh['y'=8,'x'=4,'z'=8,'c'=2] {'c'}, dimensions={0} | all-to-all | bytes 524288 | tf_op jit(solution)/shard_map/all_to_all | solution.py:17
  12.0 0.7 broadcast_in_dim.18
  12.7 7.5 %all-to-all-start = ((bf16[32,16,256]{2,1,0:T(8,128)(2,1)}), bf16[32,16,256]{2,1,0:T(8,128)(2,1)S(1)}, u32[]{:S(2)}, u32[]{:S(2)}) async-start(bf16[32,16,256]{2,1,0:T(8,128)(2,1)} %broadcast_in_dim.18), calls=%async_computation | async-start | bytes 524288 | tf_op jit(solution)/shard_map/all_to_all | solution.py:17
  20.4 9.5 %all-to-all-done = bf16[32,16,256]{2,1,0:T(8,128)(2,1)S(1)} async-done(((bf16[32,16,256]{2,1,0:T(8,128)(2,1)}), bf16[32,16,256]{2,1,0:T(8,128)(2,1)S(1)}, u32[]{:S(2)}, u32[]{:S(2)}) %all-to-all-start) | async-done | bytes 262176 | tf_op jit(solution)/shard_map/all_to_all | solution.py:17
  30.2 0.4 fusion.12
  30.6 17.7 %all_to_all.62 = f32[16,1,512]{2,1,0:T(1,128)S(1)} all-to-all(f32[16,1,512]{2,1,0:T(1,128)S(1)} %broadcast_in_dim.20), channel_id=1, replica_groups=mesh['y'=8,'x'=4,'z'=8,'c'=2] {'c','y'}, dimensions={0} | all-to-all | bytes 65536 | tf_op jit(solution)/shard_map/all_to_all | solution.py:17
  48.5 12.8 %all_to_all.63 = f32[32,1,512]{2,1,0:T(1,128)S(1)} all-to-all(f32[32,1,512]{2,1,0:T(1,128)S(1)} %broadcast_in_dim.21), channel_id=1, replica_groups=mesh['y'=8,'x'=4,'z'=8,'c'=2] {'x','z'}, dimensions={0} | all-to-all | bytes 131072 | tf_op jit(solution)/shard_map/all_to_all | solution.py:17
  61.6 11.6 %all_to_all.64 = f32[16,1,512]{2,1,0:T(1,128)S(1)} all-to-all(f32[16,1,512]{2,1,0:T(1,128)S(1)} %broadcast_in_dim.22), channel_id=1, replica_groups=mesh['y'=8,'x'=4,'z'=8,'c'=2] {'c','y'}, dimensions={0} | all-to-all | bytes 65536 | tf_op jit(solution)/shard_map/all_to_all | solution.py:17
  73.5 11.8 %all_to_all.65 = f32[32,1,512]{2,1,0:T(1,128)S(1)} all-to-all(f32[32,1,512]{2,1,0:T(1,128)S(1)} %broadcast_in_dim.23), channel_id=1, replica_groups=mesh['y'=8,'x'=4,'z'=8,'c'=2] {'x','z'}, dimensions={0} | all-to-all | bytes 131072 | tf_op jit(solution)/shard_map/all_to_all | solution.py:17
  85.6 11.5 %all_to_all.66 = f32[16,1,512]{2,1,0:T(1,128)S(1)} all-to-all(f32[16,1,512]{2,1,0:T(1,128)S(1)} %broadcast_in_dim.24), channel_id=1, replica_groups=mesh['y'=8,'x'=4,'z'=8,'c'=2] {'c','y'}, dimensions={0} | all-to-all | bytes 65536 | tf_op jit(solution)/shard_map/all_to_all | solution.py:17
  97.3 11.8 %all_to_all.67 = f32[32,1,512]{2,1,0:T(1,128)S(1)} all-to-all(f32[32,1,512]{2,1,0:T(1,128)S(1)} %broadcast_in_dim.25), channel_id=1, replica_groups=mesh['y'=8,'x'=4,'z'=8,'c'=2] {'x','z'}, dimensions={0} | all-to-all | bytes 131072 | tf_op jit(solution)/shard_map/all_to_all | solution.py:17
  109.2 0.5 convolution_convert_fusion.1
  110.1 0.7 pad_maximum_fusion
  110.8 5.4 %all-to-all-start.8 = ((bf16[16,40,256]{2,1,0:T(8,128)(2,1)}), bf16[16,40,256]{2,1,0:T(8,128)(2,1)S(1)}, u32[]{:S(2)}, u32[]{:S(2)}) async-start(bf16[16,40,256]{2,1,0:T(8,128)(2,1)} %pad_maximum_fusion), calls=%async_computation.8 | async-start | bytes 655360 | tf_op jit(solution)/shard_map/all_to_all | solution.py:63
  116.2 1.0 convolution_convert_fusion
  117.2 9.7 %all-to-all-done.8 = bf16[16,40,256]{2,1,0:T(8,128)(2,1)S(1)} async-done(((bf16[16,40,256]{2,1,0:T(8,128)(2,1)}), bf16[16,40,256]{2,1,0:T(8,128)(2,1)S(1)}, u32[]{:S(2)}, u32[]{:S(2)}) %all-to-all-start.8) | async-done | bytes 327712 | tf_op jit(solution)/shard_map/all_to_all | solution.py:63
  127.0 3.9 %all-to-all-start.10 = ((bf16[32,16,256]{2,1,0:T(8,128)(2,1)}), bf16[32,16,256]{2,1,0:T(8,128)(2,1)S(1)}, u32[]{:S(2)}, u32[]{:S(2)}) async-start(bf16[32,16,256]{2,1,0:T(8,128)(2,1)} %bitcast.5), calls=%async_computation.10 | async-start | bytes 524288 | tf_op jit(solution)/shard_map/all_to_all | solution.py:68
  131.0 9.5 %all-to-all-done.10 = bf16[32,16,256]{2,1,0:T(8,128)(2,1)S(1)} async-done(((bf16[32,16,256]{2,1,0:T(8,128)(2,1)}), bf16[32,16,256]{2,1,0:T(8,128)(2,1)S(1)}, u32[]{:S(2)}, u32[]{:S(2)}) %all-to-all-start.10) | async-done | bytes 262176 | tf_op jit(solution)/shard_map/all_to_all | solution.py:68
  140.5 0.7 broadcast_in_dim.26
  141.2 5.9 %all-to-all-start.9 = ((f32[8,32,256]{2,1,0:T(8,128)}), f32[8,32,256]{2,1,0:T(8,128)S(1)}, u32[]{:S(2)}, u32[]{:S(2)}) async-start(f32[8,32,256]{2,1,0:T(8,128)} %broadcast_in_dim.26), calls=%async_computation.9 | async-start | bytes 524288 | tf_op jit(solution)/shard_map/all_to_all | solution.py:17
  147.2 0.7 multiply_subtract_fusion
  147.9 8.7 %all-to-all-done.9 = f32[8,32,256]{2,1,0:T(8,128)S(1)} async-done(((f32[8,32,256]{2,1,0:T(8,128)}), f32[8,32,256]{2,1,0:T(8,128)S(1)}, u32[]{:S(2)}, u32[]{:S(2)}) %all-to-all-start.9) | async-done | bytes 262176 | tf_op jit(solution)/shard_map/all_to_all | solution.py:17
  156.5 0.7 copy.18
  (40 shorter events, 2.3 us)
Async XLA Ops:
  1.6 10.4 %copy-start = (bf16[16,256]{1,0:T(8,128)(2,1)S(1)}, bf16[16,256]{1,0:T(8,128)(2,1)}, u32[]{:S(2)}) copy-start(bf16[16,256]{1,0:T(8,128)(2,1)} %param.2) | copy-start | bytes 24580
  12.7 17.2 %all-to-all-start = ((bf16[32,16,256]{2,1,0:T(8,128)(2,1)}), bf16[32,16,256]{2,1,0:T(8,128)(2,1)S(1)}, u32[]{:S(2)}, u32[]{:S(2)}) async-start(bf16[32,16,256]{2,1,0:T(8,128)(2,1)} %broadcast_in_dim.18), calls=%async_computation | async-start | bytes 524288 | tf_op jit(solution)/shard_map/all_to_all | solution.py:17
  110.8 16.2 %all-to-all-start.8 = ((bf16[16,40,256]{2,1,0:T(8,128)(2,1)}), bf16[16,40,256]{2,1,0:T(8,128)(2,1)S(1)}, u32[]{:S(2)}, u32[]{:S(2)}) async-start(bf16[16,40,256]{2,1,0:T(8,128)(2,1)} %pad_maximum_fusion), calls=%async_computation.8 | async-start | bytes 655360 | tf_op jit(solution)/shard_map/all_to_all | solution.py:63
  127.0 13.5 %all-to-all-start.10 = ((bf16[32,16,256]{2,1,0:T(8,128)(2,1)}), bf16[32,16,256]{2,1,0:T(8,128)(2,1)S(1)}, u32[]{:S(2)}, u32[]{:S(2)}) async-start(bf16[32,16,256]{2,1,0:T(8,128)(2,1)} %bitcast.5), calls=%async_computation.10 | async-start | bytes 524288 | tf_op jit(solution)/shard_map/all_to_all | solution.py:68
  141.2 15.3 %all-to-all-start.9 = ((f32[8,32,256]{2,1,0:T(8,128)}), f32[8,32,256]{2,1,0:T(8,128)S(1)}, u32[]{:S(2)}, u32[]{:S(2)}) async-start(f32[8,32,256]{2,1,0:T(8,128)} %broadcast_in_dim.26), calls=%async_computation.9 | async-start | bytes 524288 | tf_op jit(solution)/shard_map/all_to_all | solution.py:17

commit v3 on v2

--- a/solution.py
+++ b/solution.py
@@ -23,12 +23,16 @@
     codes = codebook.shape[0] * lax.axis_size("c")
     groups = lax.axis_size(ITEM_AXES)
     parts = lax.axis_size(CODE_AXES)
-    codebook = spread(codebook, "c").reshape(codes, width)
     gathered = spread(residuals, CODE_AXES).reshape(items, width)
+    other = lax.ppermute(codebook, "c", [(0, 1), (1, 0)])
+    first = lax.axis_index("c") == 0
+    codebook = jnp.concatenate(
+        [jnp.where(first, codebook, other), jnp.where(first, other, codebook)]
+    )
+    codes_float = codebook.astype(jnp.float32)
+    code_scale = lax.rsqrt(jnp.mean(codes_float * codes_float, axis=1) + EPSILON)
     rows_float = gathered.astype(jnp.float32)
-    codes_float = codebook.astype(jnp.float32)
     row_scale = lax.rsqrt(jnp.mean(rows_float * rows_float, axis=1) + EPSILON)
-    code_scale = lax.rsqrt(jnp.mean(codes_float * codes_float, axis=1) + EPSILON)
     similarity = lax.dot_general(
         gathered, codebook, (((1,), (1,)), ((), ())), preferred_element_type=jnp.float32
     )
@@ -70,7 +74,7 @@
     total = jnp.sum(packed.astype(jnp.float32), axis=0)
     mass_total = total[share, :share] + total[share + 1, :share]
     means = total[:share] / mass_total[:, None]
-    new_codebook = spread(means, "y").reshape(-1, width)
+    new_codebook = lax.all_gather(means, "y", axis=0, tiled=True)
 
     rebuilt = jnp.sum(rebuilt.astype(jnp.float32), axis=0)
     mine = lax.axis_index(CODE_AXES) * rows

time: 160 us -> 166 us (1.038)
  the two profiles are of different devices: /device:TPU:1 before, /device:TPU:64 now
where the time goes in v3:
time: 166 us; the launch traced here: 165 us
  blocking collectives  86.6 us (52%)
  waiting for transfers between devices  41.1 us (25%)
  starting transfers between devices  27.5 us (17%)
  local copies, waits for them, and re-layouts  3.82 us (2%)
  other arithmetic  3.31 us (2%)
  matrix products  1.9 us (1%)
    all_to_all x5, blocking collectives, spread(): return lax.all_to_all(copies, axes, 0, 0, tiled=True)  61.7 us
    all_gather x1, blocking collectives, shards(): new_codebook = lax.all_gather(means, 'y', axis=0, tiled=True)  25 us
    all_to_all x2, waiting for transfers between devices, spread(): return lax.all_to_all(copies, axes, 0, 0, tiled=True)  20.9 us
    all_to_all x2, starting transfers between devices, spread(): return lax.all_to_all(copies, axes, 0, 0, tiled=True)  17.4 us
    all_to_all x1, waiting for transfers between devices, shards(): packed = lax.all_to_all(packed, ITEM_AXES, 0, 0, tiled=True)  10.3 us
    all_to_all x1, waiting for transfers between devices, shards(): rebuilt = lax.all_to_all(rebuilt, CODE_AXES, 0, 0, tiled=True)  9.84 us
    all_to_all x1, starting transfers between devices, shards(): rebuilt = lax.all_to_all(rebuilt, CODE_AXES, 0, 0, tiled=True)  4.67 us
    all_to_all x1, starting transfers between devices, shards(): packed = lax.all_to_all(packed, ITEM_AXES, 0, 0, tiled=True)  3.54 us
  transfers between devices with their start and end apart: 5, of which 4 were waited for; matrix products, arithmetic and copies ran while one was open for 3% of the time, Pallas kernels for 0%

profile of v3, /device:TPU:64, one launch (start us, length us, event | category | flops | bytes accessed | tf_op | source)
XLA Modules:
  0.0 165.1 jit_solution(7260050627973847385)
XLA Ops:
  0.6 1.9 %collective-permute-start = (bf16[256,256]{1,0:T(8,128)(2,1)}, bf16[256,256]{1,0:T(8,128)(2,1)S(1)}, u32[]{:S(2)}, u32[]{:S(2)}) collective-permute-start(bf16[256,256]{1,0:T(8,128)(2,1)} %param.3), channel_id=1, source_target_pairs={{0,1},{1,0},{2,3},{3,2},{4,5},{5,4},{6,7},{7,6},{8,9},{9,8},{10,11... | collective-permute-start | bytes 393224 | tf_op jit(solution)/shard_map/ppermute | solution.py:27
  2.6 1.4 broadcast_in_dim.14
  4.0 12.7 %all-to-all-start = ((bf16[32,16,256]{2,1,0:T(8,128)(2,1)}), bf16[32,16,256]{2,1,0:T(8,128)(2,1)S(1)}, u32[]{:S(2)}, u32[]{:S(2)}) async-start(bf16[32,16,256]{2,1,0:T(8,128)(2,1)} %broadcast_in_dim.14), calls=%async_computation | async-start | bytes 524288 | tf_op jit(solution)/shard_map/all_to_all | solution.py:17
  16.9 12.7 %all-to-all-done = bf16[32,16,256]{2,1,0:T(8,128)(2,1)S(1)} async-done(((bf16[32,16,256]{2,1,0:T(8,128)(2,1)}), bf16[32,16,256]{2,1,0:T(8,128)(2,1)S(1)}, u32[]{:S(2)}, u32[]{:S(2)}) %all-to-all-start) | async-done | bytes 262176 | tf_op jit(solution)/shard_map/all_to_all | solution.py:17
  29.9 0.4 fusion.14
  30.3 14.7 %all_to_all.51 = f32[16,1,512]{2,1,0:T(1,128)S(1)} all-to-all(f32[16,1,512]{2,1,0:T(1,128)S(1)} %broadcast_in_dim.15), channel_id=1, replica_groups=mesh['y'=8,'x'=4,'z'=8,'c'=2] {'c','y'}, dimensions={0} | all-to-all | bytes 65536 | tf_op jit(solution)/shard_map/all_to_all | solution.py:17
  45.3 13.5 %all_to_all.52 = f32[32,1,512]{2,1,0:T(1,128)S(1)} all-to-all(f32[32,1,512]{2,1,0:T(1,128)S(1)} %broadcast_in_dim.16), channel_id=1, replica_groups=mesh['y'=8,'x'=4,'z'=8,'c'=2] {'x','z'}, dimensions={0} | all-to-all | bytes 131072 | tf_op jit(solution)/shard_map/all_to_all | solution.py:17
  59.0 10.2 %all_to_all.53 = f32[16,1,512]{2,1,0:T(1,128)S(1)} all-to-all(f32[16,1,512]{2,1,0:T(1,128)S(1)} %broadcast_in_dim.17), channel_id=1, replica_groups=mesh['y'=8,'x'=4,'z'=8,'c'=2] {'c','y'}, dimensions={0} | all-to-all | bytes 65536 | tf_op jit(solution)/shard_map/all_to_all | solution.py:17
  69.5 13.2 %all_to_all.54 = f32[32,1,512]{2,1,0:T(1,128)S(1)} all-to-all(f32[32,1,512]{2,1,0:T(1,128)S(1)} %broadcast_in_dim.18), channel_id=1, replica_groups=mesh['y'=8,'x'=4,'z'=8,'c'=2] {'x','z'}, dimensions={0} | all-to-all | bytes 131072 | tf_op jit(solution)/shard_map/all_to_all | solution.py:17
  82.9 10.2 %all_to_all.55 = f32[16,1,512]{2,1,0:T(1,128)S(1)} all-to-all(f32[16,1,512]{2,1,0:T(1,128)S(1)} %broadcast_in_dim.19), channel_id=1, replica_groups=mesh['y'=8,'x'=4,'z'=8,'c'=2] {'c','y'}, dimensions={0} | all-to-all | bytes 65536 | tf_op jit(solution)/shard_map/all_to_all | solution.py:17
  93.3 0.7 broadcast_in_dim.20
  93.9 4.7 %all-to-all-start.6 = ((f32[32,1,512]{2,1,0:T(1,128)}), f32[32,1,512]{2,1,0:T(1,128)S(1)}, u32[]{:S(2)}, u32[]{:S(2)}) async-start(f32[32,1,512]{2,1,0:T(1,128)} %broadcast_in_dim.20), calls=%async_computation.6 | async-start | bytes 131072 | tf_op jit(solution)/shard_map/all_to_all | solution.py:17
  98.6 1.0 convolution_convert_fusion
  99.6 8.2 %all-to-all-done.6 = f32[32,1,512]{2,1,0:T(1,128)S(1)} async-done(((f32[32,1,512]{2,1,0:T(1,128)}), f32[32,1,512]{2,1,0:T(1,128)S(1)}, u32[]{:S(2)}, u32[]{:S(2)}) %all-to-all-start.6) | async-done | bytes 65568 | tf_op jit(solution)/shard_map/all_to_all | solution.py:17
  107.8 4.7 %all-to-all-start.8 = ((bf16[32,16,256]{2,1,0:T(8,128)(2,1)}), bf16[32,16,256]{2,1,0:T(8,128)(2,1)S(1)}, u32[]{:S(2)}, u32[]{:S(2)}) async-start(bf16[32,16,256]{2,1,0:T(8,128)(2,1)} %bitcast.3), calls=%async_computation.8 | async-start | bytes 524288 | tf_op jit(solution)/shard_map/all_to_all | solution.py:72
  112.9 0.5 convolution_convert_fusion.1
  113.4 0.7 pad_maximum_fusion
  114.1 9.8 %all-to-all-done.8 = bf16[32,16,256]{2,1,0:T(8,128)(2,1)S(1)} async-done(((bf16[32,16,256]{2,1,0:T(8,128)(2,1)}), bf16[32,16,256]{2,1,0:T(8,128)(2,1)S(1)}, u32[]{:S(2)}, u32[]{:S(2)}) %all-to-all-start.8) | async-done | bytes 262176 | tf_op jit(solution)/shard_map/all_to_all | solution.py:72
  123.9 3.5 %all-to-all-start.7 = ((bf16[16,40,256]{2,1,0:T(8,128)(2,1)}), bf16[16,40,256]{2,1,0:T(8,128)(2,1)S(1)}, u32[]{:S(2)}, u32[]{:S(2)}) async-start(bf16[16,40,256]{2,1,0:T(8,128)(2,1)} %pad_maximum_fusion), calls=%async_computation.7 | async-start | bytes 655360 | tf_op jit(solution)/shard_map/all_to_all | solution.py:67
  127.6 0.6 copy-done.1
  128.3 0.7 multiply_subtract_fusion
  129.0 10.3 %all-to-all-done.7 = bf16[16,40,256]{2,1,0:T(8,128)(2,1)S(1)} async-done(((bf16[16,40,256]{2,1,0:T(8,128)(2,1)}), bf16[16,40,256]{2,1,0:T(8,128)(2,1)S(1)}, u32[]{:S(2)}, u32[]{:S(2)}) %all-to-all-start.7) | async-done | bytes 327712 | tf_op jit(solution)/shard_map/all_to_all | solution.py:67
  139.4 25.0 %all_gather.3 = f32[256,256]{1,0:T(8,128)S(1)} all-gather(f32[32,256]{1,0:T(8,128)S(1)} %slice_divide_fusion), channel_id=1, replica_groups=mesh['y'=8,'x'=4,'z'=8,'c'=2] {'y'}, dimensions={0}, use_global_device_ids=true | all-gather | bytes 294912 | tf_op jit(solution)/shard_map/all_gather | solution.py:77
  164.4 0.7 copy.17
  (41 shorter events, 2.3 us)
Async XLA Ops:
  0.6 16.1 %collective-permute-start = (bf16[256,256]{1,0:T(8,128)(2,1)}, bf16[256,256]{1,0:T(8,128)(2,1)S(1)}, u32[]{:S(2)}, u32[]{:S(2)}) collective-permute-start(bf16[256,256]{1,0:T(8,128)(2,1)} %param.3), channel_id=1, source_target_pairs={{0,1},{1,0},{2,3},{3,2},{4,5},{5,4},{6,7},{7,6},{8,9},{9,8},{10,11... | collective-permute-start | bytes 393224 | tf_op jit(solution)/shard_map/ppermute | solution.py:27
  4.0 12.7 %copy-start = (bf16[256,256]{1,0:T(8,128)(2,1)S(1)}, bf16[256,256]{1,0:T(8,128)(2,1)}, u32[]{:S(2)}) copy-start(bf16[256,256]{1,0:T(8,128)(2,1)} %param.3) | copy-start | bytes 393220
  4.0 25.7 %all-to-all-start = ((bf16[32,16,256]{2,1,0:T(8,128)(2,1)}), bf16[32,16,256]{2,1,0:T(8,128)(2,1)S(1)}, u32[]{:S(2)}, u32[]{:S(2)}) async-start(bf16[32,16,256]{2,1,0:T(8,128)(2,1)} %broadcast_in_dim.14), calls=%async_computation | async-start | bytes 524288 | tf_op jit(solution)/shard_map/all_to_all | solution.py:17
  93.9 13.9 %all-to-all-start.6 = ((f32[32,1,512]{2,1,0:T(1,128)}), f32[32,1,512]{2,1,0:T(1,128)S(1)}, u32[]{:S(2)}, u32[]{:S(2)}) async-start(f32[32,1,512]{2,1,0:T(1,128)} %broadcast_in_dim.20), calls=%async_computation.6 | async-start | bytes 131072 | tf_op jit(solution)/shard_map/all_to_all | solution.py:17
  107.8 16.1 %all-to-all-start.8 = ((bf16[32,16,256]{2,1,0:T(8,128)(2,1)}), bf16[32,16,256]{2,1,0:T(8,128)(2,1)S(1)}, u32[]{:S(2)}, u32[]{:S(2)}) async-start(bf16[32,16,256]{2,1,0:T(8,128)(2,1)} %bitcast.3), calls=%async_computation.8 | async-start | bytes 524288 | tf_op jit(solution)/shard_map/all_to_all | solution.py:72
  123.9 15.3 %all-to-all-start.7 = ((bf16[16,40,256]{2,1,0:T(8,128)(2,1)}), bf16[16,40,256]{2,1,0:T(8,128)(2,1)S(1)}, u32[]{:S(2)}, u32[]{:S(2)}) async-start(bf16[16,40,256]{2,1,0:T(8,128)(2,1)} %pad_maximum_fusion), calls=%async_computation.7 | async-start | bytes 655360 | tf_op jit(solution)/shard_map/all_to_all | solution.py:67
  127.6 0.7 copy-start.1

commit v4 on v3

--- a/solution.py
+++ b/solution.py
@@ -6,6 +6,7 @@
 ITERS = 3
 EPSILON = 1e-06
 SHARPNESS = 40.0
+MEANS = jnp.float16
 
 ITEM_AXES = ("c", "y")
 CODE_AXES = ("x", "z")
@@ -15,6 +16,11 @@
     members = lax.axis_size(axes)
     copies = jnp.broadcast_to(block[None], (members,) + block.shape)
     return lax.all_to_all(copies, axes, 0, 0, tiled=True)
+
+
+def two_terms(values):
+    high = values.astype(jnp.bfloat16)
+    return high, (values - high.astype(jnp.float32)).astype(jnp.bfloat16)
 
 
 def shards(residuals, codebook):
@@ -41,13 +47,28 @@
     )
     balance = (items * groups) / (codes * parts)
     weights_rows = None
-    for _ in range(ITERS):
+    for sweep in range(ITERS):
         scaled = kernel if weights_rows is None else kernel * weights_rows[:, None]
         column_total = jnp.sum(spread(jnp.sum(scaled, axis=0), ITEM_AXES), axis=0)
         weights_cols = balance / column_total
         row_part = jnp.sum(kernel * weights_cols[None, :], axis=1)
-        row_total = jnp.sum(spread(row_part, CODE_AXES), axis=0)
-        weights_rows = 1.0 / row_total
+        if sweep < ITERS - 1:
+            row_total = jnp.sum(spread(row_part, CODE_AXES), axis=0)
+            weights_rows = 1.0 / row_total
+
+    shares = (kernel * weights_cols[None, :]).astype(jnp.bfloat16)
+    products = jnp.dot(shares, codebook, preferred_element_type=jnp.float32)
+    products = products.astype(jnp.bfloat16).reshape(parts, rows, width)
+    terms = jnp.concatenate([t.reshape(-1, width) for t in two_terms(row_part)])
+    extra = terms.shape[0]
+    terms = jnp.pad(terms, ((0, -extra % 8), (0, 0)))
+    terms = jnp.broadcast_to(terms[None], (parts,) + terms.shape)
+    packed = jnp.concatenate([products, terms], axis=1)
+    packed = lax.all_to_all(packed, CODE_AXES, 0, 0, tiled=True)
+    total = jnp.sum(packed.astype(jnp.float32), axis=0)
+    middle = rows + extra // 2
+    row_total = total[rows:middle] + total[middle : rows + extra]
+    weights_rows = 1.0 / row_total.reshape(items)
 
     transport = (
         kernel * weights_rows[:, None] * weights_cols[None, :]
@@ -57,29 +78,22 @@
     )
     mass = jnp.sum(transport.astype(jnp.float32), axis=0)
     share = codes // groups
-    high = mass.astype(jnp.bfloat16)
-    low = (mass - high.astype(jnp.float32)).astype(jnp.bfloat16)
-    masses = jnp.stack([high.reshape(groups, share), low.reshape(groups, share)], axis=1)
+    masses = jnp.stack([t.reshape(groups, share) for t in two_terms(mass)], axis=1)
     masses = jnp.pad(masses, ((0, 0), (0, 6), (0, width - share)))
     packed = jnp.concatenate(
         [numerator.astype(jnp.bfloat16).reshape(groups, share, width), masses], axis=1
     )
     packed = lax.all_to_all(packed, ITEM_AXES, 0, 0, tiled=True)
 
-    shares = (kernel * weights_cols[None, :]).astype(jnp.bfloat16)
-    rebuilt = jnp.dot(shares, codebook, preferred_element_type=jnp.float32)
-    rebuilt = rebuilt.astype(jnp.bfloat16).reshape(parts, rows, width)
-    rebuilt = lax.all_to_all(rebuilt, CODE_AXES, 0, 0, tiled=True)
+    mine = lax.axis_index(CODE_AXES) * rows
+    own = lax.dynamic_slice_in_dim(weights_rows, mine, rows)
+    following = residuals.astype(jnp.float32) - total[:rows] * own[:, None]
 
     total = jnp.sum(packed.astype(jnp.float32), axis=0)
     mass_total = total[share, :share] + total[share + 1, :share]
     means = total[:share] / mass_total[:, None]
-    new_codebook = lax.all_gather(means, "y", axis=0, tiled=True)
-
-    rebuilt = jnp.sum(rebuilt.astype(jnp.float32), axis=0)
-    mine = lax.axis_index(CODE_AXES) * rows
-    own = lax.dynamic_slice_in_dim(weights_rows, mine, rows)
-    following = residuals.astype(jnp.float32) - rebuilt * own[:, None]
+    new_codebook = spread(means.astype(MEANS), "y").reshape(-1, width)
+    new_codebook = new_codebook.astype(jnp.float32)
     return (new_codebook, following)
 
 

time: 166 us -> 144 us (0.87)
  the two profiles are of different devices: /device:TPU:64 before, /device:TPU:1 now
where the time goes in v4:
time: 144 us; the launch traced here: 142 us
  blocking collectives  96.4 us (67%)
  starting transfers between devices  20.9 us (15%)
  waiting for transfers between devices  16.4 us (11%)
  other arithmetic  3.33 us (2%)
  local copies, waits for them, and re-layouts  3.12 us (2%)
    all_to_all x5, blocking collectives, spread(): return lax.all_to_all(copies, axes, 0, 0, tiled=True)  64.8 us
    all_to_all x1, blocking collectives, shards(): packed = lax.all_to_all(packed, ITEM_AXES, 0, 0, tiled=True)  16.9 us
    all_to_all x2, waiting for transfers between devices, spread(): return lax.all_to_all(copies, axes, 0, 0, tiled=True)  16.4 us
    all_to_all x1, blocking collectives, shards(): packed = lax.all_to_all(packed, CODE_AXES, 0, 0, tiled=True)  14.7 us
    all_to_all x2, starting transfers between devices, spread(): return lax.all_to_all(copies, axes, 0, 0, tiled=True)  12.1 us
    ppermute x1, starting transfers between devices, shards(): other = lax.ppermute(codebook, 'c', [(0, 1), (1, 0)])  8.75 us
  transfers between devices with their start and end apart: 3, of which 2 were waited for; matrix products, arithmetic and copies ran while one was open for 2% of the time, Pallas kernels for 0%

profile of v4, /device:TPU:1, one launch (start us, length us, event | category | flops | bytes accessed | tf_op | source)
XLA Modules:
  0.0 142.2 jit_solution(4474674448803900194)
XLA Ops:
  0.6 8.7 %collective-permute-start = (bf16[256,256]{1,0:T(8,128)(2,1)}, bf16[256,256]{1,0:T(8,128)(2,1)S(1)}, u32[]{:S(2)}, u32[]{:S(2)}) collective-permute-start(bf16[256,256]{1,0:T(8,128)(2,1)} %param.3), channel_id=1, source_target_pairs={{0,1},{1,0},{2,3},{3,2},{4,5},{5,4},{6,7},{7,6},{8,9},{9,8},{10,11... | collective-permute-start | bytes 393224 | tf_op jit(solution)/shard_map/ppermute | solution.py:33
  9.4 1.4 broadcast_in_dim.16
  10.8 7.7 %all-to-all-start = ((bf16[32,16,256]{2,1,0:T(8,128)(2,1)}), bf16[32,16,256]{2,1,0:T(8,128)(2,1)S(1)}, u32[]{:S(2)}, u32[]{:S(2)}) async-start(bf16[32,16,256]{2,1,0:T(8,128)(2,1)} %broadcast_in_dim.16), calls=%async_computation | async-start | bytes 524288 | tf_op jit(solution)/shard_map/all_to_all | solution.py:18
  18.7 10.1 %all-to-all-done = bf16[32,16,256]{2,1,0:T(8,128)(2,1)S(1)} async-done(((bf16[32,16,256]{2,1,0:T(8,128)(2,1)}), bf16[32,16,256]{2,1,0:T(8,128)(2,1)S(1)}, u32[]{:S(2)}, u32[]{:S(2)}) %all-to-all-start) | async-done | bytes 262176 | tf_op jit(solution)/shard_map/all_to_all | solution.py:18
  29.0 0.4 fusion.21
  29.5 16.4 %all_to_all.50 = f32[16,1,512]{2,1,0:T(1,128)S(1)} all-to-all(f32[16,1,512]{2,1,0:T(1,128)S(1)} %broadcast_in_dim.17), channel_id=1, replica_groups=mesh['y'=8,'x'=4,'z'=8,'c'=2] {'c','y'}, dimensions={0} | all-to-all | bytes 65536 | tf_op jit(solution)/shard_map/all_to_all | solution.py:18
  46.0 0.2 multiply_reduce_fusion.3
  46.2 13.4 %all_to_all.51 = f32[32,1,512]{2,1,0:T(1,128)S(1)} all-to-all(f32[32,1,512]{2,1,0:T(1,128)S(1)} %broadcast_in_dim.18), channel_id=1, replica_groups=mesh['y'=8,'x'=4,'z'=8,'c'=2] {'x','z'}, dimensions={0} | all-to-all | bytes 131072 | tf_op jit(solution)/shard_map/all_to_all | solution.py:18
  59.7 0.2 multiply_reduce_fusion.2
  59.8 11.6 %all_to_all.52 = f32[16,1,512]{2,1,0:T(1,128)S(1)} all-to-all(f32[16,1,512]{2,1,0:T(1,128)S(1)} %broadcast_in_dim.19), channel_id=1, replica_groups=mesh['y'=8,'x'=4,'z'=8,'c'=2] {'c','y'}, dimensions={0} | all-to-all | bytes 65536 | tf_op jit(solution)/shard_map/all_to_all | solution.py:18
  71.5 0.2 multiply_reduce_fusion.1
  71.7 11.8 %all_to_all.53 = f32[32,1,512]{2,1,0:T(1,128)S(1)} all-to-all(f32[32,1,512]{2,1,0:T(1,128)S(1)} %broadcast_in_dim.20), channel_id=1, replica_groups=mesh['y'=8,'x'=4,'z'=8,'c'=2] {'x','z'}, dimensions={0} | all-to-all | bytes 131072 | tf_op jit(solution)/shard_map/all_to_all | solution.py:18
  83.8 11.5 %all_to_all.54 = f32[16,1,512]{2,1,0:T(1,128)S(1)} all-to-all(f32[16,1,512]{2,1,0:T(1,128)S(1)} %broadcast_in_dim.21), channel_id=1, replica_groups=mesh['y'=8,'x'=4,'z'=8,'c'=2] {'c','y'}, dimensions={0} | all-to-all | bytes 65536 | tf_op jit(solution)/shard_map/all_to_all | solution.py:18
  95.4 0.3 convolution_convert_fusion.1
  95.9 14.7 %all_to_all.55 = bf16[32,24,256]{2,1,0:T(8,128)(2,1)S(1)} all-to-all(bf16[32,24,256]{2,1,0:T(8,128)(2,1)S(1)} %pad_maximum_fusion), channel_id=1, replica_groups=mesh['y'=8,'x'=4,'z'=8,'c'=2] {'x','z'}, dimensions={0} | all-to-all | bytes 786432 | tf_op jit(solution)/shard_map/all_to_all | solution.py:67
  110.7 0.5 convolution_convert_fusion
  111.2 0.2 convert_reduce_fusion
  111.5 16.9 %all_to_all.56 = bf16[16,40,256]{2,1,0:T(8,128)(2,1)S(1)} all-to-all(bf16[16,40,256]{2,1,0:T(8,128)(2,1)S(1)} %pad_maximum_fusion.1), channel_id=1, replica_groups=mesh['y'=8,'x'=4,'z'=8,'c'=2] {'c','y'}, dimensions={0} | all-to-all | bytes 655360 | tf_op jit(solution)/shard_map/all_to_all | solution.py:86
  128.6 0.7 broadcast_in_dim.23
  129.2 4.5 %all-to-all-start.8 = ((f16[8,32,256]{2,1,0:T(8,128)(2,1)}), f16[8,32,256]{2,1,0:T(8,128)(2,1)S(1)}, u32[]{:S(2)}, u32[]{:S(2)}) async-start(f16[8,32,256]{2,1,0:T(8,128)(2,1)} %broadcast_in_dim.23), calls=%async_computation.8 | async-start | bytes 262144 | tf_op jit(solution)/shard_map/all_to_all | solution.py:18
  133.8 0.6 copy-done.1
  134.4 0.7 fusion.11
  135.1 6.4 %all-to-all-done.8 = f16[8,32,256]{2,1,0:T(8,128)(2,1)S(1)} async-done(((f16[8,32,256]{2,1,0:T(8,128)(2,1)}), f16[8,32,256]{2,1,0:T(8,128)(2,1)S(1)}, u32[]{:S(2)}, u32[]{:S(2)}) %all-to-all-start.8) | async-done | bytes 131104 | tf_op jit(solution)/shard_map/all_to_all | solution.py:18
  141.4 0.7 bitcast_convert_fusion
  (43 shorter events, 1.7 us)
Async XLA Ops:
  0.6 17.9 %collective-permute-start = (bf16[256,256]{1,0:T(8,128)(2,1)}, bf16[256,256]{1,0:T(8,128)(2,1)S(1)}, u32[]{:S(2)}, u32[]{:S(2)}) collective-permute-start(bf16[256,256]{1,0:T(8,128)(2,1)} %param.3), channel_id=1, source_target_pairs={{0,1},{1,0},{2,3},{3,2},{4,5},{5,4},{6,7},{7,6},{8,9},{9,8},{10,11... | collective-permute-start | bytes 393224 | tf_op jit(solution)/shard_map/ppermute | solution.py:33
  10.8 7.7 %copy-start = (bf16[256,256]{1,0:T(8,128)(2,1)S(1)}, bf16[256,256]{1,0:T(8,128)(2,1)}, u32[]{:S(2)}) copy-start(bf16[256,256]{1,0:T(8,128)(2,1)} %param.3) | copy-start | bytes 393220
  10.8 18.0 %all-to-all-start = ((bf16[32,16,256]{2,1,0:T(8,128)(2,1)}), bf16[32,16,256]{2,1,0:T(8,128)(2,1)S(1)}, u32[]{:S(2)}, u32[]{:S(2)}) async-start(bf16[32,16,256]{2,1,0:T(8,128)(2,1)} %broadcast_in_dim.16), calls=%async_computation | async-start | bytes 524288 | tf_op jit(solution)/shard_map/all_to_all | solution.py:18
  129.2 12.2 %all-to-all-start.8 = ((f16[8,32,256]{2,1,0:T(8,128)(2,1)}), f16[8,32,256]{2,1,0:T(8,128)(2,1)S(1)}, u32[]{:S(2)}, u32[]{:S(2)}) async-start(f16[8,32,256]{2,1,0:T(8,128)(2,1)} %broadcast_in_dim.23), calls=%async_computation.8 | async-start | bytes 262144 | tf_op jit(solution)/shard_map/all_to_all | solution.py:18
  133.7 0.7 copy-start.1

commit v5 on v4

--- a/solution.py
+++ b/solution.py
@@ -16,6 +16,12 @@
     members = lax.axis_size(axes)
     copies = jnp.broadcast_to(block[None], (members,) + block.shape)
     return lax.all_to_all(copies, axes, 0, 0, tiled=True)
+
+
+def total_over(part, axes):
+    lanes = 256
+    parts = spread(part.astype(jnp.bfloat16).reshape(-1, lanes), axes)
+    return jnp.sum(parts.astype(jnp.float32), axis=0).reshape(part.shape)
 
 
 def two_terms(values):
@@ -49,11 +55,11 @@
     weights_rows = None
     for sweep in range(ITERS):
         scaled = kernel if weights_rows is None else kernel * weights_rows[:, None]
-        column_total = jnp.sum(spread(jnp.sum(scaled, axis=0), ITEM_AXES), axis=0)
+        column_total = total_over(jnp.sum(scaled, axis=0), ITEM_AXES)
         weights_cols = balance / column_total
         row_part = jnp.sum(kernel * weights_cols[None, :], axis=1)
         if sweep < ITERS - 1:
-            row_total = jnp.sum(spread(row_part, CODE_AXES), axis=0)
+            row_total = total_over(row_part, CODE_AXES)
             weights_rows = 1.0 / row_total
 
     shares = (kernel * weights_cols[None, :]).astype(jnp.bfloat16)

time: 144 us -> 143 us (level)
  no operation moved by 1% of the time
where the time goes in v5:
time: 143 us; the launch traced here: 141 us
  blocking collectives  95.6 us (67%)
  starting transfers between devices  20.9 us (15%)
  waiting for transfers between devices  16.4 us (11%)
  local copies, waits for them, and re-layouts  3.19 us (2%)
  other arithmetic  3.15 us (2%)
    all_to_all x5, blocking collectives, spread(): return lax.all_to_all(copies, axes, 0, 0, tiled=True)  64.2 us
    all_to_all x1, blocking collectives, shards(): packed = lax.all_to_all(packed, ITEM_AXES, 0, 0, tiled=True)  16.6 us
    all_to_all x2, waiting for transfers between devices, spread(): return lax.all_to_all(copies, axes, 0, 0, tiled=True)  16.4 us
    all_to_all x1, blocking collectives, shards(): packed = lax.all_to_all(packed, CODE_AXES, 0, 0, tiled=True)  14.8 us
    all_to_all x2, starting transfers between devices, spread(): return lax.all_to_all(copies, axes, 0, 0, tiled=True)  12.1 us
    ppermute x1, starting transfers between devices, shards(): other = lax.ppermute(codebook, 'c', [(0, 1), (1, 0)])  8.75 us
  transfers between devices with their start and end apart: 3, of which 2 were waited for; matrix products, arithmetic and copies ran while one was open for 2% of the time, Pallas kernels for 0%

profile of v5, /device:TPU:1, one launch (start us, length us, event | category | flops | bytes accessed | tf_op | source)
XLA Modules:
  0.0 141.3 jit_solution(16888109660511503155)
XLA Ops:
  0.6 8.7 %collective-permute-start = (bf16[256,256]{1,0:T(8,128)(2,1)}, bf16[256,256]{1,0:T(8,128)(2,1)S(1)}, u32[]{:S(2)}, u32[]{:S(2)}) collective-permute-start(bf16[256,256]{1,0:T(8,128)(2,1)} %param.3), channel_id=1, source_target_pairs={{0,1},{1,0},{2,3},{3,2},{4,5},{5,4},{6,7},{7,6},{8,9},{9,8},{10,11... | collective-permute-start | bytes 393224 | tf_op jit(solution)/shard_map/ppermute | solution.py:39
  9.4 1.4 %broadcast_in_dim.16 = bf16[32,16,256]{2,1,0:T(8,128)(2,1)} broadcast(bf16[16,256]{1,0:T(8,128)(2,1)} %param.2), dimensions={1,2} | broadcast | bytes 270336 | tf_op jit(solution)/shard_map/broadcast_in_dim | solution.py:17
  10.8 7.7 %all-to-all-start = ((bf16[32,16,256]{2,1,0:T(8,128)(2,1)}), bf16[32,16,256]{2,1,0:T(8,128)(2,1)S(1)}, u32[]{:S(2)}, u32[]{:S(2)}) async-start(bf16[32,16,256]{2,1,0:T(8,128)(2,1)} %broadcast_in_dim.16), calls=%async_computation | async-start | bytes 524288 | tf_op jit(solution)/shard_map/all_to_all | solution.py:18
  18.7 10.1 %all-to-all-done = bf16[32,16,256]{2,1,0:T(8,128)(2,1)S(1)} async-done(((bf16[32,16,256]{2,1,0:T(8,128)(2,1)}), bf16[32,16,256]{2,1,0:T(8,128)(2,1)S(1)}, u32[]{:S(2)}, u32[]{:S(2)}) %all-to-all-start) | async-done | bytes 262176 | tf_op jit(solution)/shard_map/all_to_all | solution.py:18
  29.0 0.4 fusion.21
  29.5 16.4 %all_to_all.45 = bf16[16,2,256]{2,1,0:T(2,128)(2,1)S(1)} all-to-all(bf16[16,2,256]{2,1,0:T(2,128)(2,1)S(1)} %broadcast_in_dim.17), channel_id=1, replica_groups=mesh['y'=8,'x'=4,'z'=8,'c'=2] {'c','y'}, dimensions={0} | all-to-all | bytes 32768 | tf_op jit(solution)/shard_map/all_to_all | solution.py:18
  45.9 0.2 multiply_reduce_fusion.3
  46.1 13.3 %all_to_all.46 = bf16[32,2,256]{2,1,0:T(2,128)(2,1)S(1)} all-to-all(bf16[32,2,256]{2,1,0:T(2,128)(2,1)S(1)} %broadcast_in_dim.18), channel_id=1, replica_groups=mesh['y'=8,'x'=4,'z'=8,'c'=2] {'x','z'}, dimensions={0} | all-to-all | bytes 65536 | tf_op jit(solution)/shard_map/all_to_all | solution.py:18
  59.5 0.2 multiply_reduce_fusion.2
  59.7 11.6 %all_to_all.47 = bf16[16,2,256]{2,1,0:T(2,128)(2,1)S(1)} all-to-all(bf16[16,2,256]{2,1,0:T(2,128)(2,1)S(1)} %broadcast_in_dim.19), channel_id=1, replica_groups=mesh['y'=8,'x'=4,'z'=8,'c'=2] {'c','y'}, dimensions={0} | all-to-all | bytes 32768 | tf_op jit(solution)/shard_map/all_to_all | solution.py:18
  71.3 0.2 multiply_reduce_fusion.1
  71.5 11.7 %all_to_all.48 = bf16[32,2,256]{2,1,0:T(2,128)(2,1)S(1)} all-to-all(bf16[32,2,256]{2,1,0:T(2,128)(2,1)S(1)} %broadcast_in_dim.20), channel_id=1, replica_groups=mesh['y'=8,'x'=4,'z'=8,'c'=2] {'x','z'}, dimensions={0} | all-to-all | bytes 65536 | tf_op jit(solution)/shard_map/all_to_all | solution.py:18
  83.4 11.3 %all_to_all.49 = bf16[16,2,256]{2,1,0:T(2,128)(2,1)S(1)} all-to-all(bf16[16,2,256]{2,1,0:T(2,128)(2,1)S(1)} %broadcast_in_dim.21), channel_id=1, replica_groups=mesh['y'=8,'x'=4,'z'=8,'c'=2] {'c','y'}, dimensions={0} | all-to-all | bytes 32768 | tf_op jit(solution)/shard_map/all_to_all | solution.py:18
  94.7 0.3 convolution_convert_fusion.1
  95.3 14.8 %all_to_all.50 = bf16[32,24,256]{2,1,0:T(8,128)(2,1)S(1)} all-to-all(bf16[32,24,256]{2,1,0:T(8,128)(2,1)S(1)} %pad_maximum_fusion), channel_id=1, replica_groups=mesh['y'=8,'x'=4,'z'=8,'c'=2] {'x','z'}, dimensions={0} | all-to-all | bytes 786432 | tf_op jit(solution)/shard_map/all_to_all | solution.py:73
  110.1 0.5 convolution_convert_fusion
  110.6 0.2 convert_reduce_fusion
  111.0 16.6 %all_to_all.51 = bf16[16,40,256]{2,1,0:T(8,128)(2,1)S(1)} all-to-all(bf16[16,40,256]{2,1,0:T(8,128)(2,1)S(1)} %pad_maximum_fusion.1), channel_id=1, replica_groups=mesh['y'=8,'x'=4,'z'=8,'c'=2] {'c','y'}, dimensions={0} | all-to-all | bytes 655360 | tf_op jit(solution)/shard_map/all_to_all | solution.py:92
  127.7 0.7 broadcast_in_dim.23
  128.4 4.5 %all-to-all-start.8 = ((f16[8,32,256]{2,1,0:T(8,128)(2,1)}), f16[8,32,256]{2,1,0:T(8,128)(2,1)S(1)}, u32[]{:S(2)}, u32[]{:S(2)}) async-start(f16[8,32,256]{2,1,0:T(8,128)(2,1)} %broadcast_in_dim.23), calls=%async_computation.8 | async-start | bytes 262144 | tf_op jit(solution)/shard_map/all_to_all | solution.py:18
  132.9 0.6 copy-done.1
  133.5 0.7 fusion.11
  134.2 6.4 %all-to-all-done.8 = f16[8,32,256]{2,1,0:T(8,128)(2,1)S(1)} async-done(((f16[8,32,256]{2,1,0:T(8,128)(2,1)}), f16[8,32,256]{2,1,0:T(8,128)(2,1)S(1)}, u32[]{:S(2)}, u32[]{:S(2)}) %all-to-all-start.8) | async-done | bytes 131104 | tf_op jit(solution)/shard_map/all_to_all | solution.py:18
  140.6 0.7 bitcast_convert_fusion
  (53 shorter events, 1.6 us)
Async XLA Ops:
  0.6 17.9 %collective-permute-start = (bf16[256,256]{1,0:T(8,128)(2,1)}, bf16[256,256]{1,0:T(8,128)(2,1)S(1)}, u32[]{:S(2)}, u32[]{:S(2)}) collective-permute-start(bf16[256,256]{1,0:T(8,128)(2,1)} %param.3), channel_id=1, source_target_pairs={{0,1},{1,0},{2,3},{3,2},{4,5},{5,4},{6,7},{7,6},{8,9},{9,8},{10,11... | collective-permute-start | bytes 393224 | tf_op jit(solution)/shard_map/ppermute | solution.py:39
  10.8 7.7 %copy-start = (bf16[256,256]{1,0:T(8,128)(2,1)S(1)}, bf16[256,256]{1,0:T(8,128)(2,1)}, u32[]{:S(2)}) copy-start(bf16[256,256]{1,0:T(8,128)(2,1)} %param.3) | copy-start | bytes 393220
  10.8 18.0 %all-to-all-start = ((bf16[32,16,256]{2,1,0:T(8,128)(2,1)}), bf16[32,16,256]{2,1,0:T(8,128)(2,1)S(1)}, u32[]{:S(2)}, u32[]{:S(2)}) async-start(bf16[32,16,256]{2,1,0:T(8,128)(2,1)} %broadcast_in_dim.16), calls=%async_computation | async-start | bytes 524288 | tf_op jit(solution)/shard_map/all_to_all | solution.py:18
  128.4 12.2 %all-to-all-start.8 = ((f16[8,32,256]{2,1,0:T(8,128)(2,1)}), f16[8,32,256]{2,1,0:T(8,128)(2,1)S(1)}, u32[]{:S(2)}, u32[]{:S(2)}) async-start(f16[8,32,256]{2,1,0:T(8,128)(2,1)} %broadcast_in_dim.23), calls=%async_computation.8 | async-start | bytes 262144 | tf_op jit(solution)/shard_map/all_to_all | solution.py:18
  132.8 0.7 copy-start.1

commit v6 on v4

v6 whole, which is shorter than its diff:
```python
import jax
import jax.numpy as jnp
from jax import lax
from jax.sharding import Mesh, PartitionSpec as P

ITERS = 3
EPSILON = 1e-06
SHARPNESS = 40.0
MEANS = jnp.float16

ITEM_AXES = ("x", "c", "l")


def spread(block, axes):
    members = lax.axis_size(axes)
    copies = jnp.broadcast_to(block[None], (members,) + block.shape)
    return lax.all_to_all(copies, axes, 0, 0, tiled=True)


def two_terms(values):
    high = values.astype(jnp.bfloat16)
    return high, (values - high.astype(jnp.float32)).astype(jnp.bfloat16)


def gather_codes(codebook):
    width = codebook.shape[1]
    across = lax.axis_size("x")
    pieces = lax.axis_size("h")
    blocks = [codebook]
    for step in range(1, across):
        ring = [(i, (i + step) % across) for i in range(across)]
        blocks.append(lax.ppermute(codebook, "x", ring))
    doubled = jnp.stack(blocks[::-1] * 2)
    first = across - 1 - lax.axis_index("x")
    own = lax.dynamic_slice_in_dim(doubled, first, across)
    other = lax.ppermute(own, "c", [(0, 1), (1, 0)])
    zero = lax.axis_index("c") == 0
    both = jnp.stack([jnp.where(zero, own, other), jnp.where(zero, other, own)], axis=1)
    both = both.reshape(across * 2, pieces, -1, width)
    return both.transpose(1, 0, 2, 3)


def shards(residuals, codebook):
    rows, width = residuals.shape
    pieces = lax.axis_size("h")
    depth = lax.axis_size("z")
    groups = lax.axis_size(ITEM_AXES)
    items = rows * pieces * depth
    share = codebook.shape[0] // lax.axis_size(("h", "l"))
    codes = codebook.shape[0] * lax.axis_size(("x", "c"))
    piece = lax.axis_index("h").astype(jnp.uint32)
    first = piece * (rows * depth)
    own_at = first + lax.axis_index("z").astype(jnp.uint32) * rows
    gathered = spread(residuals, ("h", "z")).reshape(items, width)
    codebook = gather_codes(codebook).reshape(pieces, -1, width)
    codes_float = codebook.astype(jnp.float32)
    code_scale = lax.rsqrt(jnp.mean(codes_float * codes_float, axis=2) + EPSILON)
    code_scale, piece, first, own_at = lax.optimization_barrier(
        (code_scale, piece, first, own_at)
    )
    rows_float = gathered.astype(jnp.float32)
    row_scale = lax.rsqrt(jnp.mean(rows_float * rows_float, axis=1) + EPSILON)
    row_scale = row_scale * (SHARPNESS / width)

    def kernel_of(codes, scales):
        similarity = jnp.einsum("nd,...kd->...nk", gathered, codes, preferred_element_type=jnp.float32)
        return jnp.exp(similarity * row_scale[:, None] * scales[..., None, :])

    kernel = kernel_of(codebook, code_scale).astype(jnp.bfloat16)
    own_kernel = kernel_of(
        lax.dynamic_index_in_dim(codebook, piece, keepdims=False),
        lax.dynamic_index_in_dim(code_scale, piece, keepdims=False),
    )
    kernel, own_kernel = lax.optimization_barrier((kernel, own_kernel))
    balance = (items * groups) / (codes * depth)
    weights_rows = None
    for sweep in range(ITERS):
        scaled = kernel.astype(jnp.float32)
        if weights_rows is not None:
            scaled = scaled * weights_rows[None, :, None]
        column_total = jnp.sum(spread(jnp.sum(scaled, axis=1), ITEM_AXES), axis=0)
        weights_cols = balance / column_total
        row_part = jnp.sum(
            kernel.astype(jnp.float32) * weights_cols[:, None, :], axis=(0, 2)
        )
        if sweep < ITERS - 1:
            row_total = jnp.sum(spread(row_part, "z"), axis=0)
            weights_rows = 1.0 / row_total

    mine = lax.dynamic_slice_in_dim(kernel, first, rows * depth, axis=1)
    shares = (mine.astype(jnp.float32) * weights_cols[:, None, :]).astype(jnp.bfloat16)
    products = jnp.einsum(
        "pnk,pkd->nd", shares, codebook, preferred_element_type=jnp.float32
    )
    products = products.astype(jnp.bfloat16).reshape(depth, rows, width)
    terms = jnp.concatenate([t.reshape(-1, width) for t in two_terms(row_part)])
    extra = terms.shape[0]
    terms = jnp.pad(terms, ((0, -extra % 8), (0, 0)))
    terms = jnp.broadcast_to(terms[None], (depth,) + terms.shape)
    packed = jnp.concatenate([products, terms], axis=1)
    weights_cols = lax.dynamic_index_in_dim(weights_cols, piece, keepdims=False)
    packed, weights_cols = lax.optimization_barrier((packed, weights_cols))
    packed = lax.all_to_all(packed, "z", 0, 0, tiled=True)
    total = jnp.sum(packed.astype(jnp.float32), axis=0)
    middle = rows + extra // 2
    row_total = total[rows:middle] + total[middle : rows + extra]
    weights_rows = 1.0 / row_total.reshape(items)

    transport = (own_kernel * weights_rows[:, None] * weights_cols[None, :]).astype(jnp.bfloat16)
    numerator = lax.dot_general(
        transport, gathered, (((0,), (0,)), ((), ())), preferred_element_type=jnp.float32
    )
    mass = jnp.sum(transport.astype(jnp.float32), axis=0)
    masses = jnp.stack([t.reshape(groups, share) for t in two_terms(mass)], axis=1)
    masses = jnp.pad(masses, ((0, 0), (0, 6), (0, width - share)))
    packed = jnp.concatenate(
        [numerator.astype(jnp.bfloat16).reshape(groups, share, width), masses], axis=1
    )
    packed = lax.all_to_all(packed, ITEM_AXES, 0, 0, tiled=True)

    own = lax.dynamic_slice_in_dim(weights_rows, own_at, rows)
    following = residuals.astype(jnp.float32) - total[:rows] * own[:, None]

    total = jnp.sum(packed.astype(jnp.float32), axis=0)
    mass_total = total[share, :share] + total[share + 1, :share]
    means = total[:share] / mass_total[:, None]
    new_codebook = spread(means.astype(MEANS), ("h", "l")).reshape(-1, width)
    new_codebook = new_codebook.astype(jnp.float32)
    return (new_codebook, following)


def solution(mesh):
    fine = Mesh(mesh.devices.reshape(4, 2, 4, 8, 2), ("h", "l", "x", "z", "c"))
    return jax.shard_map(
        shards,
        mesh=fine,
        in_specs=(P(("h", "l", "x", "z", "c"), None), P(("x", "z", "c"), None)),
        out_specs=(P(("x", "z", "c"), None), P(("h", "l", "x", "z", "c"), None)),
        check_vma=False,
    )
```

time: 144 us -> 138 us (0.958)
  blocking collectives: 96.4 us -> 74.6 us
  starting transfers between devices: 20.9 us -> 33 us
  other arithmetic: 3.33 us -> 5.62 us
  matrix products: 1.2 us -> 3.26 us
    all_to_all x5, blocking collectives: 64.8 us -> 52.7 us  [spread(): return lax.all_to_all(copies, axes, 0, 0, tiled=True)]
    all_to_all x2, starting transfers between devices: 12.1 us -> 19.1 us  [spread(): return lax.all_to_all(copies, axes, 0, 0, tiled=True)]
    ppermute x1 -> x4, starting transfers between devices: 8.75 us -> 14 us  [the longest x3 10.3 us: gather_codes(): blocks.append(lax.ppermute(codebook, 'x', ring))]
    all_to_all x1, blocking collectives: 16.9 us -> 12 us  [shards(): packed = lax.all_to_all(packed, ITEM_AXES, 0, 0, tiled=True)]
    all_to_all x1, blocking collectives: 14.7 us -> 9.92 us  [shards(): packed = lax.all_to_all(packed, 'z', 0, 0, tiled=True)]
    dot_general x2 -> x3, matrix products: 0.72 us -> 2.92 us  [the longest x2 2.14 us: kernel_of(): jnp.einsum('nd,...kd->...nk', gathered, codes, preferred_element_type=jnp...]
    reduce_sum x11 -> x12, other arithmetic: 1.19 us -> 3.34 us  [the longest x3 1.47 us: shards(): jnp.sum(kernel.astype(jnp.float32) * weights_cols[:, None, :], axis=(0, 2))]
  transfers between devices with their start and end apart: 3 -> 6, of which waited for: 2 -> 2; matrix products, arithmetic and copies ran while one was open for 2% -> 3% of each run, Pallas kernels for 0% -> 0%
where the time goes in v6:
time: 138 us; the launch traced here: 137 us
  blocking collectives  74.6 us (54%)
  starting transfers between devices  33 us (24%)
  waiting for transfers between devices  15 us (11%)
  other arithmetic  5.62 us (4%)
  local copies, waits for them, and re-layouts  4.43 us (3%)
  matrix products  3.26 us (2%)
    all_to_all x5, blocking collectives, spread(): return lax.all_to_all(copies, axes, 0, 0, tiled=True)  52.7 us
    all_to_all x2, starting transfers between devices, spread(): return lax.all_to_all(copies, axes, 0, 0, tiled=True)  19.1 us
    all_to_all x2, waiting for transfers between devices, spread(): return lax.all_to_all(copies, axes, 0, 0, tiled=True)  15 us
    all_to_all x1, blocking collectives, shards(): packed = lax.all_to_all(packed, ITEM_AXES, 0, 0, tiled=True)  12 us
    ppermute x3, starting transfers between devices, gather_codes(): blocks.append(lax.ppermute(codebook, 'x', ring))  10.3 us
    all_to_all x1, blocking collectives, shards(): packed = lax.all_to_all(packed, 'z', 0, 0, tiled=True)  9.92 us
    ppermute x1, starting transfers between devices, gather_codes(): other = lax.ppermute(own, 'c', [(0, 1), (1, 0)])  3.7 us
  transfers between devices with their start and end apart: 6, of which 2 were waited for; matrix products, arithmetic and copies ran while one was open for 3% of the time, Pallas kernels for 0%

profile of v6, /device:TPU:1, one launch (start us, length us, event | category | flops | bytes accessed | tf_op | source)
XLA Modules:
  0.0 137.0 jit_solution(72028892439021730)
XLA Ops:
  0.6 5.3 %collective-permute-start = (bf16[256,256]{1,0:T(8,128)(2,1)}, bf16[256,256]{1,0:T(8,128)(2,1)S(1)}, u32[]{:S(2)}, u32[]{:S(2)}) collective-permute-start(bf16[256,256]{1,0:T(8,128)(2,1)} %param.3), channel_id=1, source_target_pairs={{0,48},{16,0},{32,16},{48,32},{1,49},{17,1},{33,17},{49,33},{2,50}... | collective-permute-start | bytes 393224 | tf_op jit(solution)/shard_map/ppermute | solution.py:32
  6.0 2.4 %collective-permute-start.1 = (bf16[256,256]{1,0:T(8,128)(2,1)}, bf16[256,256]{1,0:T(8,128)(2,1)S(1)}, u32[]{:S(2)}, u32[]{:S(2)}) collective-permute-start(bf16[256,256]{1,0:T(8,128)(2,1)} %param.3), channel_id=1, source_target_pairs={{0,32},{16,48},{32,0},{48,16},{1,33},{17,49},{33,1},{49,17},{2,34}... | collective-permute-start | bytes 393224 | tf_op jit(solution)/shard_map/ppermute | solution.py:32
  8.4 2.5 %collective-permute-start.2 = (bf16[256,256]{1,0:T(8,128)(2,1)}, bf16[256,256]{1,0:T(8,128)(2,1)S(1)}, u32[]{:S(2)}, u32[]{:S(2)}) collective-permute-start(bf16[256,256]{1,0:T(8,128)(2,1)} %param.3), channel_id=1, source_target_pairs={{0,16},{16,32},{32,48},{48,0},{1,17},{17,33},{33,49},{49,1},{2,18}... | collective-permute-start | bytes 393224 | tf_op jit(solution)/shard_map/ppermute | solution.py:32
  10.9 1.4 %broadcast_in_dim.16 = bf16[32,16,256]{2,1,0:T(8,128)(2,1)} broadcast(bf16[16,256]{1,0:T(8,128)(2,1)} %param.2), dimensions={1,2} | broadcast | bytes 270336 | tf_op jit(solution)/shard_map/broadcast_in_dim | solution.py:16
  12.4 15.7 %all-to-all-start = ((bf16[32,16,256]{2,1,0:T(8,128)(2,1)}), bf16[32,16,256]{2,1,0:T(8,128)(2,1)S(1)}, u32[]{:S(2)}, u32[]{:S(2)}) async-start(bf16[32,16,256]{2,1,0:T(8,128)(2,1)} %broadcast_in_dim.16), calls=%async_computation | async-start | bytes 524288 | tf_op jit(solution)/shard_map/all_to_all | solution.py:17
  28.2 0.9 bitcast_dynamic-update-slice_fusion
  29.2 3.7 %collective-permute-start.3 = (bf16[4,256,256]{2,1,0:T(8,128)(2,1)S(1)}, bf16[4,256,256]{2,1,0:T(8,128)(2,1)S(1)}, u32[]{:S(2)}, u32[]{:S(2)}) collective-permute-start(bf16[4,256,256]{2,1,0:T(8,128)(2,1)S(1)} %constant_dynamic-slice_fusion.2), channel_id=1, source_target_pairs={{0,1},{1,0},{2,3},{3,2},{4,5},{5,4},{6,7},{7,6},{8,9},{9,8},{10,11... | collective-permute-start | bytes 1572872 | tf_op jit(solution)/shard_map/ppermute | solution.py:36
  32.9 7.4 %all-to-all-done = bf16[32,16,256]{2,1,0:T(8,128)(2,1)S(1)} async-done(((bf16[32,16,256]{2,1,0:T(8,128)(2,1)}), bf16[32,16,256]{2,1,0:T(8,128)(2,1)S(1)}, u32[]{:S(2)}, u32[]{:S(2)}) %all-to-all-start) | async-done | bytes 262176 | tf_op jit(solution)/shard_map/all_to_all | solution.py:17
  41.4 0.8 fusion.5
  42.2 1.3 fusion.8
  43.9 13.3 %all_to_all.47 = f32[16,4,512]{2,1,0:T(4,128)S(1)} all-to-all(f32[16,4,512]{2,1,0:T(4,128)S(1)} %broadcast_in_dim.17), channel_id=1, replica_groups=mesh['h'=4,'l'=2,'x'=4,'z'=8,'c'=2] {'x','c','l'}, dimensions={0} | all-to-all | bytes 262144 | tf_op jit(solution)/shard_map/all_to_all | solution.py:17
  57.8 9.4 %all_to_all.48 = f32[8,1,512]{2,1,0:T(1,128)S(1)} all-to-all(f32[8,1,512]{2,1,0:T(1,128)S(1)} %broadcast_in_dim.18), channel_id=1, replica_groups=mesh['h'=4,'l'=2,'x'=4,'z'=8,'c'=2] {'z'}, dimensions={0} | all-to-all | bytes 32768 | tf_op jit(solution)/shard_map/all_to_all | solution.py:17
  67.8 10.6 %all_to_all.49 = f32[16,4,512]{2,1,0:T(4,128)S(1)} all-to-all(f32[16,4,512]{2,1,0:T(4,128)S(1)} %broadcast_in_dim.19), channel_id=1, replica_groups=mesh['h'=4,'l'=2,'x'=4,'z'=8,'c'=2] {'x','c','l'}, dimensions={0} | all-to-all | bytes 262144 | tf_op jit(solution)/shard_map/all_to_all | solution.py:17
  79.0 9.0 %all_to_all.50 = f32[8,1,512]{2,1,0:T(1,128)S(1)} all-to-all(f32[8,1,512]{2,1,0:T(1,128)S(1)} %broadcast_in_dim.20), channel_id=1, replica_groups=mesh['h'=4,'l'=2,'x'=4,'z'=8,'c'=2] {'z'}, dimensions={0} | all-to-all | bytes 32768 | tf_op jit(solution)/shard_map/all_to_all | solution.py:17
  88.5 10.3 %all_to_all.51 = f32[16,4,512]{2,1,0:T(4,128)S(1)} all-to-all(f32[16,4,512]{2,1,0:T(4,128)S(1)} %broadcast_in_dim.21), channel_id=1, replica_groups=mesh['h'=4,'l'=2,'x'=4,'z'=8,'c'=2] {'x','c','l'}, dimensions={0} | all-to-all | bytes 262144 | tf_op jit(solution)/shard_map/all_to_all | solution.py:17
  99.4 0.7 copy-done.1
  100.1 0.8 fusion.9
  101.0 9.9 %all_to_all.52 = bf16[8,24,256]{2,1,0:T(8,128)(2,1)S(1)} all-to-all(bf16[8,24,256]{2,1,0:T(8,128)(2,1)S(1)} %pad_maximum_fusion.2), channel_id=1, replica_groups=mesh['h'=4,'l'=2,'x'=4,'z'=8,'c'=2] {'z'}, dimensions={0} | all-to-all | bytes 196608 | tf_op jit(solution)/shard_map/all_to_all | solution.py:103
  111.7 12.0 %all_to_all.53 = bf16[16,40,256]{2,1,0:T(8,128)(2,1)S(1)} all-to-all(bf16[16,40,256]{2,1,0:T(8,128)(2,1)S(1)} %pad_maximum_fusion.1), channel_id=1, replica_groups=mesh['h'=4,'l'=2,'x'=4,'z'=8,'c'=2] {'x','c','l'}, dimensions={0} | all-to-all | bytes 655360 | tf_op jit(solution)/shard_map/all_to_all | solution.py:119
  123.8 0.7 broadcast_in_dim.23
  124.5 3.4 %all-to-all-start.8 = ((f16[8,32,256]{2,1,0:T(8,128)(2,1)}), f16[8,32,256]{2,1,0:T(8,128)(2,1)S(1)}, u32[]{:S(2)}, u32[]{:S(2)}) async-start(f16[8,32,256]{2,1,0:T(8,128)(2,1)} %broadcast_in_dim.23), calls=%async_computation.8 | async-start | bytes 262144 | tf_op jit(solution)/shard_map/all_to_all | solution.py:17
  128.0 0.7 fusion.21
  128.6 7.6 %all-to-all-done.8 = f16[8,32,256]{2,1,0:T(8,128)(2,1)S(1)} async-done(((f16[8,32,256]{2,1,0:T(8,128)(2,1)}), f16[8,32,256]{2,1,0:T(8,128)(2,1)S(1)}, u32[]{:S(2)}, u32[]{:S(2)}) %all-to-all-start.8) | async-done | bytes 131104 | tf_op jit(solution)/shard_map/all_to_all | solution.py:17
  136.3 0.7 bitcast_convert_fusion
  (69 shorter events, 5.3 us)
Async XLA Ops:
  0.6 28.5 %copy-start.2 = (bf16[256,256]{1,0:T(8,128)(2,1)S(1)}, bf16[256,256]{1,0:T(8,128)(2,1)}, u32[]{:S(2)}) copy-start(bf16[256,256]{1,0:T(8,128)(2,1)} %param.3) | copy-start | bytes 393220
  0.6 27.4 %collective-permute-start = (bf16[256,256]{1,0:T(8,128)(2,1)}, bf16[256,256]{1,0:T(8,128)(2,1)S(1)}, u32[]{:S(2)}, u32[]{:S(2)}) collective-permute-start(bf16[256,256]{1,0:T(8,128)(2,1)} %param.3), channel_id=1, source_target_pairs={{0,48},{16,0},{32,16},{48,32},{1,49},{17,1},{33,17},{49,33},{2,50}... | collective-permute-start | bytes 393224 | tf_op jit(solution)/shard_map/ppermute | solution.py:32
  6.0 22.1 %collective-permute-start.1 = (bf16[256,256]{1,0:T(8,128)(2,1)}, bf16[256,256]{1,0:T(8,128)(2,1)S(1)}, u32[]{:S(2)}, u32[]{:S(2)}) collective-permute-start(bf16[256,256]{1,0:T(8,128)(2,1)} %param.3), channel_id=1, source_target_pairs={{0,32},{16,48},{32,0},{48,16},{1,33},{17,49},{33,1},{49,17},{2,34}... | collective-permute-start | bytes 393224 | tf_op jit(solution)/shard_map/ppermute | solution.py:32
  8.4 19.7 %collective-permute-start.2 = (bf16[256,256]{1,0:T(8,128)(2,1)}, bf16[256,256]{1,0:T(8,128)(2,1)S(1)}, u32[]{:S(2)}, u32[]{:S(2)}) collective-permute-start(bf16[256,256]{1,0:T(8,128)(2,1)} %param.3), channel_id=1, source_target_pairs={{0,16},{16,32},{32,48},{48,0},{1,17},{17,33},{33,49},{49,1},{2,18}... | collective-permute-start | bytes 393224 | tf_op jit(solution)/shard_map/ppermute | solution.py:32
  12.4 28.0 %all-to-all-start = ((bf16[32,16,256]{2,1,0:T(8,128)(2,1)}), bf16[32,16,256]{2,1,0:T(8,128)(2,1)S(1)}, u32[]{:S(2)}, u32[]{:S(2)}) async-start(bf16[32,16,256]{2,1,0:T(8,128)(2,1)} %broadcast_in_dim.16), calls=%async_computation | async-start | bytes 524288 | tf_op jit(solution)/shard_map/all_to_all | solution.py:17
  29.2 11.4 %collective-permute-start.3 = (bf16[4,256,256]{2,1,0:T(8,128)(2,1)S(1)}, bf16[4,256,256]{2,1,0:T(8,128)(2,1)S(1)}, u32[]{:S(2)}, u32[]{:S(2)}) collective-permute-start(bf16[4,256,256]{2,1,0:T(8,128)(2,1)S(1)} %constant_dynamic-slice_fusion.2), channel_id=1, source_target_pairs={{0,1},{1,0},{2,3},{3,2},{4,5},{5,4},{6,7},{7,6},{8,9},{9,8},{10,11... | collective-permute-start | bytes 1572872 | tf_op jit(solution)/shard_map/ppermute | solution.py:36
  41.3 1.0 copy-start
  98.9 1.2 copy-start.1
  110.9 17.0 %copy-start.3 = (bf16[16,256]{1,0:T(8,128)(2,1)S(1)}, bf16[16,256]{1,0:T(8,128)(2,1)}, u32[]{:S(2)}) copy-start(bf16[16,256]{1,0:T(8,128)(2,1)} %param.2) | copy-start | bytes 24580
  124.5 11.8 %all-to-all-start.8 = ((f16[8,32,256]{2,1,0:T(8,128)(2,1)}), f16[8,32,256]{2,1,0:T(8,128)(2,1)S(1)}, u32[]{:S(2)}, u32[]{:S(2)}) async-start(f16[8,32,256]{2,1,0:T(8,128)(2,1)} %broadcast_in_dim.23), calls=%async_computation.8 | async-start | bytes 262144 | tf_op jit(solution)/shard_map/all_to_all | solution.py:17

commit v7 on v6

--- a/solution.py
+++ b/solution.py
@@ -22,22 +22,34 @@
     return high, (values - high.astype(jnp.float32)).astype(jnp.bfloat16)
 
 
-def gather_codes(codebook):
+def turned(array, start, axis):
+    count = array.shape[axis]
+    return jnp.stack(
+        [
+            lax.dynamic_index_in_dim(array, (start + step) % count, axis, keepdims=False)
+            for step in range(count)
+        ]
+    )
+
+
+def ordered(first, mine, other):
+    return jnp.concatenate([jnp.where(first, mine, other), jnp.where(first, other, mine)])
+
+
+def gather_codes(codebook, piece):
     width = codebook.shape[1]
-    across = lax.axis_size("x")
     pieces = lax.axis_size("h")
-    blocks = [codebook]
-    for step in range(1, across):
-        ring = [(i, (i + step) % across) for i in range(across)]
-        blocks.append(lax.ppermute(codebook, "x", ring))
-    doubled = jnp.stack(blocks[::-1] * 2)
-    first = across - 1 - lax.axis_index("x")
-    own = lax.dynamic_slice_in_dim(doubled, first, across)
-    other = lax.ppermute(own, "c", [(0, 1), (1, 0)])
+    place = lax.axis_index("x")
+    block = codebook[None]
+    other = lax.ppermute(block, "x", [(0, 1), (1, 0), (2, 3), (3, 2)])
+    block = ordered(place % 2 == 0, block, other)
+    other = lax.ppermute(block, "x", [(0, 3), (3, 0), (1, 2), (2, 1)])
+    block = ordered(place < 2, block, other)
+    other = lax.ppermute(block, "c", [(0, 1), (1, 0)])
     zero = lax.axis_index("c") == 0
-    both = jnp.stack([jnp.where(zero, own, other), jnp.where(zero, other, own)], axis=1)
-    both = both.reshape(across * 2, pieces, -1, width)
-    return both.transpose(1, 0, 2, 3)
+    both = jnp.stack([jnp.where(zero, block, other), jnp.where(zero, other, block)], axis=1)
+    both = both.reshape(block.shape[0] * 2, pieces, -1, width)
+    return turned(both, piece, 1).reshape(pieces, -1, width)
 
 
 def shards(residuals, codebook):
@@ -49,15 +61,13 @@
     share = codebook.shape[0] // lax.axis_size(("h", "l"))
     codes = codebook.shape[0] * lax.axis_size(("x", "c"))
     piece = lax.axis_index("h").astype(jnp.uint32)
-    first = piece * (rows * depth)
-    own_at = first + lax.axis_index("z").astype(jnp.uint32) * rows
-    gathered = spread(residuals, ("h", "z")).reshape(items, width)
-    codebook = gather_codes(codebook).reshape(pieces, -1, width)
+    own_at = lax.axis_index("z").astype(jnp.uint32) * rows
+    gathered = spread(residuals, ("h", "z")).reshape(pieces, -1, width)
+    codebook = gather_codes(codebook, piece)
     codes_float = codebook.astype(jnp.float32)
     code_scale = lax.rsqrt(jnp.mean(codes_float * codes_float, axis=2) + EPSILON)
-    code_scale, piece, first, own_at = lax.optimization_barrier(
-        (code_scale, piece, first, own_at)
-    )
+    code_scale, own_at = lax.optimization_barrier((code_scale, own_at))
+    gathered = turned(gathered, piece, 0).reshape(items, width)
     rows_float = gathered.astype(jnp.float32)
     row_scale = lax.rsqrt(jnp.mean(rows_float * rows_float, axis=1) + EPSILON)
     row_scale = row_scale * (SHARPNESS / width)
@@ -66,31 +76,36 @@
         similarity = jnp.einsum("nd,...kd->...nk", gathered, codes, preferred_element_type=jnp.float32)
         return jnp.exp(similarity * row_scale[:, None] * scales[..., None, :])
 
-    kernel = kernel_of(codebook, code_scale).astype(jnp.bfloat16)
-    own_kernel = kernel_of(
-        lax.dynamic_index_in_dim(codebook, piece, keepdims=False),
-        lax.dynamic_index_in_dim(code_scale, piece, keepdims=False),
-    )
-    kernel, own_kernel = lax.optimization_barrier((kernel, own_kernel))
+    own_kernel = kernel_of(codebook[0], code_scale[0])
+    kernel = kernel_of(codebook[1:], code_scale[1:]).astype(jnp.bfloat16)
+    own_kernel, kernel = lax.optimization_barrier((own_kernel, kernel))
     balance = (items * groups) / (codes * depth)
     weights_rows = None
     for sweep in range(ITERS):
-        scaled = kernel.astype(jnp.float32)
+        own, rest = own_kernel, kernel.astype(jnp.float32)
         if weights_rows is not None:
-            scaled = scaled * weights_rows[None, :, None]
-        column_total = jnp.sum(spread(jnp.sum(scaled, axis=1), ITEM_AXES), axis=0)
+            own, rest = own * weights_rows[:, None], rest * weights_rows[None, :, None]
+        column_part = jnp.concatenate([jnp.sum(own, axis=0)[None], jnp.sum(rest, axis=1)])
+        column_total = jnp.sum(spread(column_part, ITEM_AXES), axis=0)
         weights_cols = balance / column_total
-        row_part = jnp.sum(
-            kernel.astype(jnp.float32) * weights_cols[:, None, :], axis=(0, 2)
+        row_part = jnp.sum(own_kernel * weights_cols[0][None, :], axis=1) + jnp.sum(
+            kernel.astype(jnp.float32) * weights_cols[1:][:, None, :], axis=(0, 2)
         )
         if sweep < ITERS - 1:
             row_total = jnp.sum(spread(row_part, "z"), axis=0)
             weights_rows = 1.0 / row_total
 
-    mine = lax.dynamic_slice_in_dim(kernel, first, rows * depth, axis=1)
-    shares = (mine.astype(jnp.float32) * weights_cols[:, None, :]).astype(jnp.bfloat16)
-    products = jnp.einsum(
-        "pnk,pkd->nd", shares, codebook, preferred_element_type=jnp.float32
+    size = rows * depth
+    own_kernel, kernel, weights_cols = lax.optimization_barrier((own_kernel, kernel, weights_cols))
+    mine = own_kernel[:size] * weights_cols[0][None, :]
+    rest = kernel[:, :size].astype(jnp.float32) * weights_cols[1:][:, None, :]
+    products = jnp.dot(
+        mine.astype(jnp.bfloat16), codebook[0], preferred_element_type=jnp.float32
+    ) + jnp.einsum(
+        "pnk,pkd->nd",
+        rest.astype(jnp.bfloat16),
+        codebook[1:],
+        preferred_element_type=jnp.float32,
     )
     products = products.astype(jnp.bfloat16).reshape(depth, rows, width)
     terms = jnp.concatenate([t.reshape(-1, width) for t in two_terms(row_part)])
@@ -98,8 +113,7 @@
     terms = jnp.pad(terms, ((0, -extra % 8), (0, 0)))
     terms = jnp.broadcast_to(terms[None], (depth,) + terms.shape)
     packed = jnp.concatenate([products, terms], axis=1)
-    weights_cols = lax.dynamic_index_in_dim(weights_cols, piece, keepdims=False)
-    packed, weights_cols = lax.optimization_barrier((packed, weights_cols))
+    packed, weights_cols = lax.optimization_barrier((packed, weights_cols[0]))
     packed = lax.all_to_all(packed, "z", 0, 0, tiled=True)
     total = jnp.sum(packed.astype(jnp.float32), axis=0)
     middle = rows + extra // 2

time: 138 us -> 138 us (level)
  waiting for transfers between devices: 15 us -> 18.1 us
  local copies, waits for them, and re-layouts: 4.43 us -> 2.55 us
  blocking collectives: 74.6 us -> 73.2 us
    ppermute x4 -> x3, waiting for transfers between devices: 0.01 us -> 2.54 us  [the longest x1 2.54 us: gather_codes(): other = lax.ppermute(block, 'x', [(0, 1), (1, 0), (2, 3), (3, 2)])]
    unnamed x16 -> x7, local copies, waits for them, and re-layouts: 1.74 us -> 0.02 us
    ppermute x4 -> x3, starting transfers between devices: 14 us -> 13.1 us  [the longest x1 5.19 us: gather_codes(): other = lax.ppermute(block, 'x', [(0, 3), (3, 0), (1, 2), (2, 1)])]
    reduce_sum x9 -> x15, other arithmetic: 2.91 us -> 3.2 us  [the longest x3 1.16 us: shards(): jnp.sum(kernel.astype(jnp.float32) * weights_cols[1:][:, None, :], axis=(...]
  transfers between devices with their start and end apart: 6 -> 5, of which waited for: 2 -> 3; matrix products, arithmetic and copies ran while one was open for 3% -> 2% of each run, Pallas kernels for 0% -> 0%
where the time goes in v7:
time: 138 us; the launch traced here: 137 us
  blocking collectives  73.2 us (53%)
  starting transfers between devices  32.2 us (23%)
  waiting for transfers between devices  18.1 us (13%)
  other arithmetic  6.95 us (5%)
  matrix products  3.32 us (2%)
  local copies, waits for them, and re-layouts  2.55 us (2%)
    all_to_all x5, blocking collectives, spread(): return lax.all_to_all(copies, axes, 0, 0, tiled=True)  51.3 us
    all_to_all x2, starting transfers between devices, spread(): return lax.all_to_all(copies, axes, 0, 0, tiled=True)  19.1 us
    all_to_all x2, waiting for transfers between devices, spread(): return lax.all_to_all(copies, axes, 0, 0, tiled=True)  15.6 us
    all_to_all x1, blocking collectives, shards(): packed = lax.all_to_all(packed, ITEM_AXES, 0, 0, tiled=True)  12 us
    all_to_all x1, blocking collectives, shards(): packed = lax.all_to_all(packed, 'z', 0, 0, tiled=True)  9.92 us
    ppermute x1, starting transfers between devices, gather_codes(): other = lax.ppermute(block, 'x', [(0, 3), (3, 0), (1, 2), (2, 1)])  5.19 us
    ppermute x1, starting transfers between devices, gather_codes(): other = lax.ppermute(block, 'c', [(0, 1), (1, 0)])  4 us
    ppermute x1, starting transfers between devices, gather_codes(): other = lax.ppermute(block, 'x', [(0, 1), (1, 0), (2, 3), (3, 2)])  3.94 us
  transfers between devices with their start and end apart: 5, of which 3 were waited for; matrix products, arithmetic and copies ran while one was open for 2% of the time, Pallas kernels for 0%

profile of v7, /device:TPU:1, one launch (start us, length us, event | category | flops | bytes accessed | tf_op | source)
XLA Modules:
  0.0 137.4 jit_solution(4213185029386653719)
XLA Ops:
  0.6 3.9 %collective-permute-start = (bf16[1,256,256]{2,1,0:T(8,128)(2,1)}, bf16[1,256,256]{2,1,0:T(8,128)(2,1)S(1)}, u32[]{:S(2)}, u32[]{:S(2)}) collective-permute-start(bf16[1,256,256]{2,1,0:T(8,128)(2,1)} %bitcast.67), channel_id=1, source_target_pairs={{0,16},{16,0},{32,48},{48,32},{1,17},{17,1},{33,49},{49,33},{2,18}... | collective-permute-start | bytes 393224 | tf_op jit(solution)/shard_map/ppermute | solution.py:44
  4.6 2.5 %collective-permute-done = bf16[1,256,256]{2,1,0:T(8,128)(2,1)S(1)} collective-permute-done((bf16[1,256,256]{2,1,0:T(8,128)(2,1)}, bf16[1,256,256]{2,1,0:T(8,128)(2,1)S(1)}, u32[]{:S(2)}, u32[]{:S(2)}) %collective-permute-start) | collective-permute-done | bytes 131104 | tf_op jit(solution)/shard_map/ppermute | solution.py:44
  7.1 0.9 broadcast_select_fusion.3
  8.1 5.2 %collective-permute-start.1 = (bf16[2,256,256]{2,1,0:T(8,128)(2,1)S(1)}, bf16[2,256,256]{2,1,0:T(8,128)(2,1)S(1)}, u32[]{:S(2)}, u32[]{:S(2)}) collective-permute-start(bf16[2,256,256]{2,1,0:T(8,128)(2,1)S(1)} %pad_maximum_fusion.7), channel_id=1, source_target_pairs={{0,48},{48,0},{16,32},{32,16},{1,49},{49,1},{17,33},{33,17},{2,50}... | collective-permute-start | bytes 786440 | tf_op jit(solution)/shard_map/ppermute | solution.py:46
  13.3 1.4 %broadcast_in_dim.24 = bf16[32,16,256]{2,1,0:T(8,128)(2,1)} broadcast(bf16[16,256]{1,0:T(8,128)(2,1)} %param.2), dimensions={1,2} | broadcast | bytes 270336 | tf_op jit(solution)/shard_map/broadcast_in_dim | solution.py:16
  14.7 15.7 %all-to-all-start = ((bf16[32,16,256]{2,1,0:T(8,128)(2,1)}), bf16[32,16,256]{2,1,0:T(8,128)(2,1)S(1)}, u32[]{:S(2)}, u32[]{:S(2)}) async-start(bf16[32,16,256]{2,1,0:T(8,128)(2,1)} %broadcast_in_dim.24), calls=%async_computation | async-start | bytes 524288 | tf_op jit(solution)/shard_map/all_to_all | solution.py:17
  30.5 4.0 %collective-permute-start.2 = (bf16[4,256,256]{2,1,0:T(8,128)(2,1)S(1)}, bf16[4,256,256]{2,1,0:T(8,128)(2,1)S(1)}, u32[]{:S(2)}, u32[]{:S(2)}) collective-permute-start(bf16[4,256,256]{2,1,0:T(8,128)(2,1)S(1)} %pad_maximum_fusion.2), channel_id=1, source_target_pairs={{0,1},{1,0},{2,3},{3,2},{4,5},{5,4},{6,7},{7,6},{8,9},{9,8},{10,11... | collective-permute-start | bytes 1572872 | tf_op jit(solution)/shard_map/ppermute | solution.py:48
  34.5 7.9 %all-to-all-done = bf16[32,16,256]{2,1,0:T(8,128)(2,1)S(1)} async-done(((bf16[32,16,256]{2,1,0:T(8,128)(2,1)}), bf16[32,16,256]{2,1,0:T(8,128)(2,1)S(1)}, u32[]{:S(2)}, u32[]{:S(2)}) %all-to-all-start) | async-done | bytes 262176 | tf_op jit(solution)/shard_map/all_to_all | solution.py:17
  43.4 0.7 fusion.5
  45.0 12.3 %all_to_all.47 = f32[16,4,512]{2,1,0:T(4,128)S(1)} all-to-all(f32[16,4,512]{2,1,0:T(4,128)S(1)} %broadcast_in_dim.27), channel_id=1, replica_groups=mesh['h'=4,'l'=2,'x'=4,'z'=8,'c'=2] {'x','c','l'}, dimensions={0} | all-to-all | bytes 262144 | tf_op jit(solution)/shard_map/all_to_all | solution.py:17
  57.9 9.1 %all_to_all.48 = f32[8,1,512]{2,1,0:T(1,128)S(1)} all-to-all(f32[8,1,512]{2,1,0:T(1,128)S(1)} %broadcast_in_dim.28), channel_id=1, replica_groups=mesh['h'=4,'l'=2,'x'=4,'z'=8,'c'=2] {'z'}, dimensions={0} | all-to-all | bytes 32768 | tf_op jit(solution)/shard_map/all_to_all | solution.py:17
  67.6 10.6 %all_to_all.49 = f32[16,4,512]{2,1,0:T(4,128)S(1)} all-to-all(f32[16,4,512]{2,1,0:T(4,128)S(1)} %broadcast_in_dim.30), channel_id=1, replica_groups=mesh['h'=4,'l'=2,'x'=4,'z'=8,'c'=2] {'x','c','l'}, dimensions={0} | all-to-all | bytes 262144 | tf_op jit(solution)/shard_map/all_to_all | solution.py:17
  78.9 9.0 %all_to_all.50 = f32[8,1,512]{2,1,0:T(1,128)S(1)} all-to-all(f32[8,1,512]{2,1,0:T(1,128)S(1)} %broadcast_in_dim.31), channel_id=1, replica_groups=mesh['h'=4,'l'=2,'x'=4,'z'=8,'c'=2] {'z'}, dimensions={0} | all-to-all | bytes 32768 | tf_op jit(solution)/shard_map/all_to_all | solution.py:17
  88.5 10.3 %all_to_all.51 = f32[16,4,512]{2,1,0:T(4,128)S(1)} all-to-all(f32[16,4,512]{2,1,0:T(4,128)S(1)} %broadcast_in_dim.33), channel_id=1, replica_groups=mesh['h'=4,'l'=2,'x'=4,'z'=8,'c'=2] {'x','c','l'}, dimensions={0} | all-to-all | bytes 262144 | tf_op jit(solution)/shard_map/all_to_all | solution.py:17
  99.1 0.4 fusion.4
  99.5 1.6 %convolution_bitcast_fusion = f32[128,256]{1,0:T(8,128)S(1)} fusion(f32[3,512]{1,0:T(4,128)S(1)} %slice.71, bf16[3,512,512]{1,2,0:T(8,128)(2,1)S(1)} %fusion.5, bf16[1,512,256]{2,1,0:T(8,128)(2,1)} %bitcast.60, bf16[1,512,256]{2,1,0:T(8,128)(2,1)} %bitcast.63, bf16[1,512,256]{2,1,0:T(8,128)(2,1)S(1)} %bitcast.57), kind=kOutput, calls=%fused_computation.19 | convolution fusion | flops 102039552 | bytes 1318912 | tf_op jit(solution)/shard_map/pnk,pkd->nd/dot_general | solution.py:104
  101.3 9.9 %all_to_all.52 = bf16[8,24,256]{2,1,0:T(8,128)(2,1)S(1)} all-to-all(bf16[8,24,256]{2,1,0:T(8,128)(2,1)S(1)} %pad_maximum_fusion.8), channel_id=1, replica_groups=mesh['h'=4,'l'=2,'x'=4,'z'=8,'c'=2] {'z'}, dimensions={0} | all-to-all | bytes 196608 | tf_op jit(solution)/shard_map/all_to_all | solution.py:117
  111.3 0.5 convolution_convert_fusion
  112.1 12.0 %all_to_all.53 = bf16[16,40,256]{2,1,0:T(8,128)(2,1)S(1)} all-to-all(bf16[16,40,256]{2,1,0:T(8,128)(2,1)S(1)} %pad_maximum_fusion.3), channel_id=1, replica_groups=mesh['h'=4,'l'=2,'x'=4,'z'=8,'c'=2] {'x','c','l'}, dimensions={0} | all-to-all | bytes 655360 | tf_op jit(solution)/shard_map/all_to_all | solution.py:133
  124.3 0.7 broadcast_in_dim.35
  124.9 3.4 %all-to-all-start.8 = ((f16[8,32,256]{2,1,0:T(8,128)(2,1)}), f16[8,32,256]{2,1,0:T(8,128)(2,1)S(1)}, u32[]{:S(2)}, u32[]{:S(2)}) async-start(f16[8,32,256]{2,1,0:T(8,128)(2,1)} %broadcast_in_dim.35), calls=%async_computation.8 | async-start | bytes 262144 | tf_op jit(solution)/shard_map/all_to_all | solution.py:17
  128.4 0.7 fusion.19
  129.1 7.6 %all-to-all-done.8 = f16[8,32,256]{2,1,0:T(8,128)(2,1)S(1)} async-done(((f16[8,32,256]{2,1,0:T(8,128)(2,1)}), f16[8,32,256]{2,1,0:T(8,128)(2,1)S(1)}, u32[]{:S(2)}, u32[]{:S(2)}) %all-to-all-start.8) | async-done | bytes 131104 | tf_op jit(solution)/shard_map/all_to_all | solution.py:17
  136.7 0.7 bitcast_convert_fusion
  (80 shorter events, 5.2 us)
Async XLA Ops:
  0.6 6.5 %collective-permute-start = (bf16[1,256,256]{2,1,0:T(8,128)(2,1)}, bf16[1,256,256]{2,1,0:T(8,128)(2,1)S(1)}, u32[]{:S(2)}, u32[]{:S(2)}) collective-permute-start(bf16[1,256,256]{2,1,0:T(8,128)(2,1)} %bitcast.67), channel_id=1, source_target_pairs={{0,16},{16,0},{32,48},{48,32},{1,17},{17,1},{33,49},{49,33},{2,18}... | collective-permute-start | bytes 393224 | tf_op jit(solution)/shard_map/ppermute | solution.py:44
  8.1 22.3 %collective-permute-start.1 = (bf16[2,256,256]{2,1,0:T(8,128)(2,1)S(1)}, bf16[2,256,256]{2,1,0:T(8,128)(2,1)S(1)}, u32[]{:S(2)}, u32[]{:S(2)}) collective-permute-start(bf16[2,256,256]{2,1,0:T(8,128)(2,1)S(1)} %pad_maximum_fusion.7), channel_id=1, source_target_pairs={{0,48},{48,0},{16,32},{32,16},{1,49},{49,1},{17,33},{33,17},{2,50}... | collective-permute-start | bytes 786440 | tf_op jit(solution)/shard_map/ppermute | solution.py:46
  14.7 27.8 %all-to-all-start = ((bf16[32,16,256]{2,1,0:T(8,128)(2,1)}), bf16[32,16,256]{2,1,0:T(8,128)(2,1)S(1)}, u32[]{:S(2)}, u32[]{:S(2)}) async-start(bf16[32,16,256]{2,1,0:T(8,128)(2,1)} %broadcast_in_dim.24), calls=%async_computation | async-start | bytes 524288 | tf_op jit(solution)/shard_map/all_to_all | solution.py:17
  30.5 12.2 %collective-permute-start.2 = (bf16[4,256,256]{2,1,0:T(8,128)(2,1)S(1)}, bf16[4,256,256]{2,1,0:T(8,128)(2,1)S(1)}, u32[]{:S(2)}, u32[]{:S(2)}) collective-permute-start(bf16[4,256,256]{2,1,0:T(8,128)(2,1)S(1)} %pad_maximum_fusion.2), channel_id=1, source_target_pairs={{0,1},{1,0},{2,3},{3,2},{4,5},{5,4},{6,7},{7,6},{8,9},{9,8},{10,11... | collective-permute-start | bytes 1572872 | tf_op jit(solution)/shard_map/ppermute | solution.py:48
  43.0 1.2 copy-start
  43.0 1.2 copy-start.1
  111.8 16.6 %copy-start.2 = (bf16[16,256]{1,0:T(8,128)(2,1)S(1)}, bf16[16,256]{1,0:T(8,128)(2,1)}, u32[]{:S(2)}) copy-start(bf16[16,256]{1,0:T(8,128)(2,1)} %param.2) | copy-start | bytes 24580
  124.9 11.8 %all-to-all-start.8 = ((f16[8,32,256]{2,1,0:T(8,128)(2,1)}), f16[8,32,256]{2,1,0:T(8,128)(2,1)S(1)}, u32[]{:S(2)}, u32[]{:S(2)}) async-start(f16[8,32,256]{2,1,0:T(8,128)(2,1)} %broadcast_in_dim.35), calls=%async_computation.8 | async-start | bytes 262144 | tf_op jit(solution)/shard_map/all_to_all | solution.py:17

commit v8 on v7

--- a/solution.py
+++ b/solution.py
@@ -32,23 +32,38 @@
     )
 
 
-def ordered(first, mine, other):
-    return jnp.concatenate([jnp.where(first, mine, other), jnp.where(first, other, mine)])
-
-
 def gather_codes(codebook, piece):
     width = codebook.shape[1]
     pieces = lax.axis_size("h")
-    place = lax.axis_index("x")
-    block = codebook[None]
-    other = lax.ppermute(block, "x", [(0, 1), (1, 0), (2, 3), (3, 2)])
-    block = ordered(place % 2 == 0, block, other)
-    other = lax.ppermute(block, "x", [(0, 3), (3, 0), (1, 2), (2, 1)])
-    block = ordered(place < 2, block, other)
+    across = lax.axis_size("x")
+    place, core = lax.axis_index("x"), lax.axis_index("c")
+    pairs = ([1, 0, 3, 2], [3, 2, 1, 0])
+
+    def swap(block, turn):
+        return lax.ppermute(
+            block,
+            ("x", "c"),
+            [(x * 2 + c, pairs[turn ^ c][x] * 2 + c) for x in range(across) for c in range(2)],
+        )
+
+    other = swap(codebook, 0)
+    block = jnp.stack([codebook, other])
+    other = swap(block, 1)
+    block = jnp.concatenate([block, other])
+    near, far = place ^ 1, across - 1 - place
+    held = [
+        jnp.where(
+            x == place,
+            0,
+            jnp.where(x == near, 1 + core, jnp.where(x == far, 2 - core, 3)),
+        )
+        for x in range(across)
+    ]
+    block = jnp.stack([lax.dynamic_index_in_dim(block, at, keepdims=False) for at in held])
     other = lax.ppermute(block, "c", [(0, 1), (1, 0)])
-    zero = lax.axis_index("c") == 0
+    zero = core == 0
     both = jnp.stack([jnp.where(zero, block, other), jnp.where(zero, other, block)], axis=1)
-    both = both.reshape(block.shape[0] * 2, pieces, -1, width)
+    both = both.reshape(across * 2, pieces, -1, width)
     return turned(both, piece, 1).reshape(pieces, -1, width)
 
 
@@ -86,7 +101,9 @@
         if weights_rows is not None:
             own, rest = own * weights_rows[:, None], rest * weights_rows[None, :, None]
         column_part = jnp.concatenate([jnp.sum(own, axis=0)[None], jnp.sum(rest, axis=1)])
-        column_total = jnp.sum(spread(column_part, ITEM_AXES), axis=0)
+        column_part = lax.optimization_barrier(column_part)
+        column_parts = spread(column_part.astype(jnp.bfloat16), ITEM_AXES)
+        column_total = jnp.sum(column_parts.astype(jnp.float32), axis=0)
         weights_cols = balance / column_total
         row_part = jnp.sum(own_kernel * weights_cols[0][None, :], axis=1) + jnp.sum(
             kernel.astype(jnp.float32) * weights_cols[1:][:, None, :], axis=(0, 2)
@@ -97,16 +114,13 @@
 
     size = rows * depth
     own_kernel, kernel, weights_cols = lax.optimization_barrier((own_kernel, kernel, weights_cols))
-    mine = own_kernel[:size] * weights_cols[0][None, :]
-    rest = kernel[:, :size].astype(jnp.float32) * weights_cols[1:][:, None, :]
-    products = jnp.dot(
-        mine.astype(jnp.bfloat16), codebook[0], preferred_element_type=jnp.float32
-    ) + jnp.einsum(
-        "pnk,pkd->nd",
-        rest.astype(jnp.bfloat16),
-        codebook[1:],
-        preferred_element_type=jnp.float32,
-    )
+    products = 0.0
+    for part in range(pieces):
+        mine = own_kernel[:size] if part == 0 else kernel[part - 1, :size]
+        mine = mine.astype(jnp.float32) * weights_cols[part][None, :]
+        products = products + jnp.dot(
+            mine.astype(jnp.bfloat16), codebook[part], preferred_element_type=jnp.float32
+        )
     products = products.astype(jnp.bfloat16).reshape(depth, rows, width)
     terms = jnp.concatenate([t.reshape(-1, width) for t in two_terms(row_part)])
     extra = terms.shape[0]

time: 138 us -> 138 us (level)
  waiting for transfers between devices: 18.1 us -> 15.1 us
    all_to_all x2, waiting for transfers between devices: 15.6 us -> 12.5 us  [spread(): return lax.all_to_all(copies, axes, 0, 0, tiled=True)]
    ppermute x2, starting transfers between devices: 9.13 us -> 7.3 us  [swap(): lax.ppermute(block, ('x', 'c'), [(x * 2 + c, pairs[turn ^ c][x] * 2 + c)...]
where the time goes in v8:
time: 138 us; the launch traced here: 137 us
  blocking collectives  74.4 us (54%)
  starting transfers between devices  32.1 us (23%)
  waiting for transfers between devices  15.1 us (11%)
  other arithmetic  7.88 us (6%)
  matrix products  3.7 us (3%)
  local copies, waits for them, and re-layouts  2.59 us (2%)
    all_to_all x5, blocking collectives, spread(): return lax.all_to_all(copies, axes, 0, 0, tiled=True)  52.6 us
    all_to_all x2, starting transfers between devices, spread(): return lax.all_to_all(copies, axes, 0, 0, tiled=True)  19.6 us
    all_to_all x2, waiting for transfers between devices, spread(): return lax.all_to_all(copies, axes, 0, 0, tiled=True)  12.5 us
    all_to_all x1, blocking collectives, shards(): packed = lax.all_to_all(packed, ITEM_AXES, 0, 0, tiled=True)  11.9 us
    all_to_all x1, blocking collectives, shards(): packed = lax.all_to_all(packed, 'z', 0, 0, tiled=True)  9.92 us
    ppermute x2, starting transfers between devices, swap(): lax.ppermute(block, ('x', 'c'), [(x * 2 + c, pairs[turn ^ c][x] * 2 + c)...  7.3 us
    ppermute x1, starting transfers between devices, gather_codes(): other = lax.ppermute(block, 'c', [(0, 1), (1, 0)])  5.27 us
  transfers between devices with their start and end apart: 5, of which 3 were waited for; matrix products, arithmetic and copies ran while one was open for 2% of the time, Pallas kernels for 0%

profile of v8, /device:TPU:1, one launch (start us, length us, event | category | flops | bytes accessed | tf_op | source)
XLA Modules:
  0.0 137.0 jit_solution(9796706063717411992)
XLA Ops:
  0.6 5.2 %collective-permute-start = (bf16[256,256]{1,0:T(8,128)(2,1)}, bf16[256,256]{1,0:T(8,128)(2,1)S(1)}, u32[]{:S(2)}, u32[]{:S(2)}) collective-permute-start(bf16[256,256]{1,0:T(8,128)(2,1)} %param.3), channel_id=1, source_target_pairs={{0,16},{1,49},{16,0},{17,33},{32,48},{33,17},{48,32},{49,1},{2,18}... | collective-permute-start | bytes 393224 | tf_op jit(solution)/shard_map/ppermute | solution.py:43
  5.8 2.6 %collective-permute-done = bf16[256,256]{1,0:T(8,128)(2,1)S(1)} collective-permute-done((bf16[256,256]{1,0:T(8,128)(2,1)}, bf16[256,256]{1,0:T(8,128)(2,1)S(1)}, u32[]{:S(2)}, u32[]{:S(2)}) %collective-permute-start) | collective-permute-done | bytes 131104 | tf_op jit(solution)/shard_map/ppermute | solution.py:43
  8.4 0.9 pad_maximum_fusion.5
  9.3 2.1 %collective-permute-start.1 = (bf16[2,256,256]{2,1,0:T(8,128)(2,1)S(1)}, bf16[2,256,256]{2,1,0:T(8,128)(2,1)S(1)}, u32[]{:S(2)}, u32[]{:S(2)}) collective-permute-start(bf16[2,256,256]{2,1,0:T(8,128)(2,1)S(1)} %pad_maximum_fusion.5), channel_id=1, source_target_pairs={{0,48},{1,17},{16,32},{17,1},{32,16},{33,49},{48,0},{49,33},{2,50}... | collective-permute-start | bytes 786440 | tf_op jit(solution)/shard_map/ppermute | solution.py:43
  11.4 1.4 %broadcast_in_dim.22 = bf16[32,16,256]{2,1,0:T(8,128)(2,1)} broadcast(bf16[16,256]{1,0:T(8,128)(2,1)} %param.2), dimensions={1,2} | broadcast | bytes 270336 | tf_op jit(solution)/shard_map/broadcast_in_dim | solution.py:16
  12.9 16.0 %all-to-all-start = ((bf16[32,16,256]{2,1,0:T(8,128)(2,1)}), bf16[32,16,256]{2,1,0:T(8,128)(2,1)S(1)}, u32[]{:S(2)}, u32[]{:S(2)}) async-start(bf16[32,16,256]{2,1,0:T(8,128)(2,1)} %broadcast_in_dim.22), calls=%async_computation | async-start | bytes 524288 | tf_op jit(solution)/shard_map/all_to_all | solution.py:17
  28.9 1.0 pad_maximum_fusion.1
  30.0 5.3 %collective-permute-start.2 = (bf16[4,256,256]{2,1,0:T(8,128)(2,1)S(1)}, bf16[4,256,256]{2,1,0:T(8,128)(2,1)S(1)}, u32[]{:S(2)}, u32[]{:S(2)}) collective-permute-start(bf16[4,256,256]{2,1,0:T(8,128)(2,1)S(1)} %pad_maximum_fusion.2), channel_id=1, source_target_pairs={{0,1},{1,0},{2,3},{3,2},{4,5},{5,4},{6,7},{7,6},{8,9},{9,8},{10,11... | collective-permute-start | bytes 1572872 | tf_op jit(solution)/shard_map/ppermute | solution.py:63
  35.3 5.4 %all-to-all-done = bf16[32,16,256]{2,1,0:T(8,128)(2,1)S(1)} async-done(((bf16[32,16,256]{2,1,0:T(8,128)(2,1)}), bf16[32,16,256]{2,1,0:T(8,128)(2,1)S(1)}, u32[]{:S(2)}, u32[]{:S(2)}) %all-to-all-start) | async-done | bytes 262176 | tf_op jit(solution)/shard_map/all_to_all | solution.py:17
  41.7 0.7 fusion.5
  43.2 13.9 %all_to_all.47 = bf16[16,4,512]{2,1,0:T(4,128)(2,1)S(1)} all-to-all(bf16[16,4,512]{2,1,0:T(4,128)(2,1)S(1)} %broadcast_in_dim.24), channel_id=1, replica_groups=mesh['h'=4,'l'=2,'x'=4,'z'=8,'c'=2] {'x','c','l'}, dimensions={0} | all-to-all | bytes 131072 | tf_op jit(solution)/shard_map/all_to_all | solution.py:17
  57.8 9.5 %all_to_all.48 = f32[8,1,512]{2,1,0:T(1,128)S(1)} all-to-all(f32[8,1,512]{2,1,0:T(1,128)S(1)} %broadcast_in_dim.25), channel_id=1, replica_groups=mesh['h'=4,'l'=2,'x'=4,'z'=8,'c'=2] {'z'}, dimensions={0} | all-to-all | bytes 32768 | tf_op jit(solution)/shard_map/all_to_all | solution.py:17
  67.9 10.2 %all_to_all.49 = bf16[16,4,512]{2,1,0:T(4,128)(2,1)S(1)} all-to-all(bf16[16,4,512]{2,1,0:T(4,128)(2,1)S(1)} %broadcast_in_dim.27), channel_id=1, replica_groups=mesh['h'=4,'l'=2,'x'=4,'z'=8,'c'=2] {'x','c','l'}, dimensions={0} | all-to-all | bytes 131072 | tf_op jit(solution)/shard_map/all_to_all | solution.py:17
  78.8 9.0 %all_to_all.50 = f32[8,1,512]{2,1,0:T(1,128)S(1)} all-to-all(f32[8,1,512]{2,1,0:T(1,128)S(1)} %broadcast_in_dim.28), channel_id=1, replica_groups=mesh['h'=4,'l'=2,'x'=4,'z'=8,'c'=2] {'z'}, dimensions={0} | all-to-all | bytes 32768 | tf_op jit(solution)/shard_map/all_to_all | solution.py:17
  88.4 9.9 %all_to_all.51 = bf16[16,4,512]{2,1,0:T(4,128)(2,1)S(1)} all-to-all(bf16[16,4,512]{2,1,0:T(4,128)(2,1)S(1)} %broadcast_in_dim.30), channel_id=1, replica_groups=mesh['h'=4,'l'=2,'x'=4,'z'=8,'c'=2] {'x','c','l'}, dimensions={0} | all-to-all | bytes 131072 | tf_op jit(solution)/shard_map/all_to_all | solution.py:17
  99.2 1.3 convolution_add_fusion.2
  101.2 9.9 %all_to_all.52 = bf16[8,24,256]{2,1,0:T(8,128)(2,1)S(1)} all-to-all(bf16[8,24,256]{2,1,0:T(8,128)(2,1)S(1)} %pad_maximum_fusion.6), channel_id=1, replica_groups=mesh['h'=4,'l'=2,'x'=4,'z'=8,'c'=2] {'z'}, dimensions={0} | all-to-all | bytes 196608 | tf_op jit(solution)/shard_map/all_to_all | solution.py:131
  111.2 0.5 convolution_convert_fusion
  112.1 11.9 %all_to_all.53 = bf16[16,40,256]{2,1,0:T(8,128)(2,1)S(1)} all-to-all(bf16[16,40,256]{2,1,0:T(8,128)(2,1)S(1)} %pad_maximum_fusion.3), channel_id=1, replica_groups=mesh['h'=4,'l'=2,'x'=4,'z'=8,'c'=2] {'x','c','l'}, dimensions={0} | all-to-all | bytes 655360 | tf_op jit(solution)/shard_map/all_to_all | solution.py:147
  124.1 0.7 broadcast_in_dim.32
  124.8 3.6 %all-to-all-start.8 = ((f16[8,32,256]{2,1,0:T(8,128)(2,1)}), f16[8,32,256]{2,1,0:T(8,128)(2,1)S(1)}, u32[]{:S(2)}, u32[]{:S(2)}) async-start(f16[8,32,256]{2,1,0:T(8,128)(2,1)} %broadcast_in_dim.32), calls=%async_computation.8 | async-start | bytes 262144 | tf_op jit(solution)/shard_map/all_to_all | solution.py:17
  128.5 0.7 fusion.35
  129.1 7.1 %all-to-all-done.8 = f16[8,32,256]{2,1,0:T(8,128)(2,1)S(1)} async-done(((f16[8,32,256]{2,1,0:T(8,128)(2,1)}), f16[8,32,256]{2,1,0:T(8,128)(2,1)S(1)}, u32[]{:S(2)}, u32[]{:S(2)}) %all-to-all-start.8) | async-done | bytes 131104 | tf_op jit(solution)/shard_map/all_to_all | solution.py:17
  136.2 0.7 bitcast_convert_fusion
  (83 shorter events, 6.3 us)
Async XLA Ops:
  0.6 7.8 %collective-permute-start = (bf16[256,256]{1,0:T(8,128)(2,1)}, bf16[256,256]{1,0:T(8,128)(2,1)S(1)}, u32[]{:S(2)}, u32[]{:S(2)}) collective-permute-start(bf16[256,256]{1,0:T(8,128)(2,1)} %param.3), channel_id=1, source_target_pairs={{0,16},{1,49},{16,0},{17,33},{32,48},{33,17},{48,32},{49,1},{2,18}... | collective-permute-start | bytes 393224 | tf_op jit(solution)/shard_map/ppermute | solution.py:43
  9.3 19.6 %collective-permute-start.1 = (bf16[2,256,256]{2,1,0:T(8,128)(2,1)S(1)}, bf16[2,256,256]{2,1,0:T(8,128)(2,1)S(1)}, u32[]{:S(2)}, u32[]{:S(2)}) collective-permute-start(bf16[2,256,256]{2,1,0:T(8,128)(2,1)S(1)} %pad_maximum_fusion.5), channel_id=1, source_target_pairs={{0,48},{1,17},{16,32},{17,1},{32,16},{33,49},{48,0},{49,33},{2,50}... | collective-permute-start | bytes 786440 | tf_op jit(solution)/shard_map/ppermute | solution.py:43
  12.9 27.9 %all-to-all-start = ((bf16[32,16,256]{2,1,0:T(8,128)(2,1)}), bf16[32,16,256]{2,1,0:T(8,128)(2,1)S(1)}, u32[]{:S(2)}, u32[]{:S(2)}) async-start(bf16[32,16,256]{2,1,0:T(8,128)(2,1)} %broadcast_in_dim.22), calls=%async_computation | async-start | bytes 524288 | tf_op jit(solution)/shard_map/all_to_all | solution.py:17
  30.0 10.9 %collective-permute-start.2 = (bf16[4,256,256]{2,1,0:T(8,128)(2,1)S(1)}, bf16[4,256,256]{2,1,0:T(8,128)(2,1)S(1)}, u32[]{:S(2)}, u32[]{:S(2)}) collective-permute-start(bf16[4,256,256]{2,1,0:T(8,128)(2,1)S(1)} %pad_maximum_fusion.2), channel_id=1, source_target_pairs={{0,1},{1,0},{2,3},{3,2},{4,5},{5,4},{6,7},{7,6},{8,9},{9,8},{10,11... | collective-permute-start | bytes 1572872 | tf_op jit(solution)/shard_map/ppermute | solution.py:63
  40.9 1.5 %copy-start.1 = (bf16[4,128,256]{2,1,0:T(8,128)(2,1)}, bf16[4,128,256]{2,1,0:T(8,128)(2,1)S(1)}, u32[]{:S(2)}) copy-start(bf16[4,128,256]{2,1,0:T(8,128)(2,1)S(1)} %get-tuple-element.23) | copy-start | bytes 786436
  41.3 1.2 copy-start
  99.0 12.2 %copy-start.2 = (bf16[4,128,256]{2,1,0:T(8,128)(2,1)S(1)}, bf16[4,128,256]{2,1,0:T(8,128)(2,1)}, u32[]{:S(2)}) copy-start(bf16[4,128,256]{2,1,0:T(8,128)(2,1)} %copy-done.1) | copy-start | bytes 786436
  111.7 16.8 %copy-start.3 = (bf16[16,256]{1,0:T(8,128)(2,1)S(1)}, bf16[16,256]{1,0:T(8,128)(2,1)}, u32[]{:S(2)}) copy-start(bf16[16,256]{1,0:T(8,128)(2,1)} %param.2) | copy-start | bytes 24580
  124.8 11.4 %all-to-all-start.8 = ((f16[8,32,256]{2,1,0:T(8,128)(2,1)}), f16[8,32,256]{2,1,0:T(8,128)(2,1)S(1)}, u32[]{:S(2)}, u32[]{:S(2)}) async-start(f16[8,32,256]{2,1,0:T(8,128)(2,1)} %broadcast_in_dim.32), calls=%async_computation.8 | async-start | bytes 262144 | tf_op jit(solution)/shard_map/all_to_all | solution.py:17

commit v9 on v8

--- a/solution.py
+++ b/solution.py
@@ -1,6 +1,8 @@
 import jax
 import jax.numpy as jnp
 from jax import lax
+from jax.experimental import pallas as pl
+from jax.experimental.pallas import tpu as pltpu
 from jax.sharding import Mesh, PartitionSpec as P
 
 ITERS = 3
@@ -15,6 +17,42 @@
     members = lax.axis_size(axes)
     copies = jnp.broadcast_to(block[None], (members,) + block.shape)
     return lax.all_to_all(copies, axes, 0, 0, tiled=True)
+
+
+def prepare_kernel(rows_ref, codes_ref, copies_ref, held_ref, block, sems, codes_sem):
+    keep = pltpu.make_async_copy(codes_ref, held_ref, codes_sem)
+    keep.start()
+    members = copies_ref.shape[0]
+    read = pltpu.make_async_copy(rows_ref, block, sems.at[members])
+    read.start()
+    read.wait()
+    writes = [
+        pltpu.make_async_copy(block, copies_ref.at[member], sems.at[member])
+        for member in range(members)
+    ]
+    for write in writes:
+        write.start()
+    for write in writes:
+        write.wait()
+    keep.wait()
+
+
+def prepare(residuals, codebook, members):
+    return pl.pallas_call(
+        prepare_kernel,
+        out_shape=(
+            jax.ShapeDtypeStruct((members,) + residuals.shape, residuals.dtype),
+            jax.ShapeDtypeStruct(codebook.shape, codebook.dtype),
+        ),
+        in_specs=[pl.BlockSpec(memory_space=pl.ANY)] * 2,
+        out_specs=(pl.BlockSpec(memory_space=pl.ANY), pl.BlockSpec(memory_space=pltpu.VMEM)),
+        scratch_shapes=[
+            pltpu.VMEM(residuals.shape, residuals.dtype),
+            pltpu.SemaphoreType.DMA((members + 1,)),
+            pltpu.SemaphoreType.DMA,
+        ],
+        compiler_params=pltpu.CompilerParams(vmem_limit_bytes=2**21),
+    )(residuals, codebook)
 
 
 def two_terms(values):
@@ -32,7 +70,7 @@
     )
 
 
-def gather_codes(codebook, piece):
+def gather_codes(codebook, held, piece):
     width = codebook.shape[1]
     pieces = lax.axis_size("h")
     across = lax.axis_size("x")
@@ -47,11 +85,11 @@
         )
 
     other = swap(codebook, 0)
-    block = jnp.stack([codebook, other])
+    block = jnp.stack([held, other])
     other = swap(block, 1)
     block = jnp.concatenate([block, other])
     near, far = place ^ 1, across - 1 - place
-    held = [
+    places = [
         jnp.where(
             x == place,
             0,
@@ -59,7 +97,7 @@
         )
         for x in range(across)
     ]
-    block = jnp.stack([lax.dynamic_index_in_dim(block, at, keepdims=False) for at in held])
+    block = jnp.stack([lax.dynamic_index_in_dim(block, at, keepdims=False) for at in places])
     other = lax.ppermute(block, "c", [(0, 1), (1, 0)])
     zero = core == 0
     both = jnp.stack([jnp.where(zero, block, other), jnp.where(zero, other, block)], axis=1)
@@ -77,50 +115,50 @@
     codes = codebook.shape[0] * lax.axis_size(("x", "c"))
     piece = lax.axis_index("h").astype(jnp.uint32)
     own_at = lax.axis_index("z").astype(jnp.uint32) * rows
-    gathered = spread(residuals, ("h", "z")).reshape(pieces, -1, width)
-    codebook = gather_codes(codebook, piece)
+    copies, held = prepare(residuals, codebook, pieces * depth)
+    gathered = lax.all_to_all(copies, ("h", "z"), 0, 0, tiled=True)
+    gathered = gathered.reshape(pieces, -1, width)
+    codebook = gather_codes(codebook, held, piece)
     codes_float = codebook.astype(jnp.float32)
     code_scale = lax.rsqrt(jnp.mean(codes_float * codes_float, axis=2) + EPSILON)
-    code_scale, own_at = lax.optimization_barrier((code_scale, own_at))
+    code_scale, own_scale, own_at = lax.optimization_barrier(
+        (code_scale, code_scale[0], own_at)
+    )
     gathered = turned(gathered, piece, 0).reshape(items, width)
     rows_float = gathered.astype(jnp.float32)
     row_scale = lax.rsqrt(jnp.mean(rows_float * rows_float, axis=1) + EPSILON)
     row_scale = row_scale * (SHARPNESS / width)
 
-    def kernel_of(codes, scales):
-        similarity = jnp.einsum("nd,...kd->...nk", gathered, codes, preferred_element_type=jnp.float32)
+    def kernel_of(gathered, codes, scales):
+        similarity = jnp.einsum(
+            "nd,...kd->...nk", gathered, codes, preferred_element_type=jnp.float32
+        )
         return jnp.exp(similarity * row_scale[:, None] * scales[..., None, :])
 
-    own_kernel = kernel_of(codebook[0], code_scale[0])
-    kernel = kernel_of(codebook[1:], code_scale[1:]).astype(jnp.bfloat16)
-    own_kernel, kernel = lax.optimization_barrier((own_kernel, kernel))
+    kernel = kernel_of(gathered, codebook, code_scale).astype(jnp.bfloat16)
+    kernel = lax.optimization_barrier(kernel)
     balance = (items * groups) / (codes * depth)
     weights_rows = None
     for sweep in range(ITERS):
-        own, rest = own_kernel, kernel.astype(jnp.float32)
+        scaled = kernel.astype(jnp.float32)
         if weights_rows is not None:
-            own, rest = own * weights_rows[:, None], rest * weights_rows[None, :, None]
-        column_part = jnp.concatenate([jnp.sum(own, axis=0)[None], jnp.sum(rest, axis=1)])
-        column_part = lax.optimization_barrier(column_part)
+            scaled = scaled * weights_rows[None, :, None]
+        column_part = lax.optimization_barrier(jnp.sum(scaled, axis=1))
         column_parts = spread(column_part.astype(jnp.bfloat16), ITEM_AXES)
         column_total = jnp.sum(column_parts.astype(jnp.float32), axis=0)
         weights_cols = balance / column_total
-        row_part = jnp.sum(own_kernel * weights_cols[0][None, :], axis=1) + jnp.sum(
-            kernel.astype(jnp.float32) * weights_cols[1:][:, None, :], axis=(0, 2)
+        row_part = jnp.sum(
+            kernel.astype(jnp.float32) * weights_cols[:, None, :], axis=(0, 2)
         )
         if sweep < ITERS - 1:
             row_total = jnp.sum(spread(row_part, "z"), axis=0)
             weights_rows = 1.0 / row_total
 
     size = rows * depth
-    own_kernel, kernel, weights_cols = lax.optimization_barrier((own_kernel, kernel, weights_cols))
-    products = 0.0
-    for part in range(pieces):
-        mine = own_kernel[:size] if part == 0 else kernel[part - 1, :size]
-        mine = mine.astype(jnp.float32) * weights_cols[part][None, :]
-        products = products + jnp.dot(
-            mine.astype(jnp.bfloat16), codebook[part], preferred_element_type=jnp.float32
-        )
+    mine = kernel[:, :size].astype(jnp.float32) * weights_cols[:, None, :]
+    products = jnp.einsum(
+        "pnk,pkd->nd", mine.astype(jnp.bfloat16), codebook, preferred_element_type=jnp.float32
+    )
     products = products.astype(jnp.bfloat16).reshape(depth, rows, width)
     terms = jnp.concatenate([t.reshape(-1, width) for t in two_terms(row_part)])
     extra = terms.shape[0]
@@ -134,6 +172,8 @@
     row_total = total[rows:middle] + total[middle : rows + extra]
     weights_rows = 1.0 / row_total.reshape(items)
 
+    again, weights_rows = lax.optimization_barrier((gathered, weights_rows))
+    own_kernel = kernel_of(again, codebook[0], own_scale)
     transport = (own_kernel * weights_rows[:, None] * weights_cols[None, :]).astype(jnp.bfloat16)
     numerator = lax.dot_general(
         transport, gathered, (((0,), (0,)), ((), ())), preferred_element_type=jnp.float32

time: 138 us -> 134 us (0.971)
  other arithmetic: 7.88 us -> 5.54 us
  waiting for transfers between devices: 15.1 us -> 13.4 us
    all_to_all x2 -> x1, starting transfers between devices: 19.6 us -> 3.57 us  [spread(): return lax.all_to_all(copies, axes, 0, 0, tiled=True)]
    all_to_all x0 -> x1, starting transfers between devices: none -> 15.9 us  [shards(): gathered = lax.all_to_all(copies, ('h', 'z'), 0, 0, tiled=True)]
    all_to_all x0 -> x1, waiting for transfers between devices: none -> 6.32 us  [shards(): gathered = lax.all_to_all(copies, ('h', 'z'), 0, 0, tiled=True)]
    all_to_all x2 -> x1, waiting for transfers between devices: 12.5 us -> 7.1 us  [spread(): return lax.all_to_all(copies, axes, 0, 0, tiled=True)]
    ppermute x2, waiting for transfers between devices: 2.56 us -> 0.01 us  [swap(): lax.ppermute(block, ('x', 'c'), [(x * 2 + c, pairs[turn ^ c][x] * 2 + c)...]
    unnamed x9, local copies, waits for them, and re-layouts: 0.02 us -> 1.62 us
    dot_general x4 -> x1, matrix products: 2.13 us -> 0.64 us  [shards(): jnp.einsum('pnk,pkd->nd', mine.astype(jnp.bfloat16), codebook, preferred_...]
    broadcast_in_dim x7 -> x6, local copies, waits for them, and re-layouts: 2.18 us -> 0.76 us  [spread(): copies = jnp.broadcast_to(block[None], (members,) + block.shape)]
  transfers between devices with their start and end apart: 5 -> 5, of which waited for: 3 -> 2; matrix products, arithmetic and copies ran while one was open for 2% -> 1% of each run, Pallas kernels for 0% -> 1%
where the time goes in v9:
time: 134 us; the launch traced here: 133 us
  blocking collectives  74.4 us (56%)
  starting transfers between devices  31.9 us (24%)
  waiting for transfers between devices  13.4 us (10%)
  other arithmetic  5.54 us (4%)
  local copies, waits for them, and re-layouts  2.82 us (2%)
  matrix products  2.61 us (2%)
    all_to_all x5, blocking collectives, spread(): return lax.all_to_all(copies, axes, 0, 0, tiled=True)  52.6 us
    all_to_all x1, starting transfers between devices, shards(): gathered = lax.all_to_all(copies, ('h', 'z'), 0, 0, tiled=True)  15.9 us
    all_to_all x1, blocking collectives, shards(): packed = lax.all_to_all(packed, ITEM_AXES, 0, 0, tiled=True)  11.9 us
    all_to_all x1, blocking collectives, shards(): packed = lax.all_to_all(packed, 'z', 0, 0, tiled=True)  9.91 us
    ppermute x2, starting transfers between devices, swap(): lax.ppermute(block, ('x', 'c'), [(x * 2 + c, pairs[turn ^ c][x] * 2 + c)...  7.12 us
    all_to_all x1, waiting for transfers between devices, spread(): return lax.all_to_all(copies, axes, 0, 0, tiled=True)  7.1 us
    all_to_all x1, waiting for transfers between devices, shards(): gathered = lax.all_to_all(copies, ('h', 'z'), 0, 0, tiled=True)  6.32 us
    ppermute x1, starting transfers between devices, gather_codes(): other = lax.ppermute(block, 'c', [(0, 1), (1, 0)])  5.27 us
  transfers between devices with their start and end apart: 5, of which 2 were waited for; matrix products, arithmetic and copies ran while one was open for 1% of the time, Pallas kernels for 1%

profile of v9, /device:TPU:1, one launch (start us, length us, event | category | flops | bytes accessed | tf_op | source)
XLA Modules:
  0.0 132.9 jit_solution(12012711615065143865)
XLA Ops:
  0.6 5.2 %collective-permute-start = (bf16[256,256]{1,0:T(8,128)(2,1)}, bf16[256,256]{1,0:T(8,128)(2,1)S(1)}, u32[]{:S(2)}, u32[]{:S(2)}) collective-permute-start(bf16[256,256]{1,0:T(8,128)(2,1)} %codes_ref.1), channel_id=1, source_target_pairs={{0,16},{1,49},{16,0},{17,33},{32,48},{33,17},{48,32},{49,1},{2,18}... | collective-permute-start | bytes 393224 | tf_op jit(solution)/shard_map/ppermute | solution.py:81
  5.9 0.9 copy-done
  6.8 0.7 copy-done.1
  7.5 1.2 shard_map.41
  8.7 1.9 %collective-permute-start.1 = (bf16[2,256,256]{2,1,0:T(8,128)(2,1)S(1)}, bf16[2,256,256]{2,1,0:T(8,128)(2,1)S(1)}, u32[]{:S(2)}, u32[]{:S(2)}) collective-permute-start(bf16[2,256,256]{2,1,0:T(8,128)(2,1)S(1)} %pad_maximum_fusion.6), channel_id=1, source_target_pairs={{0,48},{1,17},{16,32},{17,1},{32,16},{33,49},{48,0},{49,33},{2,50}... | collective-permute-start | bytes 786440 | tf_op jit(solution)/shard_map/ppermute | solution.py:81
  10.6 15.9 %all-to-all-start = ((bf16[32,16,256]{2,1,0:T(8,128)(2,1)}), bf16[32,16,256]{2,1,0:T(8,128)(2,1)S(1)}, u32[]{:S(2)}, u32[]{:S(2)}) async-start(bf16[32,16,256]{2,1,0:T(8,128)(2,1)} %get-tuple-element.11), calls=%async_computation | async-start | bytes 524288 | tf_op jit(solution)/shard_map/all_to_all | solution.py:119
  26.8 5.3 %collective-permute-start.2 = (bf16[4,256,256]{2,1,0:T(8,128)(2,1)S(1)}, bf16[4,256,256]{2,1,0:T(8,128)(2,1)S(1)}, u32[]{:S(2)}, u32[]{:S(2)}) collective-permute-start(bf16[4,256,256]{2,1,0:T(8,128)(2,1)S(1)} %pad_maximum_fusion.3), channel_id=1, source_target_pairs={{0,1},{1,0},{2,3},{3,2},{4,5},{5,4},{6,7},{7,6},{8,9},{9,8},{10,11... | collective-permute-start | bytes 1572872 | tf_op jit(solution)/shard_map/ppermute | solution.py:101
  32.1 6.3 %all-to-all-done = bf16[32,16,256]{2,1,0:T(8,128)(2,1)S(1)} async-done(((bf16[32,16,256]{2,1,0:T(8,128)(2,1)}), bf16[32,16,256]{2,1,0:T(8,128)(2,1)S(1)}, u32[]{:S(2)}, u32[]{:S(2)}) %all-to-all-start) | async-done | bytes 262176 | tf_op jit(solution)/shard_map/all_to_all | solution.py:119
  39.4 1.1 fusion.5
  40.9 13.9 %all_to_all.47 = bf16[16,4,512]{2,1,0:T(4,128)(2,1)S(1)} all-to-all(bf16[16,4,512]{2,1,0:T(4,128)(2,1)S(1)} %broadcast_in_dim.14), channel_id=1, replica_groups=mesh['h'=4,'l'=2,'x'=4,'z'=8,'c'=2] {'x','c','l'}, dimensions={0} | all-to-all | bytes 131072 | tf_op jit(solution)/shard_map/all_to_all | solution.py:19
  55.5 9.5 %all_to_all.48 = f32[8,1,512]{2,1,0:T(1,128)S(1)} all-to-all(f32[8,1,512]{2,1,0:T(1,128)S(1)} %broadcast_in_dim.15), channel_id=1, replica_groups=mesh['h'=4,'l'=2,'x'=4,'z'=8,'c'=2] {'z'}, dimensions={0} | all-to-all | bytes 32768 | tf_op jit(solution)/shard_map/all_to_all | solution.py:19
  64.9 0.5 fusion.1
  65.5 10.2 %all_to_all.49 = bf16[16,4,512]{2,1,0:T(4,128)(2,1)S(1)} all-to-all(bf16[16,4,512]{2,1,0:T(4,128)(2,1)S(1)} %broadcast_in_dim.16), channel_id=1, replica_groups=mesh['h'=4,'l'=2,'x'=4,'z'=8,'c'=2] {'x','c','l'}, dimensions={0} | all-to-all | bytes 131072 | tf_op jit(solution)/shard_map/all_to_all | solution.py:19
  76.3 9.0 %all_to_all.50 = f32[8,1,512]{2,1,0:T(1,128)S(1)} all-to-all(f32[8,1,512]{2,1,0:T(1,128)S(1)} %broadcast_in_dim.17), channel_id=1, replica_groups=mesh['h'=4,'l'=2,'x'=4,'z'=8,'c'=2] {'z'}, dimensions={0} | all-to-all | bytes 32768 | tf_op jit(solution)/shard_map/all_to_all | solution.py:19
  85.3 0.5 fusion.3
  85.8 9.9 %all_to_all.51 = bf16[16,4,512]{2,1,0:T(4,128)(2,1)S(1)} all-to-all(bf16[16,4,512]{2,1,0:T(4,128)(2,1)S(1)} %broadcast_in_dim.18), channel_id=1, replica_groups=mesh['h'=4,'l'=2,'x'=4,'z'=8,'c'=2] {'x','c','l'}, dimensions={0} | all-to-all | bytes 131072 | tf_op jit(solution)/shard_map/all_to_all | solution.py:19
  95.8 0.6 fusion.11
  97.0 9.9 %all_to_all.52 = bf16[8,24,256]{2,1,0:T(8,128)(2,1)S(1)} all-to-all(bf16[8,24,256]{2,1,0:T(8,128)(2,1)S(1)} %pad_maximum_fusion.7), channel_id=1, replica_groups=mesh['h'=4,'l'=2,'x'=4,'z'=8,'c'=2] {'z'}, dimensions={0} | all-to-all | bytes 196608 | tf_op jit(solution)/shard_map/all_to_all | solution.py:169
  108.0 11.9 %all_to_all.53 = bf16[16,40,256]{2,1,0:T(8,128)(2,1)S(1)} all-to-all(bf16[16,40,256]{2,1,0:T(8,128)(2,1)S(1)} %pad_maximum_fusion.4), channel_id=1, replica_groups=mesh['h'=4,'l'=2,'x'=4,'z'=8,'c'=2] {'x','c','l'}, dimensions={0} | all-to-all | bytes 655360 | tf_op jit(solution)/shard_map/all_to_all | solution.py:187
  120.1 0.7 broadcast_in_dim.20
  120.8 3.6 %all-to-all-start.8 = ((f16[8,32,256]{2,1,0:T(8,128)(2,1)}), f16[8,32,256]{2,1,0:T(8,128)(2,1)S(1)}, u32[]{:S(2)}, u32[]{:S(2)}) async-start(f16[8,32,256]{2,1,0:T(8,128)(2,1)} %broadcast_in_dim.20), calls=%async_computation.8 | async-start | bytes 262144 | tf_op jit(solution)/shard_map/all_to_all | solution.py:19
  124.4 0.7 fusion.21
  125.1 7.1 %all-to-all-done.8 = f16[8,32,256]{2,1,0:T(8,128)(2,1)S(1)} async-done(((f16[8,32,256]{2,1,0:T(8,128)(2,1)}), f16[8,32,256]{2,1,0:T(8,128)(2,1)S(1)}, u32[]{:S(2)}, u32[]{:S(2)}) %all-to-all-start.8) | async-done | bytes 131104 | tf_op jit(solution)/shard_map/all_to_all | solution.py:19
  132.2 0.7 bitcast_convert_fusion
  (62 shorter events, 4.5 us)
Async XLA Ops:
  0.6 8.0 %collective-permute-start = (bf16[256,256]{1,0:T(8,128)(2,1)}, bf16[256,256]{1,0:T(8,128)(2,1)S(1)}, u32[]{:S(2)}, u32[]{:S(2)}) collective-permute-start(bf16[256,256]{1,0:T(8,128)(2,1)} %codes_ref.1), channel_id=1, source_target_pairs={{0,16},{1,49},{16,0},{17,33},{32,48},{33,17},{48,32},{49,1},{2,18}... | collective-permute-start | bytes 393224 | tf_op jit(solution)/shard_map/ppermute | solution.py:81
  5.8 0.9 copy-start
  6.8 0.7 copy-start.1
  8.7 17.9 %collective-permute-start.1 = (bf16[2,256,256]{2,1,0:T(8,128)(2,1)S(1)}, bf16[2,256,256]{2,1,0:T(8,128)(2,1)S(1)}, u32[]{:S(2)}, u32[]{:S(2)}) collective-permute-start(bf16[2,256,256]{2,1,0:T(8,128)(2,1)S(1)} %pad_maximum_fusion.6), channel_id=1, source_target_pairs={{0,48},{1,17},{16,32},{17,1},{32,16},{33,49},{48,0},{49,33},{2,50}... | collective-permute-start | bytes 786440 | tf_op jit(solution)/shard_map/ppermute | solution.py:81
  10.6 27.8 %all-to-all-start = ((bf16[32,16,256]{2,1,0:T(8,128)(2,1)}), bf16[32,16,256]{2,1,0:T(8,128)(2,1)S(1)}, u32[]{:S(2)}, u32[]{:S(2)}) async-start(bf16[32,16,256]{2,1,0:T(8,128)(2,1)} %get-tuple-element.11), calls=%async_computation | async-start | bytes 524288 | tf_op jit(solution)/shard_map/all_to_all | solution.py:119
  26.8 11.8 %collective-permute-start.2 = (bf16[4,256,256]{2,1,0:T(8,128)(2,1)S(1)}, bf16[4,256,256]{2,1,0:T(8,128)(2,1)S(1)}, u32[]{:S(2)}, u32[]{:S(2)}) collective-permute-start(bf16[4,256,256]{2,1,0:T(8,128)(2,1)S(1)} %pad_maximum_fusion.3), channel_id=1, source_target_pairs={{0,1},{1,0},{2,3},{3,2},{4,5},{5,4},{6,7},{7,6},{8,9},{9,8},{10,11... | collective-permute-start | bytes 1572872 | tf_op jit(solution)/shard_map/ppermute | solution.py:101
  39.4 1.2 copy-start.3
  96.4 10.5 %slice-start = ((f32[4,512]{1,0:T(4,128)}), f32[1,512]{1,0:T(1,128)S(1)}, s32[]{:S(2)}) async-start(f32[4,512]{1,0:T(4,128)} %copy-done.3), calls=%async_computation.9 | async-start | bytes 4096 | tf_op jit(solution)/shard_map/slice | solution.py:125
  107.5 16.9 %copy-start.2 = (bf16[16,256]{1,0:T(8,128)(2,1)S(1)}, bf16[16,256]{1,0:T(8,128)(2,1)}, u32[]{:S(2)}) copy-start(bf16[16,256]{1,0:T(8,128)(2,1)} %rows_ref.1) | copy-start | bytes 24580
  120.8 11.4 %all-to-all-start.8 = ((f16[8,32,256]{2,1,0:T(8,128)(2,1)}), f16[8,32,256]{2,1,0:T(8,128)(2,1)S(1)}, u32[]{:S(2)}, u32[]{:S(2)}) async-start(f16[8,32,256]{2,1,0:T(8,128)(2,1)} %broadcast_in_dim.20), calls=%async_computation.8 | async-start | bytes 262144 | tf_op jit(solution)/shard_map/all_to_all | solution.py:19

commit v10 on v9

--- a/solution.py
+++ b/solution.py
@@ -19,9 +19,7 @@
     return lax.all_to_all(copies, axes, 0, 0, tiled=True)
 
 
-def prepare_kernel(rows_ref, codes_ref, copies_ref, held_ref, block, sems, codes_sem):
-    keep = pltpu.make_async_copy(codes_ref, held_ref, codes_sem)
-    keep.start()
+def copies_kernel(rows_ref, copies_ref, block, sems):
     members = copies_ref.shape[0]
     read = pltpu.make_async_copy(rows_ref, block, sems.at[members])
     read.start()
@@ -34,25 +32,31 @@
         write.start()
     for write in writes:
         write.wait()
-    keep.wait()
-
-
-def prepare(residuals, codebook, members):
+
+
+def copies_of(block, members):
     return pl.pallas_call(
-        prepare_kernel,
-        out_shape=(
-            jax.ShapeDtypeStruct((members,) + residuals.shape, residuals.dtype),
-            jax.ShapeDtypeStruct(codebook.shape, codebook.dtype),
-        ),
-        in_specs=[pl.BlockSpec(memory_space=pl.ANY)] * 2,
-        out_specs=(pl.BlockSpec(memory_space=pl.ANY), pl.BlockSpec(memory_space=pltpu.VMEM)),
+        copies_kernel,
+        out_shape=jax.ShapeDtypeStruct((members,) + block.shape, block.dtype),
+        in_specs=[pl.BlockSpec(memory_space=pl.ANY)],
+        out_specs=pl.BlockSpec(memory_space=pl.ANY),
         scratch_shapes=[
-            pltpu.VMEM(residuals.shape, residuals.dtype),
+            pltpu.VMEM(block.shape, block.dtype),
             pltpu.SemaphoreType.DMA((members + 1,)),
-            pltpu.SemaphoreType.DMA,
         ],
+    )(block)
+
+
+def hold_kernel(block_ref, held_ref):
+    held_ref[...] = block_ref[...]
+
+
+def hold(block):
+    return pl.pallas_call(
+        hold_kernel,
+        out_shape=jax.ShapeDtypeStruct(block.shape, block.dtype),
         compiler_params=pltpu.CompilerParams(vmem_limit_bytes=2**21),
-    )(residuals, codebook)
+    )(block)
 
 
 def two_terms(values):
@@ -70,7 +74,7 @@
     )
 
 
-def gather_codes(codebook, held, piece):
+def gather_codes(codebook, piece):
     width = codebook.shape[1]
     pieces = lax.axis_size("h")
     across = lax.axis_size("x")
@@ -84,10 +88,11 @@
             [(x * 2 + c, pairs[turn ^ c][x] * 2 + c) for x in range(across) for c in range(2)],
         )
 
-    other = swap(codebook, 0)
-    block = jnp.stack([held, other])
-    other = swap(block, 1)
-    block = jnp.concatenate([block, other])
+    first = swap(codebook, 0)
+    second = swap(codebook, 1)
+    third = swap(first, 1)
+    own = hold(codebook)
+    block = jnp.stack([own, first, second, third])
     near, far = place ^ 1, across - 1 - place
     places = [
         jnp.where(
@@ -115,10 +120,10 @@
     codes = codebook.shape[0] * lax.axis_size(("x", "c"))
     piece = lax.axis_index("h").astype(jnp.uint32)
     own_at = lax.axis_index("z").astype(jnp.uint32) * rows
-    copies, held = prepare(residuals, codebook, pieces * depth)
+    copies = copies_of(residuals, pieces * depth)
     gathered = lax.all_to_all(copies, ("h", "z"), 0, 0, tiled=True)
     gathered = gathered.reshape(pieces, -1, width)
-    codebook = gather_codes(codebook, held, piece)
+    codebook = gather_codes(codebook, piece)
     codes_float = codebook.astype(jnp.float32)
     code_scale = lax.rsqrt(jnp.mean(codes_float * codes_float, axis=2) + EPSILON)
     code_scale, own_scale, own_at = lax.optimization_barrier(

time: 134 us -> 135 us (level)
  starting transfers between devices: 31.9 us -> 34.5 us
    ppermute x2 -> x3, starting transfers between devices: 7.12 us -> 9.88 us  [swap(): lax.ppermute(block, ('x', 'c'), [(x * 2 + c, pairs[turn ^ c][x] * 2 + c)...]
  transfers between devices with their start and end apart: 5 -> 6, of which waited for: 2 -> 3; matrix products, arithmetic and copies ran while one was open for 1% -> 1% of each run, Pallas kernels for 1% -> 1%
where the time goes in v10:
time: 135 us
  blocking collectives  74 us (55%)
  starting transfers between devices  34.5 us (26%)
  waiting for transfers between devices  13.1 us (10%)
  other arithmetic  5.53 us (4%)
  matrix products  2.61 us (2%)
  local copies, waits for them, and re-layouts  2.11 us (2%)
  Pallas kernels  1.72 us (1%)
    all_to_all x5, blocking collectives, spread(): return lax.all_to_all(copies, axes, 0, 0, tiled=True)  52.2 us
    all_to_all x1, starting transfers between devices, shards(): gathered = lax.all_to_all(copies, ('h', 'z'), 0, 0, tiled=True)  15.7 us
    all_to_all x1, blocking collectives, shards(): packed = lax.all_to_all(packed, ITEM_AXES, 0, 0, tiled=True)  11.9 us
    all_to_all x1, blocking collectives, shards(): packed = lax.all_to_all(packed, 'z', 0, 0, tiled=True)  9.92 us
    ppermute x3, starting transfers between devices, swap(): lax.ppermute(block, ('x', 'c'), [(x * 2 + c, pairs[turn ^ c][x] * 2 + c)...  9.88 us
    all_to_all x1, waiting for transfers between devices, spread(): return lax.all_to_all(copies, axes, 0, 0, tiled=True)  7.1 us
    all_to_all x1, waiting for transfers between devices, shards(): gathered = lax.all_to_all(copies, ('h', 'z'), 0, 0, tiled=True)  5.34 us
    ppermute x1, starting transfers between devices, gather_codes(): other = lax.ppermute(block, 'c', [(0, 1), (1, 0)])  5.32 us
  transfers between devices with their start and end apart: 6, of which 3 were waited for; matrix products, arithmetic and copies ran while one was open for 1% of the time, Pallas kernels for 1%

profile of v10, /device:TPU:1, one launch (start us, length us, event | category | flops | bytes accessed | tf_op | source)
XLA Modules:
  0.0 134.6 jit_solution(13934140534176741799)
XLA Ops:
  0.6 5.2 %collective-permute-start = (bf16[256,256]{1,0:T(8,128)(2,1)}, bf16[256,256]{1,0:T(8,128)(2,1)S(1)}, u32[]{:S(2)}, u32[]{:S(2)}) collective-permute-start(bf16[256,256]{1,0:T(8,128)(2,1)} %block_ref.1), channel_id=1, source_target_pairs={{0,16},{1,49},{16,0},{17,33},{32,48},{33,17},{48,32},{49,1},{2,18}... | collective-permute-start | bytes 393224 | tf_op jit(solution)/shard_map/ppermute | solution.py:85
  5.8 1.9 %collective-permute-start.1 = (bf16[256,256]{1,0:T(8,128)(2,1)}, bf16[256,256]{1,0:T(8,128)(2,1)S(1)}, u32[]{:S(2)}, u32[]{:S(2)}) collective-permute-start(bf16[256,256]{1,0:T(8,128)(2,1)} %block_ref.1), channel_id=1, source_target_pairs={{0,48},{1,17},{16,32},{17,1},{32,16},{33,49},{48,0},{49,33},{2,50}... | collective-permute-start | bytes 393224 | tf_op jit(solution)/shard_map/ppermute | solution.py:85
  7.8 0.6 collective-permute-done
  8.4 2.8 %collective-permute-start.2 = (bf16[256,256]{1,0:T(8,128)(2,1)S(1)}, bf16[256,256]{1,0:T(8,128)(2,1)S(1)}, u32[]{:S(2)}, u32[]{:S(2)}) collective-permute-start(bf16[256,256]{1,0:T(8,128)(2,1)S(1)} %collective-permute-done), channel_id=1, source_target_pairs={{0,48},{1,17},{16,32},{17,1},{32,16},{33,49},{48,0},{49,33},{2,50}... | collective-permute-start | bytes 393224 | tf_op jit(solution)/shard_map/ppermute | solution.py:85
  11.2 1.7 %shard_map.41 = bf16[32,16,256]{2,1,0:T(8,128)(2,1)} custom-call(bf16[16,256]{1,0:T(8,128)(2,1)} %rows_ref.1), custom_call_target="tpu_custom_call" | custom-call | tf_op jit(solution)/shard_map/pallas_call | solution.py:38
  12.9 15.7 %all-to-all-start = ((bf16[32,16,256]{2,1,0:T(8,128)(2,1)}), bf16[32,16,256]{2,1,0:T(8,128)(2,1)S(1)}, u32[]{:S(2)}, u32[]{:S(2)}) async-start(bf16[32,16,256]{2,1,0:T(8,128)(2,1)} %shard_map.41), calls=%async_computation | async-start | bytes 524288 | tf_op jit(solution)/shard_map/all_to_all | solution.py:124
  28.6 0.9 copy-done
  29.8 5.3 %collective-permute-start.3 = (bf16[4,256,256]{2,1,0:T(8,128)(2,1)S(1)}, bf16[4,256,256]{2,1,0:T(8,128)(2,1)S(1)}, u32[]{:S(2)}, u32[]{:S(2)}) collective-permute-start(bf16[4,256,256]{2,1,0:T(8,128)(2,1)S(1)} %pad_maximum_fusion.3), channel_id=1, source_target_pairs={{0,1},{1,0},{2,3},{3,2},{4,5},{5,4},{6,7},{7,6},{8,9},{9,8},{10,11... | collective-permute-start | bytes 1572872 | tf_op jit(solution)/shard_map/ppermute | solution.py:106
  35.1 5.3 %all-to-all-done = bf16[32,16,256]{2,1,0:T(8,128)(2,1)S(1)} async-done(((bf16[32,16,256]{2,1,0:T(8,128)(2,1)}), bf16[32,16,256]{2,1,0:T(8,128)(2,1)S(1)}, u32[]{:S(2)}, u32[]{:S(2)}) %all-to-all-start) | async-done | bytes 262176 | tf_op jit(solution)/shard_map/all_to_all | solution.py:124
  41.5 1.1 fusion.5
  43.0 13.6 %all_to_all.47 = bf16[16,4,512]{2,1,0:T(4,128)(2,1)S(1)} all-to-all(bf16[16,4,512]{2,1,0:T(4,128)(2,1)S(1)} %broadcast_in_dim.14), channel_id=1, replica_groups=mesh['h'=4,'l'=2,'x'=4,'z'=8,'c'=2] {'x','c','l'}, dimensions={0} | all-to-all | bytes 131072 | tf_op jit(solution)/shard_map/all_to_all | solution.py:19
  57.1 9.5 %all_to_all.48 = f32[8,1,512]{2,1,0:T(1,128)S(1)} all-to-all(f32[8,1,512]{2,1,0:T(1,128)S(1)} %broadcast_in_dim.15), channel_id=1, replica_groups=mesh['h'=4,'l'=2,'x'=4,'z'=8,'c'=2] {'z'}, dimensions={0} | all-to-all | bytes 32768 | tf_op jit(solution)/shard_map/all_to_all | solution.py:19
  66.6 0.5 fusion.1
  67.1 10.2 %all_to_all.49 = bf16[16,4,512]{2,1,0:T(4,128)(2,1)S(1)} all-to-all(bf16[16,4,512]{2,1,0:T(4,128)(2,1)S(1)} %broadcast_in_dim.16), channel_id=1, replica_groups=mesh['h'=4,'l'=2,'x'=4,'z'=8,'c'=2] {'x','c','l'}, dimensions={0} | all-to-all | bytes 131072 | tf_op jit(solution)/shard_map/all_to_all | solution.py:19
  77.9 9.0 %all_to_all.50 = f32[8,1,512]{2,1,0:T(1,128)S(1)} all-to-all(f32[8,1,512]{2,1,0:T(1,128)S(1)} %broadcast_in_dim.17), channel_id=1, replica_groups=mesh['h'=4,'l'=2,'x'=4,'z'=8,'c'=2] {'z'}, dimensions={0} | all-to-all | bytes 32768 | tf_op jit(solution)/shard_map/all_to_all | solution.py:19
  87.5 9.9 %all_to_all.51 = bf16[16,4,512]{2,1,0:T(4,128)(2,1)S(1)} all-to-all(bf16[16,4,512]{2,1,0:T(4,128)(2,1)S(1)} %broadcast_in_dim.18), channel_id=1, replica_groups=mesh['h'=4,'l'=2,'x'=4,'z'=8,'c'=2] {'x','c','l'}, dimensions={0} | all-to-all | bytes 131072 | tf_op jit(solution)/shard_map/all_to_all | solution.py:19
  97.5 0.6 fusion.11
  98.7 9.9 %all_to_all.52 = bf16[8,24,256]{2,1,0:T(8,128)(2,1)S(1)} all-to-all(bf16[8,24,256]{2,1,0:T(8,128)(2,1)S(1)} %pad_maximum_fusion.6), channel_id=1, replica_groups=mesh['h'=4,'l'=2,'x'=4,'z'=8,'c'=2] {'z'}, dimensions={0} | all-to-all | bytes 196608 | tf_op jit(solution)/shard_map/all_to_all | solution.py:174
  109.7 11.9 %all_to_all.53 = bf16[16,40,256]{2,1,0:T(8,128)(2,1)S(1)} all-to-all(bf16[16,40,256]{2,1,0:T(8,128)(2,1)S(1)} %pad_maximum_fusion.4), channel_id=1, replica_groups=mesh['h'=4,'l'=2,'x'=4,'z'=8,'c'=2] {'x','c','l'}, dimensions={0} | all-to-all | bytes 655360 | tf_op jit(solution)/shard_map/all_to_all | solution.py:192
  121.8 0.7 broadcast_in_dim.20
  122.4 3.6 %all-to-all-start.8 = ((f16[8,32,256]{2,1,0:T(8,128)(2,1)}), f16[8,32,256]{2,1,0:T(8,128)(2,1)S(1)}, u32[]{:S(2)}, u32[]{:S(2)}) async-start(f16[8,32,256]{2,1,0:T(8,128)(2,1)} %broadcast_in_dim.20), calls=%async_computation.8 | async-start | bytes 262144 | tf_op jit(solution)/shard_map/all_to_all | solution.py:19
  126.1 0.7 fusion.21
  126.8 7.1 %all-to-all-done.8 = f16[8,32,256]{2,1,0:T(8,128)(2,1)S(1)} async-done(((f16[8,32,256]{2,1,0:T(8,128)(2,1)}), f16[8,32,256]{2,1,0:T(8,128)(2,1)S(1)}, u32[]{:S(2)}, u32[]{:S(2)}) %all-to-all-start.8) | async-done | bytes 131104 | tf_op jit(solution)/shard_map/all_to_all | solution.py:19
  133.9 0.7 bitcast_convert_fusion
  (62 shorter events, 5.0 us)
Async XLA Ops:
  0.6 7.8 %collective-permute-start = (bf16[256,256]{1,0:T(8,128)(2,1)}, bf16[256,256]{1,0:T(8,128)(2,1)S(1)}, u32[]{:S(2)}, u32[]{:S(2)}) collective-permute-start(bf16[256,256]{1,0:T(8,128)(2,1)} %block_ref.1), channel_id=1, source_target_pairs={{0,16},{1,49},{16,0},{17,33},{32,48},{33,17},{48,32},{49,1},{2,18}... | collective-permute-start | bytes 393224 | tf_op jit(solution)/shard_map/ppermute | solution.py:85
  5.8 23.7 %collective-permute-start.1 = (bf16[256,256]{1,0:T(8,128)(2,1)}, bf16[256,256]{1,0:T(8,128)(2,1)S(1)}, u32[]{:S(2)}, u32[]{:S(2)}) collective-permute-start(bf16[256,256]{1,0:T(8,128)(2,1)} %block_ref.1), channel_id=1, source_target_pairs={{0,48},{1,17},{16,32},{17,1},{32,16},{33,49},{48,0},{49,33},{2,50}... | collective-permute-start | bytes 393224 | tf_op jit(solution)/shard_map/ppermute | solution.py:85
  8.4 21.2 %collective-permute-start.2 = (bf16[256,256]{1,0:T(8,128)(2,1)S(1)}, bf16[256,256]{1,0:T(8,128)(2,1)S(1)}, u32[]{:S(2)}, u32[]{:S(2)}) collective-permute-start(bf16[256,256]{1,0:T(8,128)(2,1)S(1)} %collective-permute-done), channel_id=1, source_target_pairs={{0,48},{1,17},{16,32},{17,1},{32,16},{33,49},{48,0},{49,33},{2,50}... | collective-permute-start | bytes 393224 | tf_op jit(solution)/shard_map/ppermute | solution.py:85
  12.9 27.6 %all-to-all-start = ((bf16[32,16,256]{2,1,0:T(8,128)(2,1)}), bf16[32,16,256]{2,1,0:T(8,128)(2,1)S(1)}, u32[]{:S(2)}, u32[]{:S(2)}) async-start(bf16[32,16,256]{2,1,0:T(8,128)(2,1)} %shard_map.41), calls=%async_computation | async-start | bytes 524288 | tf_op jit(solution)/shard_map/all_to_all | solution.py:124
  28.6 0.9 copy-start
  29.8 10.9 %collective-permute-start.3 = (bf16[4,256,256]{2,1,0:T(8,128)(2,1)S(1)}, bf16[4,256,256]{2,1,0:T(8,128)(2,1)S(1)}, u32[]{:S(2)}, u32[]{:S(2)}) collective-permute-start(bf16[4,256,256]{2,1,0:T(8,128)(2,1)S(1)} %pad_maximum_fusion.3), channel_id=1, source_target_pairs={{0,1},{1,0},{2,3},{3,2},{4,5},{5,4},{6,7},{7,6},{8,9},{9,8},{10,11... | collective-permute-start | bytes 1572872 | tf_op jit(solution)/shard_map/ppermute | solution.py:106
  41.5 1.2 copy-start.2
  98.1 10.5 %slice-start = ((f32[4,512]{1,0:T(4,128)}), f32[1,512]{1,0:T(1,128)S(1)}, s32[]{:S(2)}) async-start(f32[4,512]{1,0:T(4,128)} %copy-done.2), calls=%async_computation.9 | async-start | bytes 4096 | tf_op jit(solution)/shard_map/slice | solution.py:130
  109.2 16.9 %copy-start.1 = (bf16[16,256]{1,0:T(8,128)(2,1)S(1)}, bf16[16,256]{1,0:T(8,128)(2,1)}, u32[]{:S(2)}) copy-start(bf16[16,256]{1,0:T(8,128)(2,1)} %rows_ref.1) | copy-start | bytes 24580
  122.4 11.4 %all-to-all-start.8 = ((f16[8,32,256]{2,1,0:T(8,128)(2,1)}), f16[8,32,256]{2,1,0:T(8,128)(2,1)S(1)}, u32[]{:S(2)}, u32[]{:S(2)}) async-start(f16[8,32,256]{2,1,0:T(8,128)(2,1)} %broadcast_in_dim.20), calls=%async_computation.8 | async-start | bytes 262144 | tf_op jit(solution)/shard_map/all_to_all | solution.py:19

commit v11 on v9

--- a/solution.py
+++ b/solution.py
@@ -19,40 +19,16 @@
     return lax.all_to_all(copies, axes, 0, 0, tiled=True)
 
 
-def prepare_kernel(rows_ref, codes_ref, copies_ref, held_ref, block, sems, codes_sem):
-    keep = pltpu.make_async_copy(codes_ref, held_ref, codes_sem)
-    keep.start()
-    members = copies_ref.shape[0]
-    read = pltpu.make_async_copy(rows_ref, block, sems.at[members])
-    read.start()
-    read.wait()
-    writes = [
-        pltpu.make_async_copy(block, copies_ref.at[member], sems.at[member])
-        for member in range(members)
-    ]
-    for write in writes:
-        write.start()
-    for write in writes:
-        write.wait()
-    keep.wait()
+def hold_kernel(block_ref, held_ref):
+    held_ref[...] = block_ref[...]
 
 
-def prepare(residuals, codebook, members):
+def hold(block):
     return pl.pallas_call(
-        prepare_kernel,
-        out_shape=(
-            jax.ShapeDtypeStruct((members,) + residuals.shape, residuals.dtype),
-            jax.ShapeDtypeStruct(codebook.shape, codebook.dtype),
-        ),
-        in_specs=[pl.BlockSpec(memory_space=pl.ANY)] * 2,
-        out_specs=(pl.BlockSpec(memory_space=pl.ANY), pl.BlockSpec(memory_space=pltpu.VMEM)),
-        scratch_shapes=[
-            pltpu.VMEM(residuals.shape, residuals.dtype),
-            pltpu.SemaphoreType.DMA((members + 1,)),
-            pltpu.SemaphoreType.DMA,
-        ],
+        hold_kernel,
+        out_shape=jax.ShapeDtypeStruct(block.shape, block.dtype),
         compiler_params=pltpu.CompilerParams(vmem_limit_bytes=2**21),
-    )(residuals, codebook)
+    )(block)
 
 
 def two_terms(values):
@@ -115,9 +91,8 @@
     codes = codebook.shape[0] * lax.axis_size(("x", "c"))
     piece = lax.axis_index("h").astype(jnp.uint32)
     own_at = lax.axis_index("z").astype(jnp.uint32) * rows
-    copies, held = prepare(residuals, codebook, pieces * depth)
-    gathered = lax.all_to_all(copies, ("h", "z"), 0, 0, tiled=True)
-    gathered = gathered.reshape(pieces, -1, width)
+    gathered = spread(residuals, ("h", "z")).reshape(pieces, -1, width)
+    held = hold(codebook)
     codebook = gather_codes(codebook, held, piece)
     codes_float = codebook.astype(jnp.float32)
     code_scale = lax.rsqrt(jnp.mean(codes_float * codes_float, axis=2) + EPSILON)

time: 134 us -> 135 us (level)
  waiting for transfers between devices: 13.4 us -> 15.1 us
    all_to_all x1 -> x2, starting transfers between devices: 3.57 us -> 19.6 us  [spread(): return lax.all_to_all(copies, axes, 0, 0, tiled=True)]
    all_to_all x1 -> x0, starting transfers between devices: 15.9 us -> none  [shards(): gathered = lax.all_to_all(copies, ('h', 'z'), 0, 0, tiled=True)]
    all_to_all x1 -> x2, waiting for transfers between devices: 7.1 us -> 13.4 us  [spread(): return lax.all_to_all(copies, axes, 0, 0, tiled=True)]
    all_to_all x1 -> x0, waiting for transfers between devices: 6.32 us -> none  [shards(): gathered = lax.all_to_all(copies, ('h', 'z'), 0, 0, tiled=True)]
    ppermute x2, waiting for transfers between devices: 0.01 us -> 1.63 us  [swap(): lax.ppermute(block, ('x', 'c'), [(x * 2 + c, pairs[turn ^ c][x] * 2 + c)...]
    broadcast_in_dim x6 -> x7, local copies, waits for them, and re-layouts: 0.76 us -> 2.18 us  [spread(): copies = jnp.broadcast_to(block[None], (members,) + block.shape)]
  transfers between devices with their start and end apart: 5 -> 5, of which waited for: 2 -> 3; matrix products, arithmetic and copies ran while one was open for 1% -> 2% of each run, Pallas kernels for 1% -> 0%
where the time goes in v11:
time: 135 us; the launch traced here: 134 us
  blocking collectives  74.4 us (55%)
  starting transfers between devices  32.1 us (24%)
  waiting for transfers between devices  15.1 us (11%)
  other arithmetic  5.54 us (4%)
  local copies, waits for them, and re-layouts  3.54 us (3%)
  matrix products  2.61 us (2%)
    all_to_all x5, blocking collectives, spread(): return lax.all_to_all(copies, axes, 0, 0, tiled=True)  52.6 us
    all_to_all x2, starting transfers between devices, spread(): return lax.all_to_all(copies, axes, 0, 0, tiled=True)  19.6 us
    all_to_all x2, waiting for transfers between devices, spread(): return lax.all_to_all(copies, axes, 0, 0, tiled=True)  13.4 us
    all_to_all x1, blocking collectives, shards(): packed = lax.all_to_all(packed, ITEM_AXES, 0, 0, tiled=True)  11.9 us
    all_to_all x1, blocking collectives, shards(): packed = lax.all_to_all(packed, 'z', 0, 0, tiled=True)  9.92 us
    ppermute x2, starting transfers between devices, swap(): lax.ppermute(block, ('x', 'c'), [(x * 2 + c, pairs[turn ^ c][x] * 2 + c)...  7.3 us
    ppermute x1, starting transfers between devices, gather_codes(): other = lax.ppermute(block, 'c', [(0, 1), (1, 0)])  5.27 us
  transfers between devices with their start and end apart: 5, of which 3 were waited for; matrix products, arithmetic and copies ran while one was open for 2% of the time, Pallas kernels for 0%

profile of v11, /device:TPU:1, one launch (start us, length us, event | category | flops | bytes accessed | tf_op | source)
XLA Modules:
  0.0 134.3 jit_solution(1427626388212388150)
XLA Ops:
  0.6 5.2 %collective-permute-start = (bf16[256,256]{1,0:T(8,128)(2,1)}, bf16[256,256]{1,0:T(8,128)(2,1)S(1)}, u32[]{:S(2)}, u32[]{:S(2)}) collective-permute-start(bf16[256,256]{1,0:T(8,128)(2,1)} %block_ref.1), channel_id=1, source_target_pairs={{0,16},{1,49},{16,0},{17,33},{32,48},{33,17},{48,32},{49,1},{2,18}... | collective-permute-start | bytes 393224 | tf_op jit(solution)/shard_map/ppermute | solution.py:57
  5.9 0.9 copy-done
  6.8 1.6 %collective-permute-done = bf16[256,256]{1,0:T(8,128)(2,1)S(1)} collective-permute-done((bf16[256,256]{1,0:T(8,128)(2,1)}, bf16[256,256]{1,0:T(8,128)(2,1)S(1)}, u32[]{:S(2)}, u32[]{:S(2)}) %collective-permute-start) | collective-permute-done | bytes 131104 | tf_op jit(solution)/shard_map/ppermute | solution.py:57
  8.4 2.1 %collective-permute-start.1 = (bf16[2,256,256]{2,1,0:T(8,128)(2,1)S(1)}, bf16[2,256,256]{2,1,0:T(8,128)(2,1)S(1)}, u32[]{:S(2)}, u32[]{:S(2)}) collective-permute-start(bf16[2,256,256]{2,1,0:T(8,128)(2,1)S(1)} %pad_maximum_fusion.6), channel_id=1, source_target_pairs={{0,48},{1,17},{16,32},{17,1},{32,16},{33,49},{48,0},{49,33},{2,50}... | collective-permute-start | bytes 786440 | tf_op jit(solution)/shard_map/ppermute | solution.py:57
  10.5 1.4 %broadcast_in_dim.16 = bf16[32,16,256]{2,1,0:T(8,128)(2,1)} broadcast(bf16[16,256]{1,0:T(8,128)(2,1)} %param.2), dimensions={1,2} | broadcast | bytes 270336 | tf_op jit(solution)/shard_map/broadcast_in_dim | solution.py:18
  11.9 16.0 %all-to-all-start = ((bf16[32,16,256]{2,1,0:T(8,128)(2,1)}), bf16[32,16,256]{2,1,0:T(8,128)(2,1)S(1)}, u32[]{:S(2)}, u32[]{:S(2)}) async-start(bf16[32,16,256]{2,1,0:T(8,128)(2,1)} %broadcast_in_dim.16), calls=%async_computation | async-start | bytes 524288 | tf_op jit(solution)/shard_map/all_to_all | solution.py:19
  28.2 5.3 %collective-permute-start.2 = (bf16[4,256,256]{2,1,0:T(8,128)(2,1)S(1)}, bf16[4,256,256]{2,1,0:T(8,128)(2,1)S(1)}, u32[]{:S(2)}, u32[]{:S(2)}) collective-permute-start(bf16[4,256,256]{2,1,0:T(8,128)(2,1)S(1)} %pad_maximum_fusion.3), channel_id=1, source_target_pairs={{0,1},{1,0},{2,3},{3,2},{4,5},{5,4},{6,7},{7,6},{8,9},{9,8},{10,11... | collective-permute-start | bytes 1572872 | tf_op jit(solution)/shard_map/ppermute | solution.py:77
  33.5 6.3 %all-to-all-done = bf16[32,16,256]{2,1,0:T(8,128)(2,1)S(1)} async-done(((bf16[32,16,256]{2,1,0:T(8,128)(2,1)}), bf16[32,16,256]{2,1,0:T(8,128)(2,1)S(1)}, u32[]{:S(2)}, u32[]{:S(2)}) %all-to-all-start) | async-done | bytes 262176 | tf_op jit(solution)/shard_map/all_to_all | solution.py:19
  40.8 1.1 fusion.5
  42.4 13.9 %all_to_all.47 = bf16[16,4,512]{2,1,0:T(4,128)(2,1)S(1)} all-to-all(bf16[16,4,512]{2,1,0:T(4,128)(2,1)S(1)} %broadcast_in_dim.17), channel_id=1, replica_groups=mesh['h'=4,'l'=2,'x'=4,'z'=8,'c'=2] {'x','c','l'}, dimensions={0} | all-to-all | bytes 131072 | tf_op jit(solution)/shard_map/all_to_all | solution.py:19
  56.9 9.4 %all_to_all.48 = f32[8,1,512]{2,1,0:T(1,128)S(1)} all-to-all(f32[8,1,512]{2,1,0:T(1,128)S(1)} %broadcast_in_dim.18), channel_id=1, replica_groups=mesh['h'=4,'l'=2,'x'=4,'z'=8,'c'=2] {'z'}, dimensions={0} | all-to-all | bytes 32768 | tf_op jit(solution)/shard_map/all_to_all | solution.py:19
  66.3 0.5 fusion.1
  66.9 10.2 %all_to_all.49 = bf16[16,4,512]{2,1,0:T(4,128)(2,1)S(1)} all-to-all(bf16[16,4,512]{2,1,0:T(4,128)(2,1)S(1)} %broadcast_in_dim.19), channel_id=1, replica_groups=mesh['h'=4,'l'=2,'x'=4,'z'=8,'c'=2] {'x','c','l'}, dimensions={0} | all-to-all | bytes 131072 | tf_op jit(solution)/shard_map/all_to_all | solution.py:19
  77.7 9.0 %all_to_all.50 = f32[8,1,512]{2,1,0:T(1,128)S(1)} all-to-all(f32[8,1,512]{2,1,0:T(1,128)S(1)} %broadcast_in_dim.20), channel_id=1, replica_groups=mesh['h'=4,'l'=2,'x'=4,'z'=8,'c'=2] {'z'}, dimensions={0} | all-to-all | bytes 32768 | tf_op jit(solution)/shard_map/all_to_all | solution.py:19
  86.7 0.5 fusion.3
  87.2 9.9 %all_to_all.51 = bf16[16,4,512]{2,1,0:T(4,128)(2,1)S(1)} all-to-all(bf16[16,4,512]{2,1,0:T(4,128)(2,1)S(1)} %broadcast_in_dim.21), channel_id=1, replica_groups=mesh['h'=4,'l'=2,'x'=4,'z'=8,'c'=2] {'x','c','l'}, dimensions={0} | all-to-all | bytes 131072 | tf_op jit(solution)/shard_map/all_to_all | solution.py:19
  97.2 0.6 fusion.11
  98.4 9.9 %all_to_all.52 = bf16[8,24,256]{2,1,0:T(8,128)(2,1)S(1)} all-to-all(bf16[8,24,256]{2,1,0:T(8,128)(2,1)S(1)} %pad_maximum_fusion.7), channel_id=1, replica_groups=mesh['h'=4,'l'=2,'x'=4,'z'=8,'c'=2] {'z'}, dimensions={0} | all-to-all | bytes 196608 | tf_op jit(solution)/shard_map/all_to_all | solution.py:144
  109.4 11.9 %all_to_all.53 = bf16[16,40,256]{2,1,0:T(8,128)(2,1)S(1)} all-to-all(bf16[16,40,256]{2,1,0:T(8,128)(2,1)S(1)} %pad_maximum_fusion.4), channel_id=1, replica_groups=mesh['h'=4,'l'=2,'x'=4,'z'=8,'c'=2] {'x','c','l'}, dimensions={0} | all-to-all | bytes 655360 | tf_op jit(solution)/shard_map/all_to_all | solution.py:162
  121.5 0.7 broadcast_in_dim.23
  122.2 3.6 %all-to-all-start.8 = ((f16[8,32,256]{2,1,0:T(8,128)(2,1)}), f16[8,32,256]{2,1,0:T(8,128)(2,1)S(1)}, u32[]{:S(2)}, u32[]{:S(2)}) async-start(f16[8,32,256]{2,1,0:T(8,128)(2,1)} %broadcast_in_dim.23), calls=%async_computation.8 | async-start | bytes 262144 | tf_op jit(solution)/shard_map/all_to_all | solution.py:19
  125.8 0.7 fusion.21
  126.5 7.1 %all-to-all-done.8 = f16[8,32,256]{2,1,0:T(8,128)(2,1)S(1)} async-done(((f16[8,32,256]{2,1,0:T(8,128)(2,1)}), f16[8,32,256]{2,1,0:T(8,128)(2,1)S(1)}, u32[]{:S(2)}, u32[]{:S(2)}) %all-to-all-start.8) | async-done | bytes 131104 | tf_op jit(solution)/shard_map/all_to_all | solution.py:19
  133.6 0.7 bitcast_convert_fusion
  (61 shorter events, 4.5 us)
Async XLA Ops:
  0.6 7.8 %collective-permute-start = (bf16[256,256]{1,0:T(8,128)(2,1)}, bf16[256,256]{1,0:T(8,128)(2,1)S(1)}, u32[]{:S(2)}, u32[]{:S(2)}) collective-permute-start(bf16[256,256]{1,0:T(8,128)(2,1)} %block_ref.1), channel_id=1, source_target_pairs={{0,16},{1,49},{16,0},{17,33},{32,48},{33,17},{48,32},{49,1},{2,18}... | collective-permute-start | bytes 393224 | tf_op jit(solution)/shard_map/ppermute | solution.py:57
  5.8 0.9 copy-start
  8.4 19.6 %collective-permute-start.1 = (bf16[2,256,256]{2,1,0:T(8,128)(2,1)S(1)}, bf16[2,256,256]{2,1,0:T(8,128)(2,1)S(1)}, u32[]{:S(2)}, u32[]{:S(2)}) collective-permute-start(bf16[2,256,256]{2,1,0:T(8,128)(2,1)S(1)} %pad_maximum_fusion.6), channel_id=1, source_target_pairs={{0,48},{1,17},{16,32},{17,1},{32,16},{33,49},{48,0},{49,33},{2,50}... | collective-permute-start | bytes 786440 | tf_op jit(solution)/shard_map/ppermute | solution.py:57
  11.9 27.9 %all-to-all-start = ((bf16[32,16,256]{2,1,0:T(8,128)(2,1)}), bf16[32,16,256]{2,1,0:T(8,128)(2,1)S(1)}, u32[]{:S(2)}, u32[]{:S(2)}) async-start(bf16[32,16,256]{2,1,0:T(8,128)(2,1)} %broadcast_in_dim.16), calls=%async_computation | async-start | bytes 524288 | tf_op jit(solution)/shard_map/all_to_all | solution.py:19
  28.2 11.8 %collective-permute-start.2 = (bf16[4,256,256]{2,1,0:T(8,128)(2,1)S(1)}, bf16[4,256,256]{2,1,0:T(8,128)(2,1)S(1)}, u32[]{:S(2)}, u32[]{:S(2)}) collective-permute-start(bf16[4,256,256]{2,1,0:T(8,128)(2,1)S(1)} %pad_maximum_fusion.3), channel_id=1, source_target_pairs={{0,1},{1,0},{2,3},{3,2},{4,5},{5,4},{6,7},{7,6},{8,9},{9,8},{10,11... | collective-permute-start | bytes 1572872 | tf_op jit(solution)/shard_map/ppermute | solution.py:77
  40.8 1.2 copy-start.2
  97.9 10.5 %slice-start = ((f32[4,512]{1,0:T(4,128)}), f32[1,512]{1,0:T(1,128)S(1)}, s32[]{:S(2)}) async-start(f32[4,512]{1,0:T(4,128)} %copy-done.2), calls=%async_computation.9 | async-start | bytes 4096 | tf_op jit(solution)/shard_map/slice | solution.py:100
  108.9 16.9 %copy-start.1 = (bf16[16,256]{1,0:T(8,128)(2,1)S(1)}, bf16[16,256]{1,0:T(8,128)(2,1)}, u32[]{:S(2)}) copy-start(bf16[16,256]{1,0:T(8,128)(2,1)} %param.2) | copy-start | bytes 24580
  122.2 11.4 %all-to-all-start.8 = ((f16[8,32,256]{2,1,0:T(8,128)(2,1)}), f16[8,32,256]{2,1,0:T(8,128)(2,1)S(1)}, u32[]{:S(2)}, u32[]{:S(2)}) async-start(f16[8,32,256]{2,1,0:T(8,128)(2,1)} %broadcast_in_dim.23), calls=%async_computation.8 | async-start | bytes 262144 | tf_op jit(solution)/shard_map/all_to_all | solution.py:19

commit v12 on v11

--- a/solution.py
+++ b/solution.py
@@ -62,19 +62,26 @@
 
     other = swap(codebook, 0)
     block = jnp.stack([held, other])
-    other = swap(block, 1)
-    block = jnp.concatenate([block, other])
-    near, far = place ^ 1, across - 1 - place
-    places = [
-        jnp.where(
-            x == place,
-            0,
-            jnp.where(x == near, 1 + core, jnp.where(x == far, 2 - core, 3)),
+    last = swap(block, 1)
+    other = lax.ppermute(block, "c", [(0, 1), (1, 0)])
+    other_last = lax.ppermute(last, "c", [(0, 1), (1, 0)])
+
+    def in_order(block, core):
+        near, far = place ^ 1, across - 1 - place
+        places = [
+            jnp.where(
+                x == place,
+                0,
+                jnp.where(x == near, 1 + core, jnp.where(x == far, 2 - core, 3)),
+            )
+            for x in range(across)
+        ]
+        return jnp.stack(
+            [lax.dynamic_index_in_dim(block, at, keepdims=False) for at in places]
         )
-        for x in range(across)
-    ]
-    block = jnp.stack([lax.dynamic_index_in_dim(block, at, keepdims=False) for at in places])
-    other = lax.ppermute(block, "c", [(0, 1), (1, 0)])
+
+    block = in_order(jnp.concatenate([block, last]), core)
+    other = in_order(jnp.concatenate([other, other_last]), 1 - core)
     zero = core == 0
     both = jnp.stack([jnp.where(zero, block, other), jnp.where(zero, other, block)], axis=1)
     both = both.reshape(across * 2, pieces, -1, width)

time: 135 us -> 138 us (1.022)
  waiting for transfers between devices: 15.1 us -> 19 us
  blocking collectives: 74.4 us -> 71.2 us
  starting transfers between devices: 32.1 us -> 34.1 us
    all_to_all x2, starting transfers between devices: 19.6 us -> 15.6 us  [spread(): return lax.all_to_all(copies, axes, 0, 0, tiled=True)]
    all_to_all x2, waiting for transfers between devices: 13.4 us -> 17.4 us  [spread(): return lax.all_to_all(copies, axes, 0, 0, tiled=True)]
    ppermute x1, starting transfers between devices: 5.27 us -> 8.99 us  [gather_codes(): other = lax.ppermute(block, 'c', [(0, 1), (1, 0)])]
    all_to_all x5, blocking collectives: 52.6 us -> 49.4 us  [spread(): return lax.all_to_all(copies, axes, 0, 0, tiled=True)]
    ppermute x0 -> x1, starting transfers between devices: none -> 2.2 us  [gather_codes(): other_last = lax.ppermute(last, 'c', [(0, 1), (1, 0)])]
  transfers between devices with their start and end apart: 5 -> 6, of which waited for: 3 -> 3; matrix products, arithmetic and copies ran while one was open for 2% -> 2% of each run, Pallas kernels for 0% -> 0%
where the time goes in v12:
time: 138 us; the launch traced here: 137 us
  blocking collectives  71.2 us (52%)
  starting transfers between devices  34.1 us (25%)
  waiting for transfers between devices  19 us (14%)
  other arithmetic  5.51 us (4%)
  local copies, waits for them, and re-layouts  3.55 us (3%)
  matrix products  2.61 us (2%)
    all_to_all x5, blocking collectives, spread(): return lax.all_to_all(copies, axes, 0, 0, tiled=True)  49.4 us
    all_to_all x2, waiting for transfers between devices, spread(): return lax.all_to_all(copies, axes, 0, 0, tiled=True)  17.4 us
    all_to_all x2, starting transfers between devices, spread(): return lax.all_to_all(copies, axes, 0, 0, tiled=True)  15.6 us
    all_to_all x1, blocking collectives, shards(): packed = lax.all_to_all(packed, ITEM_AXES, 0, 0, tiled=True)  11.9 us
    all_to_all x1, blocking collectives, shards(): packed = lax.all_to_all(packed, 'z', 0, 0, tiled=True)  9.91 us
    ppermute x1, starting transfers between devices, gather_codes(): other = lax.ppermute(block, 'c', [(0, 1), (1, 0)])  8.99 us
    ppermute x2, starting transfers between devices, swap(): lax.ppermute(block, ('x', 'c'), [(x * 2 + c, pairs[turn ^ c][x] * 2 + c)...  7.3 us
  transfers between devices with their start and end apart: 6, of which 3 were waited for; matrix products, arithmetic and copies ran while one was open for 2% of the time, Pallas kernels for 0%

profile of v12, /device:TPU:1, one launch (start us, length us, event | category | flops | bytes accessed | tf_op | source)
XLA Modules:
  0.0 137.1 jit_solution(12556505387674108047)
XLA Ops:
  0.6 5.2 %collective-permute-start = (bf16[256,256]{1,0:T(8,128)(2,1)}, bf16[256,256]{1,0:T(8,128)(2,1)S(1)}, u32[]{:S(2)}, u32[]{:S(2)}) collective-permute-start(bf16[256,256]{1,0:T(8,128)(2,1)} %block_ref.1), channel_id=1, source_target_pairs={{0,16},{1,49},{16,0},{17,33},{32,48},{33,17},{48,32},{49,1},{2,18}... | collective-permute-start | bytes 393224 | tf_op jit(solution)/shard_map/ppermute | solution.py:57
  5.9 0.9 copy-done
  6.8 1.6 %collective-permute-done = bf16[256,256]{1,0:T(8,128)(2,1)S(1)} collective-permute-done((bf16[256,256]{1,0:T(8,128)(2,1)}, bf16[256,256]{1,0:T(8,128)(2,1)S(1)}, u32[]{:S(2)}, u32[]{:S(2)}) %collective-permute-start) | collective-permute-done | bytes 131104 | tf_op jit(solution)/shard_map/ppermute | solution.py:57
  8.4 2.1 %collective-permute-start.1 = (bf16[2,256,256]{2,1,0:T(8,128)(2,1)S(1)}, bf16[2,256,256]{2,1,0:T(8,128)(2,1)S(1)}, u32[]{:S(2)}, u32[]{:S(2)}) collective-permute-start(bf16[2,256,256]{2,1,0:T(8,128)(2,1)S(1)} %pad_maximum_fusion.7), channel_id=1, source_target_pairs={{0,48},{1,17},{16,32},{17,1},{32,16},{33,49},{48,0},{49,33},{2,50}... | collective-permute-start | bytes 786440 | tf_op jit(solution)/shard_map/ppermute | solution.py:57
  10.5 9.0 %collective-permute-start.2 = (bf16[2,256,256]{2,1,0:T(8,128)(2,1)S(1)}, bf16[2,256,256]{2,1,0:T(8,128)(2,1)S(1)}, u32[]{:S(2)}, u32[]{:S(2)}) collective-permute-start(bf16[2,256,256]{2,1,0:T(8,128)(2,1)S(1)} %pad_maximum_fusion.7), channel_id=1, source_target_pairs={{0,1},{1,0},{2,3},{3,2},{4,5},{5,4},{6,7},{7,6},{8,9},{9,8},{10,11... | collective-permute-start | bytes 786440 | tf_op jit(solution)/shard_map/ppermute | solution.py:66
  19.5 1.4 %broadcast_in_dim.16 = bf16[32,16,256]{2,1,0:T(8,128)(2,1)} broadcast(bf16[16,256]{1,0:T(8,128)(2,1)} %param.2), dimensions={1,2} | broadcast | bytes 270336 | tf_op jit(solution)/shard_map/broadcast_in_dim | solution.py:18
  20.9 12.0 %all-to-all-start = ((bf16[32,16,256]{2,1,0:T(8,128)(2,1)}), bf16[32,16,256]{2,1,0:T(8,128)(2,1)S(1)}, u32[]{:S(2)}, u32[]{:S(2)}) async-start(bf16[32,16,256]{2,1,0:T(8,128)(2,1)} %broadcast_in_dim.16), calls=%async_computation | async-start | bytes 524288 | tf_op jit(solution)/shard_map/all_to_all | solution.py:19
  33.0 2.2 %collective-permute-start.3 = (bf16[2,256,256]{2,1,0:T(8,128)(2,1)S(1)}, bf16[2,256,256]{2,1,0:T(8,128)(2,1)S(1)}, u32[]{:S(2)}, u32[]{:S(2)}) collective-permute-start(bf16[2,256,256]{2,1,0:T(8,128)(2,1)S(1)} %collective-permute-done.1), channel_id=1, source_target_pairs={{0,1},{1,0},{2,3},{3,2},{4,5},{5,4},{6,7},{7,6},{8,9},{9,8},{10,11... | collective-permute-start | bytes 786440 | tf_op jit(solution)/shard_map/ppermute | solution.py:67
  35.4 10.3 %all-to-all-done = bf16[32,16,256]{2,1,0:T(8,128)(2,1)S(1)} async-done(((bf16[32,16,256]{2,1,0:T(8,128)(2,1)}), bf16[32,16,256]{2,1,0:T(8,128)(2,1)S(1)}, u32[]{:S(2)}, u32[]{:S(2)}) %all-to-all-start) | async-done | bytes 262176 | tf_op jit(solution)/shard_map/all_to_all | solution.py:19
  46.7 1.1 fusion.5
  48.3 10.5 %all_to_all.47 = bf16[16,4,512]{2,1,0:T(4,128)(2,1)S(1)} all-to-all(bf16[16,4,512]{2,1,0:T(4,128)(2,1)S(1)} %broadcast_in_dim.17), channel_id=1, replica_groups=mesh['h'=4,'l'=2,'x'=4,'z'=8,'c'=2] {'x','c','l'}, dimensions={0} | all-to-all | bytes 131072 | tf_op jit(solution)/shard_map/all_to_all | solution.py:19
  59.3 9.8 %all_to_all.48 = f32[8,1,512]{2,1,0:T(1,128)S(1)} all-to-all(f32[8,1,512]{2,1,0:T(1,128)S(1)} %broadcast_in_dim.18), channel_id=1, replica_groups=mesh['h'=4,'l'=2,'x'=4,'z'=8,'c'=2] {'z'}, dimensions={0} | all-to-all | bytes 32768 | tf_op jit(solution)/shard_map/all_to_all | solution.py:19
  69.1 0.5 fusion.1
  69.6 10.2 %all_to_all.49 = bf16[16,4,512]{2,1,0:T(4,128)(2,1)S(1)} all-to-all(bf16[16,4,512]{2,1,0:T(4,128)(2,1)S(1)} %broadcast_in_dim.19), channel_id=1, replica_groups=mesh['h'=4,'l'=2,'x'=4,'z'=8,'c'=2] {'x','c','l'}, dimensions={0} | all-to-all | bytes 131072 | tf_op jit(solution)/shard_map/all_to_all | solution.py:19
  80.4 9.0 %all_to_all.50 = f32[8,1,512]{2,1,0:T(1,128)S(1)} all-to-all(f32[8,1,512]{2,1,0:T(1,128)S(1)} %broadcast_in_dim.20), channel_id=1, replica_groups=mesh['h'=4,'l'=2,'x'=4,'z'=8,'c'=2] {'z'}, dimensions={0} | all-to-all | bytes 32768 | tf_op jit(solution)/shard_map/all_to_all | solution.py:19
  89.9 9.9 %all_to_all.51 = bf16[16,4,512]{2,1,0:T(4,128)(2,1)S(1)} all-to-all(bf16[16,4,512]{2,1,0:T(4,128)(2,1)S(1)} %broadcast_in_dim.21), channel_id=1, replica_groups=mesh['h'=4,'l'=2,'x'=4,'z'=8,'c'=2] {'x','c','l'}, dimensions={0} | all-to-all | bytes 131072 | tf_op jit(solution)/shard_map/all_to_all | solution.py:19
  99.9 0.6 fusion.11
  101.2 9.9 %all_to_all.52 = bf16[8,24,256]{2,1,0:T(8,128)(2,1)S(1)} all-to-all(bf16[8,24,256]{2,1,0:T(8,128)(2,1)S(1)} %pad_maximum_fusion.8), channel_id=1, replica_groups=mesh['h'=4,'l'=2,'x'=4,'z'=8,'c'=2] {'z'}, dimensions={0} | all-to-all | bytes 196608 | tf_op jit(solution)/shard_map/all_to_all | solution.py:151
  112.2 11.9 %all_to_all.53 = bf16[16,40,256]{2,1,0:T(8,128)(2,1)S(1)} all-to-all(bf16[16,40,256]{2,1,0:T(8,128)(2,1)S(1)} %pad_maximum_fusion.5), channel_id=1, replica_groups=mesh['h'=4,'l'=2,'x'=4,'z'=8,'c'=2] {'x','c','l'}, dimensions={0} | all-to-all | bytes 655360 | tf_op jit(solution)/shard_map/all_to_all | solution.py:169
  124.2 0.7 broadcast_in_dim.23
  124.9 3.6 %all-to-all-start.8 = ((f16[8,32,256]{2,1,0:T(8,128)(2,1)}), f16[8,32,256]{2,1,0:T(8,128)(2,1)S(1)}, u32[]{:S(2)}, u32[]{:S(2)}) async-start(f16[8,32,256]{2,1,0:T(8,128)(2,1)} %broadcast_in_dim.23), calls=%async_computation.8 | async-start | bytes 262144 | tf_op jit(solution)/shard_map/all_to_all | solution.py:19
  128.6 0.7 fusion.21
  129.3 7.1 %all-to-all-done.8 = f16[8,32,256]{2,1,0:T(8,128)(2,1)S(1)} async-done(((f16[8,32,256]{2,1,0:T(8,128)(2,1)}), f16[8,32,256]{2,1,0:T(8,128)(2,1)S(1)}, u32[]{:S(2)}, u32[]{:S(2)}) %all-to-all-start.8) | async-done | bytes 131104 | tf_op jit(solution)/shard_map/all_to_all | solution.py:19
  136.4 0.7 bitcast_convert_fusion
  (64 shorter events, 5.0 us)
Async XLA Ops:
  0.6 7.8 %collective-permute-start = (bf16[256,256]{1,0:T(8,128)(2,1)}, bf16[256,256]{1,0:T(8,128)(2,1)S(1)}, u32[]{:S(2)}, u32[]{:S(2)}) collective-permute-start(bf16[256,256]{1,0:T(8,128)(2,1)} %block_ref.1), channel_id=1, source_target_pairs={{0,16},{1,49},{16,0},{17,33},{32,48},{33,17},{48,32},{49,1},{2,18}... | collective-permute-start | bytes 393224 | tf_op jit(solution)/shard_map/ppermute | solution.py:57
  5.8 0.9 copy-start
  8.4 24.6 %collective-permute-start.1 = (bf16[2,256,256]{2,1,0:T(8,128)(2,1)S(1)}, bf16[2,256,256]{2,1,0:T(8,128)(2,1)S(1)}, u32[]{:S(2)}, u32[]{:S(2)}) collective-permute-start(bf16[2,256,256]{2,1,0:T(8,128)(2,1)S(1)} %pad_maximum_fusion.7), channel_id=1, source_target_pairs={{0,48},{1,17},{16,32},{17,1},{32,16},{33,49},{48,0},{49,33},{2,50}... | collective-permute-start | bytes 786440 | tf_op jit(solution)/shard_map/ppermute | solution.py:57
  10.5 24.7 %collective-permute-start.2 = (bf16[2,256,256]{2,1,0:T(8,128)(2,1)S(1)}, bf16[2,256,256]{2,1,0:T(8,128)(2,1)S(1)}, u32[]{:S(2)}, u32[]{:S(2)}) collective-permute-start(bf16[2,256,256]{2,1,0:T(8,128)(2,1)S(1)} %pad_maximum_fusion.7), channel_id=1, source_target_pairs={{0,1},{1,0},{2,3},{3,2},{4,5},{5,4},{6,7},{7,6},{8,9},{9,8},{10,11... | collective-permute-start | bytes 786440 | tf_op jit(solution)/shard_map/ppermute | solution.py:66
  20.9 24.7 %all-to-all-start = ((bf16[32,16,256]{2,1,0:T(8,128)(2,1)}), bf16[32,16,256]{2,1,0:T(8,128)(2,1)S(1)}, u32[]{:S(2)}, u32[]{:S(2)}) async-start(bf16[32,16,256]{2,1,0:T(8,128)(2,1)} %broadcast_in_dim.16), calls=%async_computation | async-start | bytes 524288 | tf_op jit(solution)/shard_map/all_to_all | solution.py:19
  33.0 12.8 %collective-permute-start.3 = (bf16[2,256,256]{2,1,0:T(8,128)(2,1)S(1)}, bf16[2,256,256]{2,1,0:T(8,128)(2,1)S(1)}, u32[]{:S(2)}, u32[]{:S(2)}) collective-permute-start(bf16[2,256,256]{2,1,0:T(8,128)(2,1)S(1)} %collective-permute-done.1), channel_id=1, source_target_pairs={{0,1},{1,0},{2,3},{3,2},{4,5},{5,4},{6,7},{7,6},{8,9},{9,8},{10,11... | collective-permute-start | bytes 786440 | tf_op jit(solution)/shard_map/ppermute | solution.py:67
  46.7 1.2 copy-start.2
  100.6 10.5 %slice-start = ((f32[4,512]{1,0:T(4,128)}), f32[1,512]{1,0:T(1,128)S(1)}, s32[]{:S(2)}) async-start(f32[4,512]{1,0:T(4,128)} %copy-done.2), calls=%async_computation.9 | async-start | bytes 4096 | tf_op jit(solution)/shard_map/slice | solution.py:107
  111.6 17.0 %copy-start.1 = (bf16[16,256]{1,0:T(8,128)(2,1)S(1)}, bf16[16,256]{1,0:T(8,128)(2,1)}, u32[]{:S(2)}) copy-start(bf16[16,256]{1,0:T(8,128)(2,1)} %param.2) | copy-start | bytes 24580
  124.9 11.5 %all-to-all-start.8 = ((f16[8,32,256]{2,1,0:T(8,128)(2,1)}), f16[8,32,256]{2,1,0:T(8,128)(2,1)S(1)}, u32[]{:S(2)}, u32[]{:S(2)}) async-start(f16[8,32,256]{2,1,0:T(8,128)(2,1)} %broadcast_in_dim.23), calls=%async_computation.8 | async-start | bytes 262144 | tf_op jit(solution)/shard_map/all_to_all | solution.py:19

commit v13 on v12

--- a/solution.py
+++ b/solution.py
@@ -133,8 +133,10 @@
             kernel.astype(jnp.float32) * weights_cols[:, None, :], axis=(0, 2)
         )
         if sweep < ITERS - 1:
-            row_total = jnp.sum(spread(row_part, "z"), axis=0)
-            weights_rows = 1.0 / row_total
+            row_part = lax.optimization_barrier(row_part).astype(jnp.bfloat16)
+            row_parts = spread(row_part.reshape(-1, width), "z")
+            row_total = jnp.sum(row_parts.astype(jnp.float32), axis=0)
+            weights_rows = 1.0 / row_total.reshape(items)
 
     size = rows * depth
     mine = kernel[:, :size].astype(jnp.float32) * weights_cols[:, None, :]

time: 138 us -> 138 us (level)
  no operation moved by 1% of the time
where the time goes in v13:
time: 138 us; the launch traced here: 137 us
  blocking collectives  71.1 us (52%)
  starting transfers between devices  34.1 us (25%)
  waiting for transfers between devices  19 us (14%)
  other arithmetic  5.49 us (4%)
  local copies, waits for them, and re-layouts  3.6 us (3%)
  matrix products  2.61 us (2%)
    all_to_all x5, blocking collectives, spread(): return lax.all_to_all(copies, axes, 0, 0, tiled=True)  49.3 us
    all_to_all x2, waiting for transfers between devices, spread(): return lax.all_to_all(copies, axes, 0, 0, tiled=True)  17.4 us
    all_to_all x2, starting transfers between devices, spread(): return lax.all_to_all(copies, axes, 0, 0, tiled=True)  15.6 us
    all_to_all x1, blocking collectives, shards(): packed = lax.all_to_all(packed, ITEM_AXES, 0, 0, tiled=True)  11.9 us
    all_to_all x1, blocking collectives, shards(): packed = lax.all_to_all(packed, 'z', 0, 0, tiled=True)  9.91 us
    ppermute x1, starting transfers between devices, gather_codes(): other = lax.ppermute(block, 'c', [(0, 1), (1, 0)])  8.99 us
    ppermute x2, starting transfers between devices, swap(): lax.ppermute(block, ('x', 'c'), [(x * 2 + c, pairs[turn ^ c][x] * 2 + c)...  7.3 us
  transfers between devices with their start and end apart: 6, of which 3 were waited for; matrix products, arithmetic and copies ran while one was open for 2% of the time, Pallas kernels for 0%

profile of v13, /device:TPU:1, one launch (start us, length us, event | category | flops | bytes accessed | tf_op | source)
XLA Modules:
  0.0 137.0 jit_solution(6584132627470571254)
XLA Ops:
  0.6 5.2 %collective-permute-start = (bf16[256,256]{1,0:T(8,128)(2,1)}, bf16[256,256]{1,0:T(8,128)(2,1)S(1)}, u32[]{:S(2)}, u32[]{:S(2)}) collective-permute-start(bf16[256,256]{1,0:T(8,128)(2,1)} %block_ref.1), channel_id=1, source_target_pairs={{0,16},{1,49},{16,0},{17,33},{32,48},{33,17},{48,32},{49,1},{2,18}... | collective-permute-start | bytes 393224 | tf_op jit(solution)/shard_map/ppermute | solution.py:57
  5.9 0.9 copy-done
  6.8 1.6 %collective-permute-done = bf16[256,256]{1,0:T(8,128)(2,1)S(1)} collective-permute-done((bf16[256,256]{1,0:T(8,128)(2,1)}, bf16[256,256]{1,0:T(8,128)(2,1)S(1)}, u32[]{:S(2)}, u32[]{:S(2)}) %collective-permute-start) | collective-permute-done | bytes 131104 | tf_op jit(solution)/shard_map/ppermute | solution.py:57
  8.4 2.1 %collective-permute-start.1 = (bf16[2,256,256]{2,1,0:T(8,128)(2,1)S(1)}, bf16[2,256,256]{2,1,0:T(8,128)(2,1)S(1)}, u32[]{:S(2)}, u32[]{:S(2)}) collective-permute-start(bf16[2,256,256]{2,1,0:T(8,128)(2,1)S(1)} %pad_maximum_fusion.7), channel_id=1, source_target_pairs={{0,48},{1,17},{16,32},{17,1},{32,16},{33,49},{48,0},{49,33},{2,50}... | collective-permute-start | bytes 786440 | tf_op jit(solution)/shard_map/ppermute | solution.py:57
  10.5 9.0 %collective-permute-start.2 = (bf16[2,256,256]{2,1,0:T(8,128)(2,1)S(1)}, bf16[2,256,256]{2,1,0:T(8,128)(2,1)S(1)}, u32[]{:S(2)}, u32[]{:S(2)}) collective-permute-start(bf16[2,256,256]{2,1,0:T(8,128)(2,1)S(1)} %pad_maximum_fusion.7), channel_id=1, source_target_pairs={{0,1},{1,0},{2,3},{3,2},{4,5},{5,4},{6,7},{7,6},{8,9},{9,8},{10,11... | collective-permute-start | bytes 786440 | tf_op jit(solution)/shard_map/ppermute | solution.py:66
  19.5 1.4 %broadcast_in_dim.20 = bf16[32,16,256]{2,1,0:T(8,128)(2,1)} broadcast(bf16[16,256]{1,0:T(8,128)(2,1)} %param.2), dimensions={1,2} | broadcast | bytes 270336 | tf_op jit(solution)/shard_map/broadcast_in_dim | solution.py:18
  20.9 12.0 %all-to-all-start = ((bf16[32,16,256]{2,1,0:T(8,128)(2,1)}), bf16[32,16,256]{2,1,0:T(8,128)(2,1)S(1)}, u32[]{:S(2)}, u32[]{:S(2)}) async-start(bf16[32,16,256]{2,1,0:T(8,128)(2,1)} %broadcast_in_dim.20), calls=%async_computation | async-start | bytes 524288 | tf_op jit(solution)/shard_map/all_to_all | solution.py:19
  33.0 2.2 %collective-permute-start.3 = (bf16[2,256,256]{2,1,0:T(8,128)(2,1)S(1)}, bf16[2,256,256]{2,1,0:T(8,128)(2,1)S(1)}, u32[]{:S(2)}, u32[]{:S(2)}) collective-permute-start(bf16[2,256,256]{2,1,0:T(8,128)(2,1)S(1)} %collective-permute-done.1), channel_id=1, source_target_pairs={{0,1},{1,0},{2,3},{3,2},{4,5},{5,4},{6,7},{7,6},{8,9},{9,8},{10,11... | collective-permute-start | bytes 786440 | tf_op jit(solution)/shard_map/ppermute | solution.py:67
  35.4 10.3 %all-to-all-done = bf16[32,16,256]{2,1,0:T(8,128)(2,1)S(1)} async-done(((bf16[32,16,256]{2,1,0:T(8,128)(2,1)}), bf16[32,16,256]{2,1,0:T(8,128)(2,1)S(1)}, u32[]{:S(2)}, u32[]{:S(2)}) %all-to-all-start) | async-done | bytes 262176 | tf_op jit(solution)/shard_map/all_to_all | solution.py:19
  46.7 1.1 fusion.5
  48.3 10.5 %all_to_all.45 = bf16[16,4,512]{2,1,0:T(4,128)(2,1)S(1)} all-to-all(bf16[16,4,512]{2,1,0:T(4,128)(2,1)S(1)} %broadcast_in_dim.21), channel_id=1, replica_groups=mesh['h'=4,'l'=2,'x'=4,'z'=8,'c'=2] {'x','c','l'}, dimensions={0} | all-to-all | bytes 131072 | tf_op jit(solution)/shard_map/all_to_all | solution.py:19
  59.3 9.7 %all_to_all.46 = bf16[8,2,256]{2,1,0:T(2,128)(2,1)S(1)} all-to-all(bf16[8,2,256]{2,1,0:T(2,128)(2,1)S(1)} %broadcast_in_dim.23), channel_id=1, replica_groups=mesh['h'=4,'l'=2,'x'=4,'z'=8,'c'=2] {'z'}, dimensions={0} | all-to-all | bytes 16384 | tf_op jit(solution)/shard_map/all_to_all | solution.py:19
  69.6 10.2 %all_to_all.47 = bf16[16,4,512]{2,1,0:T(4,128)(2,1)S(1)} all-to-all(bf16[16,4,512]{2,1,0:T(4,128)(2,1)S(1)} %broadcast_in_dim.24), channel_id=1, replica_groups=mesh['h'=4,'l'=2,'x'=4,'z'=8,'c'=2] {'x','c','l'}, dimensions={0} | all-to-all | bytes 131072 | tf_op jit(solution)/shard_map/all_to_all | solution.py:19
  80.4 8.9 %all_to_all.48 = bf16[8,2,256]{2,1,0:T(2,128)(2,1)S(1)} all-to-all(bf16[8,2,256]{2,1,0:T(2,128)(2,1)S(1)} %broadcast_in_dim.26), channel_id=1, replica_groups=mesh['h'=4,'l'=2,'x'=4,'z'=8,'c'=2] {'z'}, dimensions={0} | all-to-all | bytes 16384 | tf_op jit(solution)/shard_map/all_to_all | solution.py:19
  89.3 0.5 fusion.3
  89.9 10.0 %all_to_all.49 = bf16[16,4,512]{2,1,0:T(4,128)(2,1)S(1)} all-to-all(bf16[16,4,512]{2,1,0:T(4,128)(2,1)S(1)} %broadcast_in_dim.27), channel_id=1, replica_groups=mesh['h'=4,'l'=2,'x'=4,'z'=8,'c'=2] {'x','c','l'}, dimensions={0} | all-to-all | bytes 131072 | tf_op jit(solution)/shard_map/all_to_all | solution.py:19
  99.9 0.6 fusion.11
  101.1 9.9 %all_to_all.50 = bf16[8,24,256]{2,1,0:T(8,128)(2,1)S(1)} all-to-all(bf16[8,24,256]{2,1,0:T(8,128)(2,1)S(1)} %pad_maximum_fusion.8), channel_id=1, replica_groups=mesh['h'=4,'l'=2,'x'=4,'z'=8,'c'=2] {'z'}, dimensions={0} | all-to-all | bytes 196608 | tf_op jit(solution)/shard_map/all_to_all | solution.py:153
  112.1 11.9 %all_to_all.51 = bf16[16,40,256]{2,1,0:T(8,128)(2,1)S(1)} all-to-all(bf16[16,40,256]{2,1,0:T(8,128)(2,1)S(1)} %pad_maximum_fusion.5), channel_id=1, replica_groups=mesh['h'=4,'l'=2,'x'=4,'z'=8,'c'=2] {'x','c','l'}, dimensions={0} | all-to-all | bytes 655360 | tf_op jit(solution)/shard_map/all_to_all | solution.py:171
  124.2 0.7 broadcast_in_dim.29
  124.8 3.6 %all-to-all-start.8 = ((f16[8,32,256]{2,1,0:T(8,128)(2,1)}), f16[8,32,256]{2,1,0:T(8,128)(2,1)S(1)}, u32[]{:S(2)}, u32[]{:S(2)}) async-start(f16[8,32,256]{2,1,0:T(8,128)(2,1)} %broadcast_in_dim.29), calls=%async_computation.8 | async-start | bytes 262144 | tf_op jit(solution)/shard_map/all_to_all | solution.py:19
  128.5 0.7 fusion.21
  129.2 7.1 %all-to-all-done.8 = f16[8,32,256]{2,1,0:T(8,128)(2,1)S(1)} async-done(((f16[8,32,256]{2,1,0:T(8,128)(2,1)}), f16[8,32,256]{2,1,0:T(8,128)(2,1)S(1)}, u32[]{:S(2)}, u32[]{:S(2)}) %all-to-all-start.8) | async-done | bytes 131104 | tf_op jit(solution)/shard_map/all_to_all | solution.py:19
  136.3 0.7 bitcast_convert_fusion
  (68 shorter events, 5.0 us)
Async XLA Ops:
  0.6 7.8 %collective-permute-start = (bf16[256,256]{1,0:T(8,128)(2,1)}, bf16[256,256]{1,0:T(8,128)(2,1)S(1)}, u32[]{:S(2)}, u32[]{:S(2)}) collective-permute-start(bf16[256,256]{1,0:T(8,128)(2,1)} %block_ref.1), channel_id=1, source_target_pairs={{0,16},{1,49},{16,0},{17,33},{32,48},{33,17},{48,32},{49,1},{2,18}... | collective-permute-start | bytes 393224 | tf_op jit(solution)/shard_map/ppermute | solution.py:57
  5.8 0.9 copy-start
  8.4 24.6 %collective-permute-start.1 = (bf16[2,256,256]{2,1,0:T(8,128)(2,1)S(1)}, bf16[2,256,256]{2,1,0:T(8,128)(2,1)S(1)}, u32[]{:S(2)}, u32[]{:S(2)}) collective-permute-start(bf16[2,256,256]{2,1,0:T(8,128)(2,1)S(1)} %pad_maximum_fusion.7), channel_id=1, source_target_pairs={{0,48},{1,17},{16,32},{17,1},{32,16},{33,49},{48,0},{49,33},{2,50}... | collective-permute-start | bytes 786440 | tf_op jit(solution)/shard_map/ppermute | solution.py:57
  10.5 24.7 %collective-permute-start.2 = (bf16[2,256,256]{2,1,0:T(8,128)(2,1)S(1)}, bf16[2,256,256]{2,1,0:T(8,128)(2,1)S(1)}, u32[]{:S(2)}, u32[]{:S(2)}) collective-permute-start(bf16[2,256,256]{2,1,0:T(8,128)(2,1)S(1)} %pad_maximum_fusion.7), channel_id=1, source_target_pairs={{0,1},{1,0},{2,3},{3,2},{4,5},{5,4},{6,7},{7,6},{8,9},{9,8},{10,11... | collective-permute-start | bytes 786440 | tf_op jit(solution)/shard_map/ppermute | solution.py:66
  20.9 24.7 %all-to-all-start = ((bf16[32,16,256]{2,1,0:T(8,128)(2,1)}), bf16[32,16,256]{2,1,0:T(8,128)(2,1)S(1)}, u32[]{:S(2)}, u32[]{:S(2)}) async-start(bf16[32,16,256]{2,1,0:T(8,128)(2,1)} %broadcast_in_dim.20), calls=%async_computation | async-start | bytes 524288 | tf_op jit(solution)/shard_map/all_to_all | solution.py:19
  33.0 12.8 %collective-permute-start.3 = (bf16[2,256,256]{2,1,0:T(8,128)(2,1)S(1)}, bf16[2,256,256]{2,1,0:T(8,128)(2,1)S(1)}, u32[]{:S(2)}, u32[]{:S(2)}) collective-permute-start(bf16[2,256,256]{2,1,0:T(8,128)(2,1)S(1)} %collective-permute-done.1), channel_id=1, source_target_pairs={{0,1},{1,0},{2,3},{3,2},{4,5},{5,4},{6,7},{7,6},{8,9},{9,8},{10,11... | collective-permute-start | bytes 786440 | tf_op jit(solution)/shard_map/ppermute | solution.py:67
  46.7 1.2 copy-start.2
  100.5 10.5 %slice-start = ((f32[4,512]{1,0:T(4,128)}), f32[1,512]{1,0:T(1,128)S(1)}, s32[]{:S(2)}) async-start(f32[4,512]{1,0:T(4,128)} %copy-done.2), calls=%async_computation.9 | async-start | bytes 4096 | tf_op jit(solution)/shard_map/slice | solution.py:107
  111.5 17.0 %copy-start.1 = (bf16[16,256]{1,0:T(8,128)(2,1)S(1)}, bf16[16,256]{1,0:T(8,128)(2,1)}, u32[]{:S(2)}) copy-start(bf16[16,256]{1,0:T(8,128)(2,1)} %param.2) | copy-start | bytes 24580
  124.8 11.5 %all-to-all-start.8 = ((f16[8,32,256]{2,1,0:T(8,128)(2,1)}), f16[8,32,256]{2,1,0:T(8,128)(2,1)S(1)}, u32[]{:S(2)}, u32[]{:S(2)}) async-start(f16[8,32,256]{2,1,0:T(8,128)(2,1)} %broadcast_in_dim.29), calls=%async_computation.8 | async-start | bytes 262144 | tf_op jit(solution)/shard_map/all_to_all | solution.py:19
